TPU v7x, 128 devices: a whole 4x4x4 slice. The times are simulated.
128 devices in a mesh: depth: 2 (over core), tiles: 64 (over z, y, x).
Axes of the slice: x: 4, y: 4, z: 4, core: 2. Of those that a mesh axis runs over, the one named last changes fastest.
Arguments:
- transmission: float32 [4, 2, 64, 256, 256], P('depth', None, 'tiles'), may hold values from -0.4 to 1.3
- illumination: float32 [2, 256, 256], replicated, may hold values from -6 to 6
- fresnel_taps: float32 [2, 31], replicated, may hold values from -1 to 1
- intensity: float32 [64, 2, 256, 256], P('tiles'), may hold values from 0 to 2
- offsets: int32 [64, 2, 2], P('tiles'), may hold values from 0 to 255, as said below
- counts: int32 [64], P('tiles'), may hold values from 0 to 2, as said below
Outputs:
- object_gradient: float32 [4, 2, 64, 256, 256], P('depth', None, 'tiles')
Inputs may be any that keep to these rules, and one draw needn't show every extreme that they name: `offsets`: A tile in the last row of tiles has row offset 0 in every slot, and a tile in the last column of tiles has column offset 0 in every slot, so every patch lies inside the object. Slots j >= counts[t] of tile t are unused.
All inputs are finite; a program needn't handle non-finite values.
Results may differ from a plain program's by a relative error of at most 0.0003.
Values sent between devices are 32-bit elements; how exact they have to be, the bound alone decides.
No kernel may reach another device: no remote copies, remote signals or barrier semaphores. Data moves between devices by JAX's collectives and lax.ppermute only.
A program may use at most 64 MiB of HBM per device.

v0:
```python
import functools
import math

import jax
import jax.numpy as jnp
from jax import lax
from jax.experimental import pallas as pl
from jax.experimental.pallas import tpu as pltpu
from jax.sharding import PartitionSpec as P

GX = 4
ROWS = 16
TILES = 64
N = 256
CH = 32
BF = jnp.bfloat16
F32 = jnp.float32
FIELD = jax.ShapeDtypeStruct((2, N, N), F32)
VS = pl.BlockSpec(memory_space=pltpu.VMEM)
SS = pl.BlockSpec(memory_space=pltpu.SMEM)


def split(x):
    high = x.astype(BF)
    return high, (x - high.astype(F32)).astype(BF)


def dot3(left_high, left_low, right_high, right_low):
    dot = functools.partial(jnp.dot, preferred_element_type=F32)
    return dot(left_high, right_high) + dot(left_high, right_low) + dot(left_low, right_high)


def put_left(refs, index, re, im):
    for ref, r, m in zip(refs, split(re), split(im)):
        ref[index, 0:N, 0:N] = r
        ref[index, N : 2 * N, N : 2 * N] = r
        ref[index, N : 2 * N, 0:N] = m
        ref[index, 0:N, N : 2 * N] = -m


def put_right(refs, index, re, im):
    for ref, r, m in zip(refs, split(re), split(im)):
        ref[index, 0:N] = r
        ref[index, N : 2 * N] = m


def tables_kernel(spot, taps, dft, left_high, left_low, right_high, right_low, a_high, a_low, b_high, b_low):
    left = (left_high, left_low)
    right = (right_high, right_low)
    a = (a_high, a_low)
    b = (b_high, b_low)
    row = lax.broadcasted_iota(jnp.int32, (N, N), 0)
    col = lax.broadcasted_iota(jnp.int32, (N, N), 1)

    def circulant(k):
        base = jnp.broadcast_to(taps[k : k + 1, :], (N, N))
        return pltpu.roll(base, 0, 1, stride=1, stride_axis=0)

    rings = [circulant(k) for k in range(4)]
    fr, fi = dft[0], dft[1]

    def bands(shift):
        inside = jnp.abs(((row - shift) & (N - 1)) - ((col - shift) & (N - 1))) <= 15
        return [jnp.where(inside, ring, 0.0) for ring in rings]

    def multiply():
        m = dot3(a_high[0], a_low[0], b_high[0], b_low[0])
        return m[:N], m[N:]

    tr, ti, ttr, tti = bands(spot[0])
    put_left(left, 0, tr, ti)
    put_left(left, 1, ttr, -tti)
    put_left(a, 0, fr, fi)
    put_right(b, 0, tr, ti)
    mr, mi = multiply()
    put_left(left, 2, mr, mi)
    put_left(a, 0, ttr, tti)
    put_right(b, 0, fr, fi)
    mr, mi = multiply()
    put_left(left, 3, mr, -mi)
    tr, ti, ttr, tti = bands(spot[1])
    put_right(right, 0, ttr, tti)
    put_right(right, 1, tr, -ti)
    put_left(a, 0, ttr, tti)
    mr, mi = multiply()
    put_right(right, 2, mr, mi)
    put_left(a, 0, fr, fi)
    put_right(b, 0, tr, ti)
    mr, mi = multiply()
    put_right(right, 3, mr, -mi)


def tables(spot, taps, dft):
    return pl.pallas_call(
        tables_kernel,
        out_shape=[jax.ShapeDtypeStruct((4, 2 * N, 2 * N), BF)] * 2
        + [jax.ShapeDtypeStruct((4, 2 * N, N), BF)] * 2,
        in_specs=[SS, VS, VS],
        out_specs=[VS] * 4,
        scratch_shapes=[pltpu.VMEM((1, 2 * N, 2 * N), BF)] * 2 + [pltpu.VMEM((1, 2 * N, N), BF)] * 2,
        compiler_params=pltpu.CompilerParams(vmem_limit_bytes=12 << 20),
        name="tables",
    )(spot, taps, dft)


def tap_rows(taps):
    rows = jnp.concatenate([taps, taps[:, ::-1]], 0)
    rows = jnp.pad(rows, ((0, 4), (0, N - rows.shape[1])))
    return jnp.roll(rows, -15, 1)


def chunks():
    return [(pl.ds(r0, CH), pl.ds(N + r0, CH), r0) for r0 in range(0, N, CH)]


def own_rows(spot, r0):
    row = lax.broadcasted_iota(jnp.int32, (CH, N), 0) + r0
    return ((row >= spot[0]).astype(jnp.int32) ^ spot[2]) == 1


def own_cols(spot):
    col = lax.broadcasted_iota(jnp.int32, (CH, N), 1)
    return ((col >= spot[1]).astype(jnp.int32) ^ spot[2]) == 1


WORK = (
    [pltpu.VMEM((2 * N, N), BF)] * 2
    + [pltpu.VMEM((2 * N, 2 * N), BF)] * 2
    + [pltpu.VMEM((2 * N, N), F32)]
)


def put_field(work, r0, re, im):
    for base, part in ((0, re), (N, im)):
        high, low = split(part)
        work[0][pl.ds(base + r0, CH)] = high
        work[1][pl.ds(base + r0, CH)] = low


def propagate(work, tabs, index):
    x_high, x_low, y_high, y_low, acc = work
    left_high, left_low, right_high, right_low = tabs
    acc[...] = dot3(left_high[index], left_low[index], x_high[...], x_low[...])
    for sl, s2, r0 in chunks():
        for ref, r, m in zip((y_high, y_low), split(acc[sl]), split(acc[s2])):
            ref[sl, 0:N] = r
            ref[s2, N : 2 * N] = r
            ref[s2, 0:N] = m
            ref[sl, N : 2 * N] = -m
    acc[...] = dot3(y_high[...], y_low[...], right_high[index], right_low[index])


def gather_patch(spot, p, own, near, far, out):
    mine_cols = own_cols(spot)
    for sl, _, r0 in chunks():
        mine_rows = own_rows(spot, r0)
        inner, outer = (mine_cols, mine_rows) if p % 2 == 0 else (mine_rows, mine_cols)
        for c in range(2):
            out[c, sl] = jnp.where(outer, jnp.where(inner, own[c, sl], near[c, sl]), far[c, sl])


def enter_slice(work, patch, wave):
    for sl, _, r0 in chunks():
        pr, pi, wr, wi = wave[0, sl], wave[1, sl], patch[0, sl], patch[1, sl]
        put_field(work, r0, pr * wr - pi * wi, pr * wi + pi * wr)


def leave(work, wave):
    acc = work[4]
    for sl, s2, _ in chunks():
        wave[0, sl] = acc[sl]
        wave[1, sl] = acc[s2]


def leave_slice(work, spot, p, patch, wave, grad, sent, onward):
    acc = work[4]
    mine_cols = own_cols(spot)
    for sl, s2, r0 in chunks():
        mr, mi, pr, pi = acc[sl], acc[s2], wave[0, sl], wave[1, sl]
        keep = own_rows(spot, r0) if p % 2 == 0 else mine_cols
        for c, g in enumerate((pr * mr + pi * mi, pr * mi - pi * mr)):
            grad[c, sl] = g
            sent[c, sl] = jnp.where(keep, 0.0, g)
        if onward:
            wr, wi = patch[0, sl], patch[1, sl]
            put_field(work, r0, wr * mr + wi * mi, wr * mi - wi * mr)


def first_kernel(spot, *refs):
    own, near, far = refs[0:2], refs[2:4], refs[4:6]
    probe, tabs = refs[6], refs[7:11]
    patches, waves = refs[11:13], refs[13:16]
    work = refs[16:]
    for c in range(2):
        waves[0][c] = pltpu.roll(pltpu.roll(probe[c], spot[0], 0), spot[1], 1)
    for p in range(2):
        gather_patch(spot, p, own[p], near[p], far[p], patches[p])
        enter_slice(work, patches[p], waves[p])
        propagate(work, tabs, 0)
        leave(work, waves[p + 1])


def second_kernel(spot, *refs):
    own, near, far = refs[0:2], refs[2:4], refs[4:6]
    measured, wave, tabs = refs[6], refs[7], refs[8:12]
    patch, middle, grad, sent, state = refs[12:17]
    last = refs[17:19]
    work = refs[19:]
    for p in range(2):
        gather_patch(spot, p, own[p], near[p], far[p], (patch, last[0])[p])
    enter_slice(work, patch, wave)
    propagate(work, tabs, 0)
    leave(work, middle)
    enter_slice(work, last[0], middle)
    propagate(work, tabs, 2)
    acc = work[4]
    scale = 2.0 * spot[3].astype(F32)
    for sl, s2, r0 in chunks():
        sr, si = acc[sl], acc[s2]
        misfit = (sr * sr + si * si - measured[sl]) * scale
        put_field(work, r0, misfit * sr, misfit * si)
    propagate(work, tabs, 3)
    leave_slice(work, spot, 3, last[0], middle, grad, sent, True)
    state[0] = work[0][...]
    state[1] = work[1][...]


def back_kernel(p, onward, spot, *refs):
    state, wave = refs[0], refs[1]
    n = 2
    patch = None
    if onward:
        patch = refs[2]
        n = 3
    tabs = refs[n : n + 4]
    outs = refs[n + 4 :]
    grad, sent = outs[0], outs[1]
    work = outs[3:] if onward else outs[2:]
    work[0][...] = state[0]
    work[1][...] = state[1]
    propagate(work, tabs, 1)
    leave_slice(work, spot, p, patch, wave, grad, sent, onward)
    if onward:
        outs[2][0] = work[0][...]
        outs[2][1] = work[1][...]


STATE = jax.ShapeDtypeStruct((2, 2 * N, N), BF)


def call(kernel, outs, spot, args, scratch=()):
    room = (20 if scratch else 8) << 20
    return pl.pallas_call(
        kernel,
        out_shape=outs,
        in_specs=[SS] + [VS] * len(args),
        out_specs=[VS] * len(outs),
        scratch_shapes=list(scratch),
        compiler_params=pltpu.CompilerParams(vmem_limit_bytes=room),
    )(spot, *args)


def blend_kernel(by_rows, spot, own, near, out):
    mine_cols = own_cols(spot)
    for sl, _, r0 in chunks():
        mask = own_rows(spot, r0) if by_rows else mine_cols
        for c in range(2):
            out[c, sl] = jnp.where(mask, own[c, sl], near[c, sl])


def turn_kernel(p, spots, grad, came, sent, kept):
    here = [spots[i] for i in range(3)]
    there = [spots[4 + i] for i in range(3)]
    cols, there_cols = own_cols(here), own_cols(there)
    for sl, _, r0 in chunks():
        rows = own_rows(here, r0)
        if p % 2 == 0:
            first, second, mask = rows, cols, there_cols
        else:
            first, second, mask = cols, rows, own_rows(there, r0)
        for c in range(2):
            g = jnp.where(first, grad[c, sl], 0.0)
            v = came[c, sl]
            sent[c, sl] = jnp.where(second, 0.0, g) + jnp.where(mask, 0.0, v)
            kept[c, sl] = jnp.where(second, g, 0.0) + jnp.where(mask, v, 0.0)


def merge_kernel(spot, *refs):
    kept, went = refs[0:4], refs[4:8]
    stay, leave_ = refs[8], refs[9]
    upper = spot[2] == 1
    for q in range(2):
        for c in range(2):
            for sl, _, _ in chunks():
                low = kept[q][c, sl] + went[q][c, sl]
                high = kept[q + 2][c, sl] + went[q + 2][c, sl]
                stay[q, c, sl] = jnp.where(upper, high, low)
                leave_[q, c, sl] = jnp.where(upper, low, high)


def order_kernel(spot, mine, other, *outs):
    upper = spot[2] == 1
    for k in range(4):
        for c in range(2):
            for sl, _, _ in chunks():
                a, b = mine[k % 2, c, sl], other[k % 2, c, sl]
                outs[k][c, sl] = jnp.where(upper, b, a) if k < 2 else jnp.where(upper, a, b)


def moved(t, dx, dy):
    return ((t // GX + dy) % ROWS) * GX + (t % GX + dx) % GX


def pairs_of(*per_core):
    out = []
    for d, step in enumerate(per_core):
        if step is not None:
            out += [(d * TILES + t, d * TILES + moved(t, *step)) for t in range(TILES)]
    return out


GATHER = (pairs_of((-1, 0), (1, 0)), pairs_of((0, -1), (0, 1)))
SCATTER = (pairs_of((1, 0), (-1, 0)), pairs_of((0, 1), (0, -1)))
INFO = (pairs_of((1, 0), (1, 0)), pairs_of((0, 1), (0, 1)))
DIAGONAL = pairs_of(None, (1, 1))
SWAP = [(d * TILES + t, (1 - d) * TILES + t) for d in range(2) for t in range(TILES)]


def permute(block, pairs):
    return lax.ppermute(block, ("depth", "tiles"), pairs)


def fourier():
    row = lax.broadcasted_iota(jnp.int32, (N, N), 0)
    col = lax.broadcasted_iota(jnp.int32, (N, N), 1)
    phase = (row * col % N).astype(F32) * (2.0 * math.pi / N)
    scale = 1.0 / math.sqrt(N)
    return jnp.stack([jnp.cos(phase) * scale, -jnp.sin(phase) * scale])


def step(transmission, illumination, fresnel_taps, intensity, offsets, counts):
    core = lax.axis_index("depth").astype(jnp.int32)
    mine = transmission[:, :, 0]
    other = permute(mine, SWAP)
    alive = (core < counts[0]).astype(jnp.int32)
    info = jnp.concatenate([jnp.where(core == 0, offsets[0, 0], offsets[0, 1]), core[None], alive[None]])
    left = permute(info, INFO[0])
    up = permute(info, INFO[1])
    upleft = permute(info, DIAGONAL)
    here = jnp.where(core == 0, info, upleft)
    at_y = jnp.where(core == 0, up, left)
    at_x = jnp.where(core == 0, left, up)
    own = call(order_kernel, [FIELD] * 4, info, [mine, other])

    near = [permute(own[p], GATHER[p % 2]) for p in range(4)]
    shared = permute(intensity[0, 1], DIAGONAL)
    measured = jnp.where(core == 0, intensity[0, 0], shared)
    far = []
    for p in range(4):
        mixed, = call(functools.partial(blend_kernel, p % 2 == 1), [FIELD], (at_y, at_x)[p % 2], [own[p], near[p]])
        far.append(permute(mixed, GATHER[1 - p % 2]))

    tabs = tables(here, tap_rows(fresnel_taps), fourier())
    _, patch1, wave0, wave1, wave2 = call(
        first_kernel, [FIELD] * 5, here, [*own[:2], *near[:2], *far[:2], illumination, *tabs], WORK
    )
    patch2, _, grad3, sent3, state = call(
        second_kernel, [FIELD] * 4 + [STATE], here, [*own[2:], *near[2:], *far[2:], measured, wave2, *tabs],
        [pltpu.VMEM((2, N, N), F32)] * 2 + WORK
    )
    grads = [None, None, None, grad3]
    came = [None, None, None, permute(sent3, SCATTER[0])]
    for p, wave, patch in ((2, wave2, patch2), (1, wave1, patch1), (0, wave0, None)):
        onward = p > 0
        outs = call(
            functools.partial(back_kernel, p, onward), [FIELD] * 2 + [STATE] * onward, here,
            [state, wave] + [patch] * onward + list(tabs), WORK
        )
        grads[p] = outs[0]
        came[p] = permute(outs[1], SCATTER[1 - p % 2])
        state = outs[2] if onward else None
    kept, went = [None] * 4, [None] * 4
    for p in (3, 2, 1, 0):
        spots = jnp.concatenate([here, (at_y, at_x)[p % 2]])
        sent, kept[p] = call(functools.partial(turn_kernel, p), [FIELD] * 2, spots, [grads[p], came[p]])
        went[p] = permute(sent, SCATTER[p % 2])
    pair = jax.ShapeDtypeStruct((2, 2, N, N), F32)
    stay, leaving = call(merge_kernel, [pair] * 2, here, [*kept, *went])
    back = permute(leaving, SWAP)
    return (stay + back)[:, :, None]


def solution(mesh):
    placed = (
        P("depth", None, "tiles", None, None),
        P(),
        P(),
        P("tiles", None, None, None),
        P("tiles", None, None),
        P("tiles"),
    )
    return jax.shard_map(
        step,
        mesh=mesh,
        in_specs=placed,
        out_specs=P("depth", None, "tiles", None, None),
        check_vma=False,
    )
```

profile of v0, /device:TPU:1, one launch (start us, length us, event | category | flops | bytes accessed | tf_op | source)
XLA Modules:
  0.0 89.0 jit_solution(8606283280287115066)
XLA Ops:
  0.0 1.4 %collective-permute-start.3 = (f32[2,2,256,256]{3,2,1,0:T(8,128)}, f32[2,2,256,256]{3,2,1,0:T(8,128)S(1)}, u32[]{:S(2)}, u32[]{:S(2)}) collective-permute-start(f32[2,2,256,256]{3,2,1,0:T(8,128)} %bitcast.15), channel_id=1, source_target_pairs={{0,64},{1,65},{2,66},{3,67},{4,68},{5,69},{6,70},{7,71},{8,72},{9,... | collective-permute-start | bytes 3145736 | tf_op jit(solution)/shard_map/ppermute | solution.py:330
  2.0 0.8 fusion.6
  2.8 0.1 pad_add_fusion.spot
  2.9 1.5 %collective-permute-start.1 = (s32[4]{0:T(128)S(1)}, s32[4]{0:T(128)S(1)}, u32[]{:S(2)}, u32[]{:S(2)}) collective-permute-start(s32[4]{0:T(128)S(1)} %pad_add_fusion.spot), channel_id=1, source_target_pairs={{0,4},{1,5},{2,6},{3,7},{4,8},{5,9},{6,10},{7,11},{8,12},{9,13},{1... | collective-permute-start | bytes 56 | tf_op jit(solution)/shard_map/ppermute | solution.py:330
  4.4 0.8 rev.3
  5.1 1.1 %negate_multiply_fusion = (f32[1,256,256]{2,1,0:T(8,128)S(1)}, f32[1,256,256]{2,1,0:T(8,128)S(1)}) fusion(), kind=kLoop, calls=%fused_computation.9 | loop fusion | flops 1114112 | bytes 524288 | tf_op jit(solution)/shard_map/mul | solution.py:338
  6.2 0.0 collective-permute-done.3.other
  6.3 0.8 shard_map.64
  7.0 1.3 %collective-permute-start.9 = (f32[2,256,256]{2,1,0:T(8,128)S(1)}, f32[2,256,256]{2,1,0:T(8,128)S(1)}, u32[]{:S(2)}, u32[]{:S(2)}) collective-permute-start(f32[2,256,256]{2,1,0:T(8,128)S(1)} %get-tuple-element.41.own.refs_0_), channel_id=1, source_target_pairs={{0,3},{1,0},{2,1},{3,2},{4,7},{5,4},{6,5},{7,6},{8,11},{9,8},{10,9... | collective-permute-start | bytes 1572872 | tf_op jit(solution)/shard_map/ppermute | solution.py:330
  8.3 1.3 %collective-permute-start.10 = (f32[2,256,256]{2,1,0:T(8,128)S(1)}, f32[2,256,256]{2,1,0:T(8,128)S(1)}, u32[]{:S(2)}, u32[]{:S(2)}) collective-permute-start(f32[2,256,256]{2,1,0:T(8,128)S(1)} %get-tuple-element.42.own.refs_1_), channel_id=1, source_target_pairs={{0,60},{1,61},{2,62},{3,63},{4,0},{5,1},{6,2},{7,3},{8,4},{9,5},{1... | collective-permute-start | bytes 1572872 | tf_op jit(solution)/shard_map/ppermute | solution.py:330
  9.6 1.0 %collective-permute-start.5 = (f32[2,256,256]{2,1,0:T(8,128)S(1)}, f32[2,256,256]{2,1,0:T(8,128)S(1)}, u32[]{:S(2)}, u32[]{:S(2)}) collective-permute-start(f32[2,256,256]{2,1,0:T(8,128)S(1)} %get-tuple-element.40.own.refs_1_), channel_id=1, source_target_pairs={{0,60},{1,61},{2,62},{3,63},{4,0},{5,1},{6,2},{7,3},{8,4},{9,5},{1... | collective-permute-start | bytes 1572872 | tf_op jit(solution)/shard_map/ppermute | solution.py:330
  10.6 1.2 %collective-permute-start.4 = (f32[2,256,256]{2,1,0:T(8,128)S(1)}, f32[2,256,256]{2,1,0:T(8,128)S(1)}, u32[]{:S(2)}, u32[]{:S(2)}) collective-permute-start(f32[2,256,256]{2,1,0:T(8,128)S(1)} %get-tuple-element.39.own.refs_0_), channel_id=1, source_target_pairs={{0,3},{1,0},{2,1},{3,2},{4,7},{5,4},{6,5},{7,6},{8,11},{9,8},{10,9... | collective-permute-start | bytes 1572872 | tf_op jit(solution)/shard_map/ppermute | solution.py:330
  11.8 0.1 slice.26
  12.0 1.0 %collective-permute-start.2 = (s32[4]{0:T(128)S(1)}, s32[4]{0:T(128)S(1)}, u32[]{:S(2)}, u32[]{:S(2)}) collective-permute-start(s32[4]{0:T(128)S(1)} %pad_add_fusion.spot), channel_id=1, source_target_pairs={{0,1},{1,2},{2,3},{3,0},{4,5},{5,6},{6,7},{7,4},{8,9},{9,10},{10,1... | collective-permute-start | bytes 56 | tf_op jit(solution)/shard_map/ppermute | solution.py:330
  12.9 9.1 %collective-permute-done.2 = s32[4]{0:T(128)S(1)} collective-permute-done((s32[4]{0:T(128)S(1)}, s32[4]{0:T(128)S(1)}, u32[]{:S(2)}, u32[]{:S(2)}) %collective-permute-start.2) | collective-permute-done | bytes 48 | tf_op jit(solution)/shard_map/ppermute | solution.py:330
  22.1 3.1 %collective-permute-start = (s32[4]{0:T(128)S(1)}, s32[4]{0:T(128)S(1)}, u32[]{:S(2)}, u32[]{:S(2)}) collective-permute-start(s32[4]{0:T(128)S(1)} %pad_add_fusion.spot), channel_id=1, source_target_pairs={{64,69},{65,70},{66,71},{67,68},{68,73},{69,74},{70,75},{71,72},{7... | collective-permute-start | bytes 56 | tf_op jit(solution)/shard_map/ppermute | solution.py:330
  25.2 0.0 collective-permute-done.9.near.refs_2_
  25.2 3.8 %collective-permute-start.8 = (f32[256,256]{1,0:T(8,128)S(1)}, f32[256,256]{1,0:T(8,128)S(1)}, u32[]{:S(2)}, u32[]{:S(2)}) collective-permute-start(f32[256,256]{1,0:T(8,128)S(1)} %slice_bitcast_fusion), channel_id=1, source_target_pairs={{64,69},{65,70},{66,71},{67,68},{68,73},{69,74},{70,75},{71,72},{7... | collective-permute-start | bytes 786440 | tf_op jit(solution)/shard_map/ppermute | solution.py:330
  29.1 0.6 shard_map.67
  29.7 0.0 collective-permute-done.10.near.refs_3_
  29.7 1.4 %collective-permute-start.11 = (f32[2,256,256]{2,1,0:T(8,128)S(1)}, f32[2,256,256]{2,1,0:T(8,128)S(1)}, u32[]{:S(2)}, u32[]{:S(2)}) collective-permute-start(f32[2,256,256]{2,1,0:T(8,128)S(1)} %shard_map.67), channel_id=1, source_target_pairs={{0,60},{1,61},{2,62},{3,63},{4,0},{5,1},{6,2},{7,3},{8,4},{9,5},{1... | collective-permute-start | bytes 1572872 | tf_op jit(solution)/shard_map/ppermute | solution.py:330
  31.0 0.6 shard_map.68
  31.6 0.0 copy-start.1
  31.7 1.0 %collective-permute-start.12 = (f32[2,256,256]{2,1,0:T(8,128)S(1)}, f32[2,256,256]{2,1,0:T(8,128)S(1)}, u32[]{:S(2)}, u32[]{:S(2)}) collective-permute-start(f32[2,256,256]{2,1,0:T(8,128)S(1)} %shard_map.68), channel_id=1, source_target_pairs={{0,3},{1,0},{2,1},{3,2},{4,7},{5,4},{6,5},{7,6},{8,11},{9,8},{10,9... | collective-permute-start | bytes 1572872 | tf_op jit(solution)/shard_map/ppermute | solution.py:330
  32.6 0.6 shard_map.66
  33.3 1.5 %collective-permute-start.7 = (f32[2,256,256]{2,1,0:T(8,128)S(1)}, f32[2,256,256]{2,1,0:T(8,128)S(1)}, u32[]{:S(2)}, u32[]{:S(2)}) collective-permute-start(f32[2,256,256]{2,1,0:T(8,128)S(1)} %shard_map.66), channel_id=1, source_target_pairs={{0,3},{1,0},{2,1},{3,2},{4,7},{5,4},{6,5},{7,6},{8,11},{9,8},{10,9... | collective-permute-start | bytes 1572872 | tf_op jit(solution)/shard_map/ppermute | solution.py:330
  34.7 0.6 shard_map.65
  35.3 0.0 collective-permute-done
  35.4 1.3 %collective-permute-start.6 = (f32[2,256,256]{2,1,0:T(8,128)S(1)}, f32[2,256,256]{2,1,0:T(8,128)S(1)}, u32[]{:S(2)}, u32[]{:S(2)}) collective-permute-start(f32[2,256,256]{2,1,0:T(8,128)S(1)} %shard_map.65), channel_id=1, source_target_pairs={{0,60},{1,61},{2,62},{3,63},{4,0},{5,1},{6,2},{7,3},{8,4},{9,5},{1... | collective-permute-start | bytes 1572872 | tf_op jit(solution)/shard_map/ppermute | solution.py:330
  36.7 0.1 pad_maximum_fusion.1.taps
  36.8 0.1 broadcast_select_fusion.3.spot
  36.8 2.7 %tables.1 = (bf16[4,512,512]{2,1,0:T(8,128)(2,1)S(1)}, bf16[4,512,512]{2,1,0:T(8,128)(2,1)S(1)}, bf16[4,512,256]{2,1,0:T(8,128)(2,1)S(1)}, bf16[4,512,256]{2,1,0:T(8,128)(2,1)S(1)}) custom-call(s32[4]{0:T(128)S(1)} %broadcast_select_fusion.3.spot, f32[8,256]{1,0:T(8,128)S(1)} %pad_maximum_fusion.1.taps, f32[2,256,256]{2,1,0:T(8,128)S(1)} %pad_maximum_fusion.dft), custom_call_target="tpu_custom_call" | custom-call | tf_op jit(solution)/shard_map/tables/pallas_call | solution.py:94
  39.6 0.0 collective-permute-done.8
  39.6 3.7 %collective-permute-done.11.refs_4_ = f32[2,256,256]{2,1,0:T(8,128)S(1)} collective-permute-done((f32[2,256,256]{2,1,0:T(8,128)S(1)}, f32[2,256,256]{2,1,0:T(8,128)S(1)}, u32[]{:S(2)}, u32[]{:S(2)}) %collective-permute-start.11) | collective-permute-done | bytes 524320 | tf_op jit(solution)/shard_map/ppermute | solution.py:330
  43.4 4.4 %shard_map.69 = (f32[2,256,256]{2,1,0:T(8,128)}, f32[2,256,256]{2,1,0:T(8,128)S(1)}, f32[2,256,256]{2,1,0:T(8,128)S(1)}, f32[2,256,256]{2,1,0:T(8,128)S(1)}, f32[2,256,256]{2,1,0:T(8,128)S(1)}) custom-call(s32[4]{0:T(128)S(1)} %broadcast_select_fusion.3.spot, f32[2,256,256]{2,1,0:T(8,128)S(1)} %get-tuple-element.41.own.refs_0_, ...), custom_call_target="tpu_custom_call" | custom-call | tf_op jit(solution)/shard_map/pallas_call | solution.py:253
  47.8 0.0 collective-permute-done.7.refs_5_
  47.8 1.2 %collective-permute-done.6.refs_4_ = f32[2,256,256]{2,1,0:T(8,128)S(1)} collective-permute-done((f32[2,256,256]{2,1,0:T(8,128)S(1)}, f32[2,256,256]{2,1,0:T(8,128)S(1)}, u32[]{:S(2)}, u32[]{:S(2)}) %collective-permute-start.6) | collective-permute-done | bytes 524320 | tf_op jit(solution)/shard_map/ppermute | solution.py:330
  49.0 6.0 %shard_map.70 = (f32[2,256,256]{2,1,0:T(8,128)S(1)}, f32[2,256,256]{2,1,0:T(8,128)}, f32[2,256,256]{2,1,0:T(8,128)S(1)}, f32[2,256,256]{2,1,0:T(8,128)S(1)}, bf16[2,512,256]{2,1,0:T(8,128)(2,1)S(1)}) custom-call(s32[4]{0:T(128)S(1)} %broadcast_select_fusion.3.spot, f32[2,256,256]{2,1,0:T(8,128)S(1)} %get-tuple-element.39.own.refs_0_, ...), custom_call_target="tpu_custom_call" | custom-call | tf_op jit(solution)/shard_map/pallas_call | solution.py:253
  55.0 1.3 %collective-permute-start.16 = (f32[2,256,256]{2,1,0:T(8,128)S(1)}, f32[2,256,256]{2,1,0:T(8,128)S(1)}, u32[]{:S(2)}, u32[]{:S(2)}) collective-permute-start(f32[2,256,256]{2,1,0:T(8,128)S(1)} %get-tuple-element.65), channel_id=1, source_target_pairs={{0,1},{1,2},{2,3},{3,0},{4,5},{5,6},{6,7},{7,4},{8,9},{9,10},{10,1... | collective-permute-start | bytes 1572872 | tf_op jit(solution)/shard_map/ppermute | solution.py:330
  56.4 2.4 %shard_map.71 = (f32[2,256,256]{2,1,0:T(8,128)S(1)}, f32[2,256,256]{2,1,0:T(8,128)S(1)}, bf16[2,512,256]{2,1,0:T(8,128)(2,1)S(1)}) custom-call(s32[4]{0:T(128)S(1)} %broadcast_select_fusion.3.spot, bf16[2,512,256]{2,1,0:T(8,128)(2,1)S(1)} %get-tuple-element.48.refs_0_, f32[2,256,256]{2,1,0:T(8,128)S(1)} %get-tuple-element.47.refs_7_.refs_1_, ...), custom_call_target="tpu_custom_call" | custom-call | tf_op jit(solution)/shard_map/pallas_call | solution.py:253
  58.8 0.4 collective-permute-start.15
  59.2 2.4 %shard_map.72 = (f32[2,256,256]{2,1,0:T(8,128)S(1)}, f32[2,256,256]{2,1,0:T(8,128)S(1)}, bf16[2,512,256]{2,1,0:T(8,128)(2,1)S(1)}) custom-call(s32[4]{0:T(128)S(1)} %broadcast_select_fusion.3.spot, bf16[2,512,256]{2,1,0:T(8,128)(2,1)S(1)} %get-tuple-element.50.refs_0_, f32[2,256,256]{2,1,0:T(8,128)S(1)} %get-tuple-element.51.refs_1_, ...), custom_call_target="tpu_custom_call" | custom-call | tf_op jit(solution)/shard_map/pallas_call | solution.py:253
  61.6 1.1 %collective-permute-start.14 = (f32[2,256,256]{2,1,0:T(8,128)S(1)}, f32[2,256,256]{2,1,0:T(8,128)S(1)}, u32[]{:S(2)}, u32[]{:S(2)}) collective-permute-start(f32[2,256,256]{2,1,0:T(8,128)S(1)} %get-tuple-element.59), channel_id=1, source_target_pairs={{0,1},{1,2},{2,3},{3,0},{4,5},{5,6},{6,7},{7,4},{8,9},{9,10},{10,1... | collective-permute-start | bytes 1572872 | tf_op jit(solution)/shard_map/ppermute | solution.py:330
  62.7 2.3 %shard_map.73 = (f32[2,256,256]{2,1,0:T(8,128)S(1)}, f32[2,256,256]{2,1,0:T(8,128)S(1)}) custom-call(s32[4]{0:T(128)S(1)} %broadcast_select_fusion.3.spot, bf16[2,512,256]{2,1,0:T(8,128)(2,1)S(1)} %get-tuple-element.53.refs_0_, f32[2,256,256]{2,1,0:T(8,128)S(1)} %get-tuple-element.54.refs_1_, ...), custom_call_target="tpu_custom_call" | custom-call | tf_op jit(solution)/shard_map/pallas_call | solution.py:253
  65.0 0.8 collective-permute-start.13
  65.8 0.1 pad_add_fusion.2
  65.9 0.0 collective-permute-done.16.came
  65.9 0.7 shard_map.77
  66.6 1.5 %collective-permute-start.20 = (f32[2,256,256]{2,1,0:T(8,128)S(1)}, f32[2,256,256]{2,1,0:T(8,128)S(1)}, u32[]{:S(2)}, u32[]{:S(2)}) collective-permute-start(f32[2,256,256]{2,1,0:T(8,128)S(1)} %get-tuple-element.70), channel_id=1, source_target_pairs={{0,4},{1,5},{2,6},{3,7},{4,8},{5,9},{6,10},{7,11},{8,12},{9,13},{1... | collective-permute-start | bytes 1572872 | tf_op jit(solution)/shard_map/ppermute | solution.py:330
  68.1 0.0 collective-permute-done.15.came
  68.1 0.7 shard_map.76
  68.8 0.6 collective-permute-start.19
  69.4 0.6 collective-permute-done.14.came
  70.0 0.7 shard_map.75
  70.7 2.4 %collective-permute-start.18 = (f32[2,256,256]{2,1,0:T(8,128)S(1)}, f32[2,256,256]{2,1,0:T(8,128)S(1)}, u32[]{:S(2)}, u32[]{:S(2)}) collective-permute-start(f32[2,256,256]{2,1,0:T(8,128)S(1)} %get-tuple-element.68), channel_id=1, source_target_pairs={{0,4},{1,5},{2,6},{3,7},{4,8},{5,9},{6,10},{7,11},{8,12},{9,13},{1... | collective-permute-start | bytes 1572872 | tf_op jit(solution)/shard_map/ppermute | solution.py:330
  73.1 0.3 collective-permute-done.13.came
  73.4 0.7 shard_map.74
  74.1 0.9 collective-permute-start.17
  75.0 4.0 %collective-permute-done.20.refs_7_ = f32[2,256,256]{2,1,0:T(8,128)S(1)} collective-permute-done((f32[2,256,256]{2,1,0:T(8,128)S(1)}, f32[2,256,256]{2,1,0:T(8,128)S(1)}, u32[]{:S(2)}, u32[]{:S(2)}) %collective-permute-start.20) | collective-permute-done | bytes 524320 | tf_op jit(solution)/shard_map/ppermute | solution.py:330
  79.0 5.3 %collective-permute-done.18.refs_5_ = f32[2,256,256]{2,1,0:T(8,128)S(1)} collective-permute-done((f32[2,256,256]{2,1,0:T(8,128)S(1)}, f32[2,256,256]{2,1,0:T(8,128)S(1)}, u32[]{:S(2)}, u32[]{:S(2)}) %collective-permute-start.18) | collective-permute-done | bytes 524320 | tf_op jit(solution)/shard_map/ppermute | solution.py:330
  84.4 0.8 shard_map.78
  85.1 0.1 collective-permute-start.21
  85.2 2.6 %collective-permute-done.21 = f32[2,2,256,256]{3,2,1,0:T(8,128)S(1)} collective-permute-done((f32[2,2,256,256]{3,2,1,0:T(8,128)S(1)}, f32[2,2,256,256]{3,2,1,0:T(8,128)S(1)}, u32[]{:S(2)}, u32[]{:S(2)}) %collective-permute-start.21) | collective-permute-done | bytes 1048608 | tf_op jit(solution)/shard_map/ppermute | solution.py:330
  87.9 1.1 %add_bitcast_fusion = f32[2,2,1,256,256]{4,3,2,1,0:T(8,128)} fusion(f32[2,2,256,256]{3,2,1,0:T(8,128)S(1)} %get-tuple-element.71, f32[2,2,256,256]{3,2,1,0:T(8,128)S(1)} %collective-permute-done.21), kind=kLoop, calls=%fused_computation | loop fusion | flops 262144 | bytes 3145728 | tf_op jit(solution)/shard_map/broadcast_in_dim | solution.py:390
  (19 shorter events, 0.1 us)
Async XLA Ops:
  0.0 6.3 %copy-start = (f32[2,2,1,256,256]{4,3,2,1,0:T(8,128)S(1)}, f32[2,2,1,256,256]{4,3,2,1,0:T(8,128)}, u32[]{:S(2)}) copy-start(f32[2,2,1,256,256]{4,3,2,1,0:T(8,128)} %param.6) | copy-start | bytes 3145732
  0.0 11.8 %copy-start.3 = (f32[2,31]{1,0:T(2,128)S(1)}, f32[2,31]{1,0:T(2,128)}, u32[]{:S(2)}) copy-start(f32[2,31]{1,0:T(2,128)} %param.8) | copy-start | bytes 748
  0.0 11.9 %copy-start.2 = (f32[1,2,256,256]{3,2,1,0:T(8,128)S(1)}, f32[1,2,256,256]{3,2,1,0:T(8,128)}, u32[]{:S(2)}) copy-start(f32[1,2,256,256]{3,2,1,0:T(8,128)} %param.9) | copy-start | bytes 1572868
  0.0 6.2 %collective-permute-start.3 = (f32[2,2,256,256]{3,2,1,0:T(8,128)}, f32[2,2,256,256]{3,2,1,0:T(8,128)S(1)}, u32[]{:S(2)}, u32[]{:S(2)}) collective-permute-start(f32[2,2,256,256]{3,2,1,0:T(8,128)} %bitcast.15), channel_id=1, source_target_pairs={{0,64},{1,65},{2,66},{3,67},{4,68},{5,69},{6,70},{7,71},{8,72},{9,... | collective-permute-start | bytes 3145736 | tf_op jit(solution)/shard_map/ppermute | solution.py:330
  2.9 9.1 %collective-permute-start.1 = (s32[4]{0:T(128)S(1)}, s32[4]{0:T(128)S(1)}, u32[]{:S(2)}, u32[]{:S(2)}) collective-permute-start(s32[4]{0:T(128)S(1)} %pad_add_fusion.spot), channel_id=1, source_target_pairs={{0,4},{1,5},{2,6},{3,7},{4,8},{5,9},{6,10},{7,11},{8,12},{9,13},{1... | collective-permute-start | bytes 56 | tf_op jit(solution)/shard_map/ppermute | solution.py:330
  7.0 18.2 %collective-permute-start.9 = (f32[2,256,256]{2,1,0:T(8,128)S(1)}, f32[2,256,256]{2,1,0:T(8,128)S(1)}, u32[]{:S(2)}, u32[]{:S(2)}) collective-permute-start(f32[2,256,256]{2,1,0:T(8,128)S(1)} %get-tuple-element.41.own.refs_0_), channel_id=1, source_target_pairs={{0,3},{1,0},{2,1},{3,2},{4,7},{5,4},{6,5},{7,6},{8,11},{9,8},{10,9... | collective-permute-start | bytes 1572872 | tf_op jit(solution)/shard_map/ppermute | solution.py:330
  8.3 21.4 %collective-permute-start.10 = (f32[2,256,256]{2,1,0:T(8,128)S(1)}, f32[2,256,256]{2,1,0:T(8,128)S(1)}, u32[]{:S(2)}, u32[]{:S(2)}) collective-permute-start(f32[2,256,256]{2,1,0:T(8,128)S(1)} %get-tuple-element.42.own.refs_1_), channel_id=1, source_target_pairs={{0,60},{1,61},{2,62},{3,63},{4,0},{5,1},{6,2},{7,3},{8,4},{9,5},{1... | collective-permute-start | bytes 1572872 | tf_op jit(solution)/shard_map/ppermute | solution.py:330
  9.6 22.0 %collective-permute-start.5 = (f32[2,256,256]{2,1,0:T(8,128)S(1)}, f32[2,256,256]{2,1,0:T(8,128)S(1)}, u32[]{:S(2)}, u32[]{:S(2)}) collective-permute-start(f32[2,256,256]{2,1,0:T(8,128)S(1)} %get-tuple-element.40.own.refs_1_), channel_id=1, source_target_pairs={{0,60},{1,61},{2,62},{3,63},{4,0},{5,1},{6,2},{7,3},{8,4},{9,5},{1... | collective-permute-start | bytes 1572872 | tf_op jit(solution)/shard_map/ppermute | solution.py:330
  10.6 22.6 %collective-permute-start.4 = (f32[2,256,256]{2,1,0:T(8,128)S(1)}, f32[2,256,256]{2,1,0:T(8,128)S(1)}, u32[]{:S(2)}, u32[]{:S(2)}) collective-permute-start(f32[2,256,256]{2,1,0:T(8,128)S(1)} %get-tuple-element.39.own.refs_0_), channel_id=1, source_target_pairs={{0,3},{1,0},{2,1},{3,2},{4,7},{5,4},{6,5},{7,6},{8,11},{9,8},{10,9... | collective-permute-start | bytes 1572872 | tf_op jit(solution)/shard_map/ppermute | solution.py:330
  12.0 10.1 %collective-permute-start.2 = (s32[4]{0:T(128)S(1)}, s32[4]{0:T(128)S(1)}, u32[]{:S(2)}, u32[]{:S(2)}) collective-permute-start(s32[4]{0:T(128)S(1)} %pad_add_fusion.spot), channel_id=1, source_target_pairs={{0,1},{1,2},{2,3},{3,0},{4,5},{5,6},{6,7},{7,4},{8,9},{9,10},{10,1... | collective-permute-start | bytes 56 | tf_op jit(solution)/shard_map/ppermute | solution.py:330
  22.1 13.3 %collective-permute-start = (s32[4]{0:T(128)S(1)}, s32[4]{0:T(128)S(1)}, u32[]{:S(2)}, u32[]{:S(2)}) collective-permute-start(s32[4]{0:T(128)S(1)} %pad_add_fusion.spot), channel_id=1, source_target_pairs={{64,69},{65,70},{66,71},{67,68},{68,73},{69,74},{70,75},{71,72},{7... | collective-permute-start | bytes 56 | tf_op jit(solution)/shard_map/ppermute | solution.py:330
  25.2 14.4 %collective-permute-start.8 = (f32[256,256]{1,0:T(8,128)S(1)}, f32[256,256]{1,0:T(8,128)S(1)}, u32[]{:S(2)}, u32[]{:S(2)}) collective-permute-start(f32[256,256]{1,0:T(8,128)S(1)} %slice_bitcast_fusion), channel_id=1, source_target_pairs={{64,69},{65,70},{66,71},{67,68},{68,73},{69,74},{70,75},{71,72},{7... | collective-permute-start | bytes 786440 | tf_op jit(solution)/shard_map/ppermute | solution.py:330
  29.7 13.7 %collective-permute-start.11 = (f32[2,256,256]{2,1,0:T(8,128)S(1)}, f32[2,256,256]{2,1,0:T(8,128)S(1)}, u32[]{:S(2)}, u32[]{:S(2)}) collective-permute-start(f32[2,256,256]{2,1,0:T(8,128)S(1)} %shard_map.67), channel_id=1, source_target_pairs={{0,60},{1,61},{2,62},{3,63},{4,0},{5,1},{6,2},{7,3},{8,4},{9,5},{1... | collective-permute-start | bytes 1572872 | tf_op jit(solution)/shard_map/ppermute | solution.py:330
  31.6 11.7 %copy-start.1 = (f32[2,256,256]{2,1,0:T(8,128)S(1)}, f32[2,256,256]{2,1,0:T(8,128)}, u32[]{:S(2)}) copy-start(f32[2,256,256]{2,1,0:T(8,128)} %refs_6_.1) | copy-start | bytes 1572868
  31.7 11.7 %collective-permute-start.12 = (f32[2,256,256]{2,1,0:T(8,128)S(1)}, f32[2,256,256]{2,1,0:T(8,128)S(1)}, u32[]{:S(2)}, u32[]{:S(2)}) collective-permute-start(f32[2,256,256]{2,1,0:T(8,128)S(1)} %shard_map.68), channel_id=1, source_target_pairs={{0,3},{1,0},{2,1},{3,2},{4,7},{5,4},{6,5},{7,6},{8,11},{9,8},{10,9... | collective-permute-start | bytes 1572872 | tf_op jit(solution)/shard_map/ppermute | solution.py:330
  33.3 14.6 %collective-permute-start.7 = (f32[2,256,256]{2,1,0:T(8,128)S(1)}, f32[2,256,256]{2,1,0:T(8,128)S(1)}, u32[]{:S(2)}, u32[]{:S(2)}) collective-permute-start(f32[2,256,256]{2,1,0:T(8,128)S(1)} %shard_map.66), channel_id=1, source_target_pairs={{0,3},{1,0},{2,1},{3,2},{4,7},{5,4},{6,5},{7,6},{8,11},{9,8},{10,9... | collective-permute-start | bytes 1572872 | tf_op jit(solution)/shard_map/ppermute | solution.py:330
  35.4 13.6 %collective-permute-start.6 = (f32[2,256,256]{2,1,0:T(8,128)S(1)}, f32[2,256,256]{2,1,0:T(8,128)S(1)}, u32[]{:S(2)}, u32[]{:S(2)}) collective-permute-start(f32[2,256,256]{2,1,0:T(8,128)S(1)} %shard_map.65), channel_id=1, source_target_pairs={{0,60},{1,61},{2,62},{3,63},{4,0},{5,1},{6,2},{7,3},{8,4},{9,5},{1... | collective-permute-start | bytes 1572872 | tf_op jit(solution)/shard_map/ppermute | solution.py:330
  55.0 10.8 %collective-permute-start.16 = (f32[2,256,256]{2,1,0:T(8,128)S(1)}, f32[2,256,256]{2,1,0:T(8,128)S(1)}, u32[]{:S(2)}, u32[]{:S(2)}) collective-permute-start(f32[2,256,256]{2,1,0:T(8,128)S(1)} %get-tuple-element.65), channel_id=1, source_target_pairs={{0,1},{1,2},{2,3},{3,0},{4,5},{5,6},{6,7},{7,4},{8,9},{9,10},{10,1... | collective-permute-start | bytes 1572872 | tf_op jit(solution)/shard_map/ppermute | solution.py:330
  58.8 9.3 %collective-permute-start.15 = (f32[2,256,256]{2,1,0:T(8,128)S(1)}, f32[2,256,256]{2,1,0:T(8,128)S(1)}, u32[]{:S(2)}, u32[]{:S(2)}) collective-permute-start(f32[2,256,256]{2,1,0:T(8,128)S(1)} %get-tuple-element.62), channel_id=1, source_target_pairs={{0,4},{1,5},{2,6},{3,7},{4,8},{5,9},{6,10},{7,11},{8,12},{9,13},{1... | collective-permute-start | bytes 1572872 | tf_op jit(solution)/shard_map/ppermute | solution.py:330
  61.6 8.4 %collective-permute-start.14 = (f32[2,256,256]{2,1,0:T(8,128)S(1)}, f32[2,256,256]{2,1,0:T(8,128)S(1)}, u32[]{:S(2)}, u32[]{:S(2)}) collective-permute-start(f32[2,256,256]{2,1,0:T(8,128)S(1)} %get-tuple-element.59), channel_id=1, source_target_pairs={{0,1},{1,2},{2,3},{3,0},{4,5},{5,6},{6,7},{7,4},{8,9},{9,10},{10,1... | collective-permute-start | bytes 1572872 | tf_op jit(solution)/shard_map/ppermute | solution.py:330
  65.0 8.4 %collective-permute-start.13 = (f32[2,256,256]{2,1,0:T(8,128)S(1)}, f32[2,256,256]{2,1,0:T(8,128)S(1)}, u32[]{:S(2)}, u32[]{:S(2)}) collective-permute-start(f32[2,256,256]{2,1,0:T(8,128)S(1)} %get-tuple-element.56), channel_id=1, source_target_pairs={{0,4},{1,5},{2,6},{3,7},{4,8},{5,9},{6,10},{7,11},{8,12},{9,13},{1... | collective-permute-start | bytes 1572872 | tf_op jit(solution)/shard_map/ppermute | solution.py:330
  66.6 12.5 %collective-permute-start.20 = (f32[2,256,256]{2,1,0:T(8,128)S(1)}, f32[2,256,256]{2,1,0:T(8,128)S(1)}, u32[]{:S(2)}, u32[]{:S(2)}) collective-permute-start(f32[2,256,256]{2,1,0:T(8,128)S(1)} %get-tuple-element.70), channel_id=1, source_target_pairs={{0,4},{1,5},{2,6},{3,7},{4,8},{5,9},{6,10},{7,11},{8,12},{9,13},{1... | collective-permute-start | bytes 1572872 | tf_op jit(solution)/shard_map/ppermute | solution.py:330
  68.8 10.2 %collective-permute-start.19 = (f32[2,256,256]{2,1,0:T(8,128)S(1)}, f32[2,256,256]{2,1,0:T(8,128)S(1)}, u32[]{:S(2)}, u32[]{:S(2)}) collective-permute-start(f32[2,256,256]{2,1,0:T(8,128)S(1)} %get-tuple-element.69), channel_id=1, source_target_pairs={{0,1},{1,2},{2,3},{3,0},{4,5},{5,6},{6,7},{7,4},{8,9},{9,10},{10,1... | collective-permute-start | bytes 1572872 | tf_op jit(solution)/shard_map/ppermute | solution.py:330
  70.7 13.7 %collective-permute-start.18 = (f32[2,256,256]{2,1,0:T(8,128)S(1)}, f32[2,256,256]{2,1,0:T(8,128)S(1)}, u32[]{:S(2)}, u32[]{:S(2)}) collective-permute-start(f32[2,256,256]{2,1,0:T(8,128)S(1)} %get-tuple-element.68), channel_id=1, source_target_pairs={{0,4},{1,5},{2,6},{3,7},{4,8},{5,9},{6,10},{7,11},{8,12},{9,13},{1... | collective-permute-start | bytes 1572872 | tf_op jit(solution)/shard_map/ppermute | solution.py:330
  74.1 10.2 %collective-permute-start.17 = (f32[2,256,256]{2,1,0:T(8,128)S(1)}, f32[2,256,256]{2,1,0:T(8,128)S(1)}, u32[]{:S(2)}, u32[]{:S(2)}) collective-permute-start(f32[2,256,256]{2,1,0:T(8,128)S(1)} %get-tuple-element.67), channel_id=1, source_target_pairs={{0,1},{1,2},{2,3},{3,0},{4,5},{5,6},{6,7},{7,4},{8,9},{9,10},{10,1... | collective-permute-start | bytes 1572872 | tf_op jit(solution)/shard_map/ppermute | solution.py:330
  85.1 2.7 %collective-permute-start.21 = (f32[2,2,256,256]{3,2,1,0:T(8,128)S(1)}, f32[2,2,256,256]{3,2,1,0:T(8,128)S(1)}, u32[]{:S(2)}, u32[]{:S(2)}) collective-permute-start(f32[2,2,256,256]{3,2,1,0:T(8,128)S(1)} %get-tuple-element.72), channel_id=1, source_target_pairs={{0,64},{1,65},{2,66},{3,67},{4,68},{5,69},{6,70},{7,71},{8,72},{9,... | collective-permute-start | bytes 3145736 | tf_op jit(solution)/shard_map/ppermute | solution.py:330
where the time goes:
time: 89.1 us; the launch traced here: 89 us
  starting transfers between devices  29.9 us (34%)
  Pallas kernels  27 us (30%)
  waiting for transfers between devices  26.9 us (30%)
  other arithmetic  3.31 us (4%)
  between operations  0.94 us (1%)
    ppermute x22, starting transfers between devices, permute(): return lax.ppermute(block, ('depth', 'tiles'), pairs)  29.9 us
    ppermute x22, waiting for transfers between devices, permute(): return lax.ppermute(block, ('depth', 'tiles'), pairs)  26.9 us
    pallas_call x15, Pallas kernels, call(): pl.pallas_call(kernel, out_shape=outs, in_specs=[SS] + [VS] * len(args),...  24.3 us
    pallas_call x1, Pallas kernels, tables(): pl.pallas_call(tables_kernel, out_shape=[jax.ShapeDtypeStruct((4, 2 * N,...  2.74 us
  transfers between devices with their start and end apart: 22, of which 8 were waited for; matrix products, arithmetic and copies ran while one was open for 3% of the time, Pallas kernels for 23%

commit v1 on v0

--- a/solution.py
+++ b/solution.py
@@ -140,23 +140,27 @@
 def propagate(work, tabs, index):
     x_high, x_low, y_high, y_low, acc = work
     left_high, left_low, right_high, right_low = tabs
-    acc[...] = dot3(left_high[index], left_low[index], x_high[...], x_low[...])
-    for sl, s2, r0 in chunks():
-        for ref, r, m in zip((y_high, y_low), split(acc[sl]), split(acc[s2])):
+    half = N // 2
+    spans = [(pl.ds(h * half, half), pl.ds(N + h * half, half)) for h in range(2)]
+    for sl, s2 in spans:
+        re = dot3(left_high[index, sl], left_low[index, sl], x_high[...], x_low[...])
+        im = dot3(left_high[index, s2], left_low[index, s2], x_high[...], x_low[...])
+        for ref, r, m in zip((y_high, y_low), split(re), split(im)):
             ref[sl, 0:N] = r
             ref[s2, N : 2 * N] = r
             ref[s2, 0:N] = m
             ref[sl, N : 2 * N] = -m
-    acc[...] = dot3(y_high[...], y_low[...], right_high[index], right_low[index])
-
-
-def gather_patch(spot, p, own, near, far, out):
+    for span in spans:
+        for part in span:
+            acc[part] = dot3(y_high[part], y_low[part], right_high[index], right_low[index])
+
+
+def gather_patch(spot, p, inner, far, out):
     mine_cols = own_cols(spot)
     for sl, _, r0 in chunks():
-        mine_rows = own_rows(spot, r0)
-        inner, outer = (mine_cols, mine_rows) if p % 2 == 0 else (mine_rows, mine_cols)
+        mask = own_rows(spot, r0) if p % 2 == 0 else mine_cols
         for c in range(2):
-            out[c, sl] = jnp.where(outer, jnp.where(inner, own[c, sl], near[c, sl]), far[c, sl])
+            out[c, sl] = jnp.where(mask, inner[c, sl], far[c, sl])
 
 
 def enter_slice(work, patch, wave):
@@ -187,40 +191,47 @@
 
 
 def first_kernel(spot, *refs):
-    own, near, far = refs[0:2], refs[2:4], refs[4:6]
-    probe, tabs = refs[6], refs[7:11]
-    patches, waves = refs[11:13], refs[13:16]
-    work = refs[16:]
+    inner, far = refs[0:2], refs[2:4]
+    probe, tabs = refs[4], refs[5:9]
+    patches, waves = refs[9:11], refs[11:14]
+    work = refs[14:]
     for c in range(2):
         waves[0][c] = pltpu.roll(pltpu.roll(probe[c], spot[0], 0), spot[1], 1)
     for p in range(2):
-        gather_patch(spot, p, own[p], near[p], far[p], patches[p])
+        gather_patch(spot, p, inner[p], far[p], patches[p])
         enter_slice(work, patches[p], waves[p])
         propagate(work, tabs, 0)
         leave(work, waves[p + 1])
 
 
 def second_kernel(spot, *refs):
-    own, near, far = refs[0:2], refs[2:4], refs[4:6]
-    measured, wave, tabs = refs[6], refs[7], refs[8:12]
-    patch, middle, grad, sent, state = refs[12:17]
-    last = refs[17:19]
-    work = refs[19:]
+    inner, far = refs[0:2], refs[2:4]
+    wave, tabs = refs[4], refs[5:9]
+    patches, middle, spectrum = refs[9:11], refs[11], refs[12]
+    work = refs[13:]
     for p in range(2):
-        gather_patch(spot, p, own[p], near[p], far[p], (patch, last[0])[p])
-    enter_slice(work, patch, wave)
+        gather_patch(spot, p, inner[p], far[p], patches[p])
+    enter_slice(work, patches[0], wave)
     propagate(work, tabs, 0)
     leave(work, middle)
-    enter_slice(work, last[0], middle)
+    enter_slice(work, patches[1], middle)
     propagate(work, tabs, 2)
-    acc = work[4]
+    leave(work, spectrum)
+
+
+def third_kernel(spot, *refs):
+    spectrum, measured, shared, wave, patch, tabs = refs[0], refs[1], refs[2], refs[3], refs[4], refs[5:9]
+    grad, sent, state = refs[9:12]
+    work = refs[12:]
+    upper = spot[2] == 1
     scale = 2.0 * spot[3].astype(F32)
-    for sl, s2, r0 in chunks():
-        sr, si = acc[sl], acc[s2]
-        misfit = (sr * sr + si * si - measured[sl]) * scale
+    for sl, _, r0 in chunks():
+        sr, si = spectrum[0, sl], spectrum[1, sl]
+        target = jnp.where(upper, shared[sl], measured[sl])
+        misfit = (sr * sr + si * si - target) * scale
         put_field(work, r0, misfit * sr, misfit * si)
     propagate(work, tabs, 3)
-    leave_slice(work, spot, 3, last[0], middle, grad, sent, True)
+    leave_slice(work, spot, 3, patch, wave, grad, sent, True)
     state[0] = work[0][...]
     state[1] = work[1][...]
 
@@ -249,7 +260,7 @@
 
 
 def call(kernel, outs, spot, args, scratch=()):
-    room = (20 if scratch else 8) << 20
+    room = (12 if scratch else 6) << 20
     return pl.pallas_call(
         kernel,
         out_shape=outs,
@@ -260,12 +271,14 @@
     )(spot, *args)
 
 
-def blend_kernel(by_rows, spot, own, near, out):
-    mine_cols = own_cols(spot)
+def blend_kernel(by_rows, spots, own, near, mixed, inner):
+    here = [spots[i] for i in range(3)]
+    there = [spots[4 + i] for i in range(3)]
     for sl, _, r0 in chunks():
-        mask = own_rows(spot, r0) if by_rows else mine_cols
-        for c in range(2):
-            out[c, sl] = jnp.where(mask, own[c, sl], near[c, sl])
+        for spot, out in ((there, mixed), (here, inner)):
+            mask = own_rows(spot, r0) if by_rows else own_cols(spot)
+            for c in range(2):
+                out[c, sl] = jnp.where(mask, own[c, sl], near[c, sl])
 
 
 def turn_kernel(p, spots, grad, came, sent, kept):
@@ -286,16 +299,23 @@
 
 
 def merge_kernel(spot, *refs):
-    kept, went = refs[0:4], refs[4:8]
-    stay, leave_ = refs[8], refs[9]
+    kept, went, stay, leaving = refs[0:4], refs[4:6], refs[6], refs[7]
     upper = spot[2] == 1
     for q in range(2):
         for c in range(2):
             for sl, _, _ in chunks():
-                low = kept[q][c, sl] + went[q][c, sl]
-                high = kept[q + 2][c, sl] + went[q + 2][c, sl]
+                low = kept[q][c, sl]
+                high = kept[q + 2][c, sl] + went[q][c, sl]
                 stay[q, c, sl] = jnp.where(upper, high, low)
-                leave_[q, c, sl] = jnp.where(upper, low, high)
+                leaving[q, c, sl] = jnp.where(upper, low, high)
+
+
+def final_kernel(spot, stay, back, *refs):
+    out = refs[4]
+    for q in range(2):
+        for c in range(2):
+            for sl, _, _ in chunks():
+                out[q, c, sl] = (stay[q, c, sl] + back[q, c, sl]) + (refs[q][c, sl] + refs[q + 2][c, sl])
 
 
 def order_kernel(spot, mine, other, *outs):
@@ -322,6 +342,8 @@
 GATHER = (pairs_of((-1, 0), (1, 0)), pairs_of((0, -1), (0, 1)))
 SCATTER = (pairs_of((1, 0), (-1, 0)), pairs_of((0, 1), (0, -1)))
 INFO = (pairs_of((1, 0), (1, 0)), pairs_of((0, 1), (0, 1)))
+STRAIGHT = [[(a, b) for a, b in way if a < TILES] for way in SCATTER]
+CROSSED = [[(a, b - TILES) for a, b in way if a >= TILES] for way in SCATTER]
 DIAGONAL = pairs_of(None, (1, 1))
 SWAP = [(d * TILES + t, (1 - d) * TILES + t) for d in range(2) for t in range(TILES)]
 
@@ -345,8 +367,8 @@
     alive = (core < counts[0]).astype(jnp.int32)
     info = jnp.concatenate([jnp.where(core == 0, offsets[0, 0], offsets[0, 1]), core[None], alive[None]])
     left = permute(info, INFO[0])
-    up = permute(info, INFO[1])
-    upleft = permute(info, DIAGONAL)
+    above = permute(jnp.concatenate([info, left]), INFO[1])
+    up, upleft = above[:4], above[4:]
     here = jnp.where(core == 0, info, upleft)
     at_y = jnp.where(core == 0, up, left)
     at_x = jnp.where(core == 0, left, up)
@@ -354,19 +376,20 @@
 
     near = [permute(own[p], GATHER[p % 2]) for p in range(4)]
     shared = permute(intensity[0, 1], DIAGONAL)
-    measured = jnp.where(core == 0, intensity[0, 0], shared)
-    far = []
+    far, inner = [], []
+    both = [jnp.concatenate([here, spot]) for spot in (at_y, at_x)]
     for p in range(4):
-        mixed, = call(functools.partial(blend_kernel, p % 2 == 1), [FIELD], (at_y, at_x)[p % 2], [own[p], near[p]])
+        mixed, kept = call(functools.partial(blend_kernel, p % 2 == 1), [FIELD] * 2, both[p % 2], [own[p], near[p]])
+        inner.append(kept)
         far.append(permute(mixed, GATHER[1 - p % 2]))
 
     tabs = tables(here, tap_rows(fresnel_taps), fourier())
     _, patch1, wave0, wave1, wave2 = call(
-        first_kernel, [FIELD] * 5, here, [*own[:2], *near[:2], *far[:2], illumination, *tabs], WORK
+        first_kernel, [FIELD] * 5, here, [*inner[:2], *far[:2], illumination, *tabs], WORK
     )
-    patch2, _, grad3, sent3, state = call(
-        second_kernel, [FIELD] * 4 + [STATE], here, [*own[2:], *near[2:], *far[2:], measured, wave2, *tabs],
-        [pltpu.VMEM((2, N, N), F32)] * 2 + WORK
+    patch2, patch3, wave3, spectrum = call(second_kernel, [FIELD] * 4, here, [*inner[2:], *far[2:], wave2, *tabs], WORK)
+    grad3, sent3, state = call(
+        third_kernel, [FIELD] * 2 + [STATE], here, [spectrum, intensity[0, 0], shared, wave3, patch3, *tabs], WORK
     )
     grads = [None, None, None, grad3]
     came = [None, None, None, permute(sent3, SCATTER[0])]
@@ -381,13 +404,17 @@
         state = outs[2] if onward else None
     kept, went = [None] * 4, [None] * 4
     for p in (3, 2, 1, 0):
-        spots = jnp.concatenate([here, (at_y, at_x)[p % 2]])
-        sent, kept[p] = call(functools.partial(turn_kernel, p), [FIELD] * 2, spots, [grads[p], came[p]])
-        went[p] = permute(sent, SCATTER[p % 2])
+        sent, kept[p] = call(functools.partial(turn_kernel, p), [FIELD] * 2, both[p % 2], [grads[p], came[p]])
+        if p > 1:
+            went[p] = permute(sent, SCATTER[p % 2])
+        else:
+            went[p] = [permute(sent, way[p % 2]) for way in (STRAIGHT, CROSSED)]
     pair = jax.ShapeDtypeStruct((2, 2, N, N), F32)
-    stay, leaving = call(merge_kernel, [pair] * 2, here, [*kept, *went])
+    stay, leaving = call(merge_kernel, [pair] * 2, here, [*kept, went[2], went[3]])
     back = permute(leaving, SWAP)
-    return (stay + back)[:, :, None]
+    last = [went[0][0], went[1][0], went[0][1], went[1][1]]
+    out, = call(final_kernel, [pair], here, [stay, back, *last])
+    return out[:, :, None]
 
 
 def solution(mesh):

time: 89.1 us -> 101 us (1.13)
  waiting for transfers between devices: 26.9 us -> 35.3 us
  local copies, waits for them, and re-layouts: 0.88 us -> 2.95 us
  Pallas kernels: 27 us -> 28.3 us
  starting transfers between devices: 29.9 us -> 31.1 us
  other arithmetic: 3.31 us -> 2.24 us
    ppermute x22 -> x23, waiting for transfers between devices: 26.9 us -> 35.3 us  [permute(): return lax.ppermute(block, ('depth', 'tiles'), pairs)]
    unnamed x8 -> x12, local copies, waits for them, and re-layouts: 0.02 us -> 2.05 us
    ppermute x22 -> x23, starting transfers between devices: 29.9 us -> 31.1 us  [permute(): return lax.ppermute(block, ('depth', 'tiles'), pairs)]
    pallas_call x15 -> x17, Pallas kernels: 24.3 us -> 25.6 us  [call(): pl.pallas_call(kernel, out_shape=outs, in_specs=[SS] + [VS] * len(args),...]
    broadcast_in_dim x1 -> x0, other arithmetic: 1.1 us -> none  [step(): return (stay + back)[:, :, None]]
  transfers between devices with their start and end apart: 22 -> 23, of which waited for: 8 -> 10; matrix products, arithmetic and copies ran while one was open for 3% -> 3% of each run, Pallas kernels for 23% -> 23%
where the time goes in v1:
time: 101 us
  waiting for transfers between devices  35.3 us (35%)
  starting transfers between devices  31.1 us (31%)
  Pallas kernels  28.3 us (28%)
  local copies, waits for them, and re-layouts  2.95 us (3%)
  other arithmetic  2.24 us (2%)
    ppermute x23, waiting for transfers between devices, permute(): return lax.ppermute(block, ('depth', 'tiles'), pairs)  35.3 us
    ppermute x23, starting transfers between devices, permute(): return lax.ppermute(block, ('depth', 'tiles'), pairs)  31.1 us
    pallas_call x17, Pallas kernels, call(): pl.pallas_call(kernel, out_shape=outs, in_specs=[SS] + [VS] * len(args),...  25.6 us
    pallas_call x1, Pallas kernels, tables(): pl.pallas_call(tables_kernel, out_shape=[jax.ShapeDtypeStruct((4, 2 * N,...  2.74 us
    unnamed x12, local copies, waits for them, and re-layouts  2.05 us
  transfers between devices with their start and end apart: 23, of which 10 were waited for; matrix products, arithmetic and copies ran while one was open for 3% of the time, Pallas kernels for 23%

profile of v1, /device:TPU:1, one launch (start us, length us, event | category | flops | bytes accessed | tf_op | source)
XLA Modules:
  0.0 100.9 jit_solution(11390808558126913562)
XLA Ops:
  0.0 1.4 %collective-permute-start.2 = (f32[2,2,256,256]{3,2,1,0:T(8,128)}, f32[2,2,256,256]{3,2,1,0:T(8,128)S(1)}, u32[]{:S(2)}, u32[]{:S(2)}) collective-permute-start(f32[2,2,256,256]{3,2,1,0:T(8,128)} %bitcast.14), channel_id=1, source_target_pairs={{0,64},{1,65},{2,66},{3,67},{4,68},{5,69},{6,70},{7,71},{8,72},{9,... | collective-permute-start | bytes 3145736 | tf_op jit(solution)/shard_map/ppermute | solution.py:352
  2.0 0.8 fusion.6
  2.8 0.1 pad_add_fusion.spot
  2.9 1.0 collective-permute-done.2.other
  3.9 1.2 %copy-done = f32[2,2,1,256,256]{4,3,2,1,0:T(8,128)S(1)} copy-done((f32[2,2,1,256,256]{4,3,2,1,0:T(8,128)S(1)}, f32[2,2,1,256,256]{4,3,2,1,0:T(8,128)}, u32[]{:S(2)}) %copy-start) | copy-done | bytes 1048600
  5.1 0.8 shard_map.64
  5.9 1.5 %collective-permute-start.8 = (f32[2,256,256]{2,1,0:T(8,128)S(1)}, f32[2,256,256]{2,1,0:T(8,128)S(1)}, u32[]{:S(2)}, u32[]{:S(2)}) collective-permute-start(f32[2,256,256]{2,1,0:T(8,128)S(1)} %get-tuple-element.58.own), channel_id=1, source_target_pairs={{0,60},{1,61},{2,62},{3,63},{4,0},{5,1},{6,2},{7,3},{8,4},{9,5},{1... | collective-permute-start | bytes 1572872 | tf_op jit(solution)/shard_map/ppermute | solution.py:352
  7.3 1.2 %collective-permute-start.7 = (f32[2,256,256]{2,1,0:T(8,128)S(1)}, f32[2,256,256]{2,1,0:T(8,128)S(1)}, u32[]{:S(2)}, u32[]{:S(2)}) collective-permute-start(f32[2,256,256]{2,1,0:T(8,128)S(1)} %get-tuple-element.56.own), channel_id=1, source_target_pairs={{0,3},{1,0},{2,1},{3,2},{4,7},{5,4},{6,5},{7,6},{8,11},{9,8},{10,9... | collective-permute-start | bytes 1572872 | tf_op jit(solution)/shard_map/ppermute | solution.py:352
  8.6 1.3 %collective-permute-start.4 = (f32[2,256,256]{2,1,0:T(8,128)S(1)}, f32[2,256,256]{2,1,0:T(8,128)S(1)}, u32[]{:S(2)}, u32[]{:S(2)}) collective-permute-start(f32[2,256,256]{2,1,0:T(8,128)S(1)} %get-tuple-element.52.own), channel_id=1, source_target_pairs={{0,60},{1,61},{2,62},{3,63},{4,0},{5,1},{6,2},{7,3},{8,4},{9,5},{1... | collective-permute-start | bytes 1572872 | tf_op jit(solution)/shard_map/ppermute | solution.py:352
  9.9 1.2 %collective-permute-start.3 = (f32[2,256,256]{2,1,0:T(8,128)S(1)}, f32[2,256,256]{2,1,0:T(8,128)S(1)}, u32[]{:S(2)}, u32[]{:S(2)}) collective-permute-start(f32[2,256,256]{2,1,0:T(8,128)S(1)} %get-tuple-element.50.own), channel_id=1, source_target_pairs={{0,3},{1,0},{2,1},{3,2},{4,7},{5,4},{6,5},{7,6},{8,11},{9,8},{10,9... | collective-permute-start | bytes 1572872 | tf_op jit(solution)/shard_map/ppermute | solution.py:352
  11.1 0.9 collective-permute-start
  12.0 10.3 %collective-permute-done = s32[4]{0:T(128)S(1)} collective-permute-done((s32[4]{0:T(128)S(1)}, s32[4]{0:T(128)S(1)}, u32[]{:S(2)}, u32[]{:S(2)}) %collective-permute-start) | collective-permute-done | bytes 48 | tf_op jit(solution)/shard_map/ppermute | solution.py:352
  22.3 0.1 pad_add_fusion.1
  22.4 1.3 %collective-permute-start.1 = (s32[8]{0:T(128)S(1)}, s32[8]{0:T(128)S(1)}, u32[]{:S(2)}, u32[]{:S(2)}) collective-permute-start(s32[8]{0:T(128)S(1)} %pad_add_fusion.1), channel_id=1, source_target_pairs={{0,4},{1,5},{2,6},{3,7},{4,8},{5,9},{6,10},{7,11},{8,12},{9,13},{1... | collective-permute-start | bytes 104 | tf_op jit(solution)/shard_map/ppermute | solution.py:352
  23.7 4.9 %collective-permute-done.1 = s32[8]{0:T(128)S(1)} collective-permute-done((s32[8]{0:T(128)S(1)}, s32[8]{0:T(128)S(1)}, u32[]{:S(2)}, u32[]{:S(2)}) %collective-permute-start.1) | collective-permute-done | bytes 64 | tf_op jit(solution)/shard_map/ppermute | solution.py:352
  28.5 0.1 broadcast_select_fusion.1
  28.6 0.1 pad_add_fusion.3
  28.7 0.0 collective-permute-done.8.near
  28.7 1.5 %shard_map.68 = (f32[2,256,256]{2,1,0:T(8,128)}, f32[2,256,256]{2,1,0:T(8,128)S(1)}) custom-call(s32[8]{0:T(128)S(1)} %get-tuple-element.99.spots, f32[2,256,256]{2,1,0:T(8,128)S(1)} %get-tuple-element.58.own, f32[2,256,256]{2,1,0:T(8,128)S(1)} %collective-permute-done.8.near), custom_call_target="tpu_custom_call" | custom-call | tf_op jit(solution)/shard_map/pallas_call | solution.py:264
  30.2 0.0 collective-permute-start.10
  30.2 1.5 %shard_map.67 = (f32[2,256,256]{2,1,0:T(8,128)}, f32[2,256,256]{2,1,0:T(8,128)S(1)}) custom-call(s32[8]{0:T(128)S(1)} %get-tuple-element.100.spots, f32[2,256,256]{2,1,0:T(8,128)S(1)} %get-tuple-element.56.own, f32[2,256,256]{2,1,0:T(8,128)S(1)} %collective-permute-done.7.near), custom_call_target="tpu_custom_call" | custom-call | tf_op jit(solution)/shard_map/pallas_call | solution.py:264
  31.7 1.5 %shard_map.66 = (f32[2,256,256]{2,1,0:T(8,128)}, f32[2,256,256]{2,1,0:T(8,128)S(1)}) custom-call(s32[8]{0:T(128)S(1)} %get-tuple-element.99.spots, f32[2,256,256]{2,1,0:T(8,128)S(1)} %get-tuple-element.52.own, f32[2,256,256]{2,1,0:T(8,128)S(1)} %collective-permute-done.4.near), custom_call_target="tpu_custom_call" | custom-call | tf_op jit(solution)/shard_map/pallas_call | solution.py:264
  33.2 1.2 %collective-permute-start.6 = (f32[2,256,256]{2,1,0:T(8,128)}, f32[2,256,256]{2,1,0:T(8,128)S(1)}, u32[]{:S(2)}, u32[]{:S(2)}) collective-permute-start(f32[2,256,256]{2,1,0:T(8,128)} %get-tuple-element.55), channel_id=1, source_target_pairs={{0,3},{1,0},{2,1},{3,2},{4,7},{5,4},{6,5},{7,6},{8,11},{9,8},{10,9... | collective-permute-start | bytes 1572872 | tf_op jit(solution)/shard_map/ppermute | solution.py:352
  34.4 0.0 collective-permute-done.3.near
  34.4 1.4 %shard_map.65 = (f32[2,256,256]{2,1,0:T(8,128)}, f32[2,256,256]{2,1,0:T(8,128)S(1)}) custom-call(s32[8]{0:T(128)S(1)} %get-tuple-element.100.spots, f32[2,256,256]{2,1,0:T(8,128)S(1)} %get-tuple-element.50.own, f32[2,256,256]{2,1,0:T(8,128)S(1)} %collective-permute-done.3.near), custom_call_target="tpu_custom_call" | custom-call | tf_op jit(solution)/shard_map/pallas_call | solution.py:264
  35.8 0.8 copy-done.2
  36.7 0.7 slice_bitcast_fusion
  37.4 2.8 %collective-permute-start.11 = (f32[256,256]{1,0:T(8,128)}, f32[256,256]{1,0:T(8,128)}, u32[]{:S(2)}, u32[]{:S(2)}) collective-permute-start(f32[256,256]{1,0:T(8,128)} %get-tuple-element.95), channel_id=1, source_target_pairs={{64,69},{65,70},{66,71},{67,68},{68,73},{69,74},{70,75},{71,72},{7... | collective-permute-start | bytes 786440 | tf_op jit(solution)/shard_map/ppermute | solution.py:352
  40.2 0.1 rev.3
  40.3 0.1 slice.34
  40.4 0.1 pad_maximum_fusion.1.taps
  40.4 1.1 %negate_multiply_fusion = (f32[1,256,256]{2,1,0:T(8,128)S(1)}, f32[1,256,256]{2,1,0:T(8,128)S(1)}) fusion(), kind=kLoop, calls=%fused_computation.9 | loop fusion | flops 1114112 | bytes 524288 | tf_op jit(solution)/shard_map/mul | solution.py:360
  41.5 2.7 %tables.1 = (bf16[4,512,512]{2,1,0:T(8,128)(2,1)S(1)}, bf16[4,512,512]{2,1,0:T(8,128)(2,1)S(1)}, bf16[4,512,256]{2,1,0:T(8,128)(2,1)S(1)}, bf16[4,512,256]{2,1,0:T(8,128)(2,1)S(1)}) custom-call(s32[4]{0:T(128)S(1)} %get-tuple-element.101.spot, f32[8,256]{1,0:T(8,128)S(1)} %pad_maximum_fusion.1.taps, f32[2,256,256]{2,1,0:T(8,128)S(1)} %pad_maximum_fusion.dft), custom_call_target="tpu_custom_call" | custom-call | tf_op jit(solution)/shard_map/tables/pallas_call | solution.py:94
  44.3 0.0 collective-permute-done.10.refs_3_
  44.3 3.5 %shard_map.69 = (f32[2,256,256]{2,1,0:T(8,128)}, f32[2,256,256]{2,1,0:T(8,128)S(1)}, f32[2,256,256]{2,1,0:T(8,128)S(1)}, f32[2,256,256]{2,1,0:T(8,128)S(1)}, f32[2,256,256]{2,1,0:T(8,128)S(1)}) custom-call(s32[4]{0:T(128)S(1)} %get-tuple-element.101.spot, f32[2,256,256]{2,1,0:T(8,128)S(1)} %get-tuple-element.57.refs_0_, ...), custom_call_target="tpu_custom_call" | custom-call | tf_op jit(solution)/shard_map/pallas_call | solution.py:264
  47.8 3.9 %collective-permute-done.5.refs_2_ = f32[2,256,256]{2,1,0:T(8,128)} collective-permute-done((f32[2,256,256]{2,1,0:T(8,128)}, f32[2,256,256]{2,1,0:T(8,128)}, u32[]{:S(2)}, u32[]{:S(2)}) %collective-permute-start.5) | collective-permute-done | bytes 524320 | tf_op jit(solution)/shard_map/ppermute | solution.py:352
  51.8 3.2 %shard_map.70 = (f32[2,256,256]{2,1,0:T(8,128)S(1)}, f32[2,256,256]{2,1,0:T(8,128)S(1)}, f32[2,256,256]{2,1,0:T(8,128)S(1)}, f32[2,256,256]{2,1,0:T(8,128)S(1)}) custom-call(s32[4]{0:T(128)S(1)} %get-tuple-element.101.spot, f32[2,256,256]{2,1,0:T(8,128)S(1)} %copy-done.3, f32[2,256,256]{2,1,0:T(8,128)S(1)} %get-tuple-element.53.refs_1_, ...), custom_call_target="tpu_custom_call" | custom-call | tf_op jit(solution)/shard_map/pallas_call | solution.py:264
  55.0 2.2 %shard_map.71 = (f32[2,256,256]{2,1,0:T(8,128)S(1)}, f32[2,256,256]{2,1,0:T(8,128)S(1)}, bf16[2,512,256]{2,1,0:T(8,128)(2,1)S(1)}) custom-call(s32[4]{0:T(128)S(1)} %get-tuple-element.101.spot, f32[2,256,256]{2,1,0:T(8,128)S(1)} %get-tuple-element.67.refs_0_, f32[256,256]{1,0:T(8,128)S(1)} %get-tuple-element.96.refs_1_, ...), custom_call_target="tpu_custom_call" | custom-call | tf_op jit(solution)/shard_map/pallas_call | solution.py:264
  57.2 2.8 %collective-permute-start.15 = (f32[2,256,256]{2,1,0:T(8,128)S(1)}, f32[2,256,256]{2,1,0:T(8,128)S(1)}, u32[]{:S(2)}, u32[]{:S(2)}) collective-permute-start(f32[2,256,256]{2,1,0:T(8,128)S(1)} %get-tuple-element.87), channel_id=1, source_target_pairs={{0,1},{1,2},{2,3},{3,0},{4,5},{5,6},{6,7},{7,4},{8,9},{9,10},{10,1... | collective-permute-start | bytes 1572872 | tf_op jit(solution)/shard_map/ppermute | solution.py:352
  59.9 1.6 %shard_map.72 = (f32[2,256,256]{2,1,0:T(8,128)S(1)}, f32[2,256,256]{2,1,0:T(8,128)S(1)}, bf16[2,512,256]{2,1,0:T(8,128)(2,1)S(1)}) custom-call(s32[4]{0:T(128)S(1)} %get-tuple-element.101.spot, bf16[2,512,256]{2,1,0:T(8,128)(2,1)S(1)} %get-tuple-element.70.refs_0_, f32[2,256,256]{2,1,0:T(8,128)S(1)} %get-tuple-element.66.refs_4_.refs_1_, ...), custom_call_target="tpu_custom_call" | custom-call | tf_op jit(solution)/shard_map/pallas_call | solution.py:264
  61.6 0.1 collective-permute-start.14
  61.7 1.6 %shard_map.73 = (f32[2,256,256]{2,1,0:T(8,128)S(1)}, f32[2,256,256]{2,1,0:T(8,128)S(1)}, bf16[2,512,256]{2,1,0:T(8,128)(2,1)S(1)}) custom-call(s32[4]{0:T(128)S(1)} %get-tuple-element.101.spot, bf16[2,512,256]{2,1,0:T(8,128)(2,1)S(1)} %get-tuple-element.72.refs_0_, f32[2,256,256]{2,1,0:T(8,128)S(1)} %get-tuple-element.73.refs_1_, ...), custom_call_target="tpu_custom_call" | custom-call | tf_op jit(solution)/shard_map/pallas_call | solution.py:264
  63.3 1.1 %collective-permute-start.13 = (f32[2,256,256]{2,1,0:T(8,128)S(1)}, f32[2,256,256]{2,1,0:T(8,128)S(1)}, u32[]{:S(2)}, u32[]{:S(2)}) collective-permute-start(f32[2,256,256]{2,1,0:T(8,128)S(1)} %get-tuple-element.81), channel_id=1, source_target_pairs={{0,1},{1,2},{2,3},{3,0},{4,5},{5,6},{6,7},{7,4},{8,9},{9,10},{10,1... | collective-permute-start | bytes 1572872 | tf_op jit(solution)/shard_map/ppermute | solution.py:352
  64.4 1.6 %shard_map.74 = (f32[2,256,256]{2,1,0:T(8,128)S(1)}, f32[2,256,256]{2,1,0:T(8,128)S(1)}) custom-call(s32[4]{0:T(128)S(1)} %get-tuple-element.101.spot, bf16[2,512,256]{2,1,0:T(8,128)(2,1)S(1)} %get-tuple-element.75.refs_0_, f32[2,256,256]{2,1,0:T(8,128)S(1)} %get-tuple-element.76.refs_1_, bf16[4,512,512]{2,1,0:T(8,128)(2,1)S(1)} %get-tuple-element.62.refs_5_.refs_3_.refs_2_, ...), custom_call_target="tpu_custom_call" | custom-call | tf_op jit(solution)/shard_map/pallas_call | solution.py:264
  66.0 1.1 %collective-permute-start.12 = (f32[2,256,256]{2,1,0:T(8,128)S(1)}, f32[2,256,256]{2,1,0:T(8,128)S(1)}, u32[]{:S(2)}, u32[]{:S(2)}) collective-permute-start(f32[2,256,256]{2,1,0:T(8,128)S(1)} %get-tuple-element.78), channel_id=1, source_target_pairs={{0,4},{1,5},{2,6},{3,7},{4,8},{5,9},{6,10},{7,11},{8,12},{9,13},{1... | collective-permute-start | bytes 1572872 | tf_op jit(solution)/shard_map/ppermute | solution.py:352
  67.1 0.7 shard_map.78
  67.8 1.3 %collective-permute-start.17 = (f32[2,256,256]{2,1,0:T(8,128)S(1)}, f32[2,256,256]{2,1,0:T(8,128)S(1)}, u32[]{:S(2)}, u32[]{:S(2)}) collective-permute-start(f32[2,256,256]{2,1,0:T(8,128)S(1)} %get-tuple-element.90), channel_id=1, source_target_pairs={{0,4},{1,5},{2,6},{3,7},{4,8},{5,9},{6,10},{7,11},{8,12},{9,13},{1... | collective-permute-start | bytes 1572872 | tf_op jit(solution)/shard_map/ppermute | solution.py:352
  69.1 0.9 collective-permute-done.14.came
  70.0 0.7 shard_map.77
  70.7 0.7 collective-permute-start.16
  71.3 0.4 collective-permute-done.13.came
  71.7 0.7 shard_map.76
  72.4 3.2 %collective-permute-done.12.came = f32[2,256,256]{2,1,0:T(8,128)S(1)} collective-permute-done((f32[2,256,256]{2,1,0:T(8,128)S(1)}, f32[2,256,256]{2,1,0:T(8,128)S(1)}, u32[]{:S(2)}, u32[]{:S(2)}) %collective-permute-start.12) | collective-permute-done | bytes 524320 | tf_op jit(solution)/shard_map/ppermute | solution.py:352
  75.6 0.7 shard_map.75
  76.3 4.6 %collective-permute-done.17.refs_5_ = f32[2,256,256]{2,1,0:T(8,128)S(1)} collective-permute-done((f32[2,256,256]{2,1,0:T(8,128)S(1)}, f32[2,256,256]{2,1,0:T(8,128)S(1)}, u32[]{:S(2)}, u32[]{:S(2)}) %collective-permute-start.17) | collective-permute-done | bytes 524320 | tf_op jit(solution)/shard_map/ppermute | solution.py:352
  80.9 0.7 shard_map.79
  81.7 0.1 collective-permute-start.18
  81.7 0.7 collective-permute-start.20
  82.4 8.6 %collective-permute-start.22 = (f32[2,256,256]{2,1,0:T(8,128)S(1)}, f32[2,256,256]{2,1,0:T(8,128)S(1)}, u32[]{:S(2)}, u32[]{:S(2)}) collective-permute-start(f32[2,256,256]{2,1,0:T(8,128)S(1)} %get-tuple-element.94), channel_id=1, source_target_pairs={{64,60},{65,61},{66,62},{67,63},{68,0},{69,1},{70,2},{71,3},{72,4}... | collective-permute-start | bytes 1572872 | tf_op jit(solution)/shard_map/ppermute | solution.py:352
  91.0 0.7 collective-permute-start.19
  91.7 1.3 %collective-permute-start.21 = (f32[2,256,256]{2,1,0:T(8,128)S(1)}, f32[2,256,256]{2,1,0:T(8,128)S(1)}, u32[]{:S(2)}, u32[]{:S(2)}) collective-permute-start(f32[2,256,256]{2,1,0:T(8,128)S(1)} %get-tuple-element.93), channel_id=1, source_target_pairs={{64,3},{65,0},{66,1},{67,2},{68,7},{69,4},{70,5},{71,6},{72,11},{7... | collective-permute-start | bytes 1572872 | tf_op jit(solution)/shard_map/ppermute | solution.py:352
  93.1 4.0 %collective-permute-done.22.refs_3_ = f32[2,256,256]{2,1,0:T(8,128)S(1)} collective-permute-done((f32[2,256,256]{2,1,0:T(8,128)S(1)}, f32[2,256,256]{2,1,0:T(8,128)S(1)}, u32[]{:S(2)}, u32[]{:S(2)}) %collective-permute-start.22) | collective-permute-done | bytes 524320 | tf_op jit(solution)/shard_map/ppermute | solution.py:352
  97.1 2.0 %collective-permute-done.21.refs_2_ = f32[2,256,256]{2,1,0:T(8,128)S(1)} collective-permute-done((f32[2,256,256]{2,1,0:T(8,128)S(1)}, f32[2,256,256]{2,1,0:T(8,128)S(1)}, u32[]{:S(2)}, u32[]{:S(2)}) %collective-permute-start.21) | collective-permute-done | bytes 524320 | tf_op jit(solution)/shard_map/ppermute | solution.py:352
  99.2 1.7 %shard_map.80 = f32[2,2,256,256]{3,2,1,0:T(8,128)} custom-call(s32[4]{0:T(128)S(1)} %get-tuple-element.101.spot, f32[2,2,256,256]{3,2,1,0:T(8,128)S(1)} %get-tuple-element.91.stay, f32[2,2,256,256]{3,2,1,0:T(8,128)S(1)} %collective-permute-done.18.back, f32[2,256,256]{2,1,0:T(8,128)S(1)} %collective-permute-done.19.refs_0_, ...), custom_call_target="tpu_custom_call" | custom-call | tf_op jit(solution)/shard_map/pallas_call | solution.py:264
  (25 shorter events, 0.1 us)
Async XLA Ops:
  0.0 3.9 %collective-permute-start.2 = (f32[2,2,256,256]{3,2,1,0:T(8,128)}, f32[2,2,256,256]{3,2,1,0:T(8,128)S(1)}, u32[]{:S(2)}, u32[]{:S(2)}) collective-permute-start(f32[2,2,256,256]{3,2,1,0:T(8,128)} %bitcast.14), channel_id=1, source_target_pairs={{0,64},{1,65},{2,66},{3,67},{4,68},{5,69},{6,70},{7,71},{8,72},{9,... | collective-permute-start | bytes 3145736 | tf_op jit(solution)/shard_map/ppermute | solution.py:352
  3.9 1.2 %copy-start = (f32[2,2,1,256,256]{4,3,2,1,0:T(8,128)S(1)}, f32[2,2,1,256,256]{4,3,2,1,0:T(8,128)}, u32[]{:S(2)}) copy-start(f32[2,2,1,256,256]{4,3,2,1,0:T(8,128)} %param.6) | copy-start | bytes 3145732
  5.9 22.8 %collective-permute-start.8 = (f32[2,256,256]{2,1,0:T(8,128)S(1)}, f32[2,256,256]{2,1,0:T(8,128)S(1)}, u32[]{:S(2)}, u32[]{:S(2)}) collective-permute-start(f32[2,256,256]{2,1,0:T(8,128)S(1)} %get-tuple-element.58.own), channel_id=1, source_target_pairs={{0,60},{1,61},{2,62},{3,63},{4,0},{5,1},{6,2},{7,3},{8,4},{9,5},{1... | collective-permute-start | bytes 1572872 | tf_op jit(solution)/shard_map/ppermute | solution.py:352
  7.3 22.8 %collective-permute-start.7 = (f32[2,256,256]{2,1,0:T(8,128)S(1)}, f32[2,256,256]{2,1,0:T(8,128)S(1)}, u32[]{:S(2)}, u32[]{:S(2)}) collective-permute-start(f32[2,256,256]{2,1,0:T(8,128)S(1)} %get-tuple-element.56.own), channel_id=1, source_target_pairs={{0,3},{1,0},{2,1},{3,2},{4,7},{5,4},{6,5},{7,6},{8,11},{9,8},{10,9... | collective-permute-start | bytes 1572872 | tf_op jit(solution)/shard_map/ppermute | solution.py:352
  8.6 23.1 %collective-permute-start.4 = (f32[2,256,256]{2,1,0:T(8,128)S(1)}, f32[2,256,256]{2,1,0:T(8,128)S(1)}, u32[]{:S(2)}, u32[]{:S(2)}) collective-permute-start(f32[2,256,256]{2,1,0:T(8,128)S(1)} %get-tuple-element.52.own), channel_id=1, source_target_pairs={{0,60},{1,61},{2,62},{3,63},{4,0},{5,1},{6,2},{7,3},{8,4},{9,5},{1... | collective-permute-start | bytes 1572872 | tf_op jit(solution)/shard_map/ppermute | solution.py:352
  9.9 24.5 %collective-permute-start.3 = (f32[2,256,256]{2,1,0:T(8,128)S(1)}, f32[2,256,256]{2,1,0:T(8,128)S(1)}, u32[]{:S(2)}, u32[]{:S(2)}) collective-permute-start(f32[2,256,256]{2,1,0:T(8,128)S(1)} %get-tuple-element.50.own), channel_id=1, source_target_pairs={{0,3},{1,0},{2,1},{3,2},{4,7},{5,4},{6,5},{7,6},{8,11},{9,8},{10,9... | collective-permute-start | bytes 1572872 | tf_op jit(solution)/shard_map/ppermute | solution.py:352
  11.1 11.2 %collective-permute-start = (s32[4]{0:T(128)S(1)}, s32[4]{0:T(128)S(1)}, u32[]{:S(2)}, u32[]{:S(2)}) collective-permute-start(s32[4]{0:T(128)S(1)} %pad_add_fusion.spot), channel_id=1, source_target_pairs={{0,1},{1,2},{2,3},{3,0},{4,5},{5,6},{6,7},{7,4},{8,9},{9,10},{10,1... | collective-permute-start | bytes 56 | tf_op jit(solution)/shard_map/ppermute | solution.py:352
  22.4 6.2 %collective-permute-start.1 = (s32[8]{0:T(128)S(1)}, s32[8]{0:T(128)S(1)}, u32[]{:S(2)}, u32[]{:S(2)}) collective-permute-start(s32[8]{0:T(128)S(1)} %pad_add_fusion.1), channel_id=1, source_target_pairs={{0,4},{1,5},{2,6},{3,7},{4,8},{5,9},{6,10},{7,11},{8,12},{9,13},{1... | collective-permute-start | bytes 104 | tf_op jit(solution)/shard_map/ppermute | solution.py:352
  28.7 8.0 %copy-start.4 = (f32[1,2,256,256]{3,2,1,0:T(8,128)S(1)}, f32[1,2,256,256]{3,2,1,0:T(8,128)}, u32[]{:S(2)}) copy-start(f32[1,2,256,256]{3,2,1,0:T(8,128)} %param.9) | copy-start | bytes 1572868
  30.2 14.1 %collective-permute-start.10 = (f32[2,256,256]{2,1,0:T(8,128)}, f32[2,256,256]{2,1,0:T(8,128)S(1)}, u32[]{:S(2)}, u32[]{:S(2)}) collective-permute-start(f32[2,256,256]{2,1,0:T(8,128)} %get-tuple-element.61), channel_id=1, source_target_pairs={{0,3},{1,0},{2,1},{3,2},{4,7},{5,4},{6,5},{7,6},{8,11},{9,8},{10,9... | collective-permute-start | bytes 1572872 | tf_op jit(solution)/shard_map/ppermute | solution.py:352
  30.2 10.0 %copy-start.5 = (f32[2,31]{1,0:T(2,128)S(1)}, f32[2,31]{1,0:T(2,128)}, u32[]{:S(2)}) copy-start(f32[2,31]{1,0:T(2,128)} %param.8) | copy-start | bytes 748
  31.7 12.6 %collective-permute-start.9 = (f32[2,256,256]{2,1,0:T(8,128)}, f32[2,256,256]{2,1,0:T(8,128)}, u32[]{:S(2)}, u32[]{:S(2)}) collective-permute-start(f32[2,256,256]{2,1,0:T(8,128)} %get-tuple-element.60), channel_id=1, source_target_pairs={{0,60},{1,61},{2,62},{3,63},{4,0},{5,1},{6,2},{7,3},{8,4},{9,5},{1... | collective-permute-start | bytes 1572872 | tf_op jit(solution)/shard_map/ppermute | solution.py:352
  33.2 11.1 %copy-start.1 = (f32[2,256,256]{2,1,0:T(8,128)S(1)}, f32[2,256,256]{2,1,0:T(8,128)}, u32[]{:S(2)}) copy-start(f32[2,256,256]{2,1,0:T(8,128)} %refs_4_.1) | copy-start | bytes 1572868
  33.2 14.6 %collective-permute-start.6 = (f32[2,256,256]{2,1,0:T(8,128)}, f32[2,256,256]{2,1,0:T(8,128)S(1)}, u32[]{:S(2)}, u32[]{:S(2)}) collective-permute-start(f32[2,256,256]{2,1,0:T(8,128)} %get-tuple-element.55), channel_id=1, source_target_pairs={{0,3},{1,0},{2,1},{3,2},{4,7},{5,4},{6,5},{7,6},{8,11},{9,8},{10,9... | collective-permute-start | bytes 1572872 | tf_op jit(solution)/shard_map/ppermute | solution.py:352
  35.8 0.8 copy-start.2
  36.7 15.1 %collective-permute-start.5 = (f32[2,256,256]{2,1,0:T(8,128)}, f32[2,256,256]{2,1,0:T(8,128)}, u32[]{:S(2)}, u32[]{:S(2)}) collective-permute-start(f32[2,256,256]{2,1,0:T(8,128)} %get-tuple-element.54), channel_id=1, source_target_pairs={{0,60},{1,61},{2,62},{3,63},{4,0},{5,1},{6,2},{7,3},{8,4},{9,5},{1... | collective-permute-start | bytes 1572872 | tf_op jit(solution)/shard_map/ppermute | solution.py:352
  37.4 17.6 %collective-permute-start.11 = (f32[256,256]{1,0:T(8,128)}, f32[256,256]{1,0:T(8,128)}, u32[]{:S(2)}, u32[]{:S(2)}) collective-permute-start(f32[256,256]{1,0:T(8,128)} %get-tuple-element.95), channel_id=1, source_target_pairs={{64,69},{65,70},{66,71},{67,68},{68,73},{69,74},{70,75},{71,72},{7... | collective-permute-start | bytes 786440 | tf_op jit(solution)/shard_map/ppermute | solution.py:352
  44.3 7.5 %copy-start.3 = (f32[2,256,256]{2,1,0:T(8,128)S(1)}, f32[2,256,256]{2,1,0:T(8,128)}, u32[]{:S(2)}) copy-start(f32[2,256,256]{2,1,0:T(8,128)} %copy-done.2) | copy-start | bytes 1572868
  57.2 9.9 %collective-permute-start.15 = (f32[2,256,256]{2,1,0:T(8,128)S(1)}, f32[2,256,256]{2,1,0:T(8,128)S(1)}, u32[]{:S(2)}, u32[]{:S(2)}) collective-permute-start(f32[2,256,256]{2,1,0:T(8,128)S(1)} %get-tuple-element.87), channel_id=1, source_target_pairs={{0,1},{1,2},{2,3},{3,0},{4,5},{5,6},{6,7},{7,4},{8,9},{9,10},{10,1... | collective-permute-start | bytes 1572872 | tf_op jit(solution)/shard_map/ppermute | solution.py:352
  61.6 8.4 %collective-permute-start.14 = (f32[2,256,256]{2,1,0:T(8,128)S(1)}, f32[2,256,256]{2,1,0:T(8,128)S(1)}, u32[]{:S(2)}, u32[]{:S(2)}) collective-permute-start(f32[2,256,256]{2,1,0:T(8,128)S(1)} %get-tuple-element.84), channel_id=1, source_target_pairs={{0,4},{1,5},{2,6},{3,7},{4,8},{5,9},{6,10},{7,11},{8,12},{9,13},{1... | collective-permute-start | bytes 1572872 | tf_op jit(solution)/shard_map/ppermute | solution.py:352
  63.3 8.4 %collective-permute-start.13 = (f32[2,256,256]{2,1,0:T(8,128)S(1)}, f32[2,256,256]{2,1,0:T(8,128)S(1)}, u32[]{:S(2)}, u32[]{:S(2)}) collective-permute-start(f32[2,256,256]{2,1,0:T(8,128)S(1)} %get-tuple-element.81), channel_id=1, source_target_pairs={{0,1},{1,2},{2,3},{3,0},{4,5},{5,6},{6,7},{7,4},{8,9},{9,10},{10,1... | collective-permute-start | bytes 1572872 | tf_op jit(solution)/shard_map/ppermute | solution.py:352
  66.0 9.6 %collective-permute-start.12 = (f32[2,256,256]{2,1,0:T(8,128)S(1)}, f32[2,256,256]{2,1,0:T(8,128)S(1)}, u32[]{:S(2)}, u32[]{:S(2)}) collective-permute-start(f32[2,256,256]{2,1,0:T(8,128)S(1)} %get-tuple-element.78), channel_id=1, source_target_pairs={{0,4},{1,5},{2,6},{3,7},{4,8},{5,9},{6,10},{7,11},{8,12},{9,13},{1... | collective-permute-start | bytes 1572872 | tf_op jit(solution)/shard_map/ppermute | solution.py:352
  67.8 13.1 %collective-permute-start.17 = (f32[2,256,256]{2,1,0:T(8,128)S(1)}, f32[2,256,256]{2,1,0:T(8,128)S(1)}, u32[]{:S(2)}, u32[]{:S(2)}) collective-permute-start(f32[2,256,256]{2,1,0:T(8,128)S(1)} %get-tuple-element.90), channel_id=1, source_target_pairs={{0,4},{1,5},{2,6},{3,7},{4,8},{5,9},{6,10},{7,11},{8,12},{9,13},{1... | collective-permute-start | bytes 1572872 | tf_op jit(solution)/shard_map/ppermute | solution.py:352
  70.7 10.2 %collective-permute-start.16 = (f32[2,256,256]{2,1,0:T(8,128)S(1)}, f32[2,256,256]{2,1,0:T(8,128)S(1)}, u32[]{:S(2)}, u32[]{:S(2)}) collective-permute-start(f32[2,256,256]{2,1,0:T(8,128)S(1)} %get-tuple-element.89), channel_id=1, source_target_pairs={{0,1},{1,2},{2,3},{3,0},{4,5},{5,6},{6,7},{7,4},{8,9},{9,10},{10,1... | collective-permute-start | bytes 1572872 | tf_op jit(solution)/shard_map/ppermute | solution.py:352
  81.7 17.5 %collective-permute-start.18 = (f32[2,2,256,256]{3,2,1,0:T(8,128)S(1)}, f32[2,2,256,256]{3,2,1,0:T(8,128)S(1)}, u32[]{:S(2)}, u32[]{:S(2)}) collective-permute-start(f32[2,2,256,256]{3,2,1,0:T(8,128)S(1)} %get-tuple-element.92), channel_id=1, source_target_pairs={{0,64},{1,65},{2,66},{3,67},{4,68},{5,69},{6,70},{7,71},{8,72},{9,... | collective-permute-start | bytes 3145736 | tf_op jit(solution)/shard_map/ppermute | solution.py:352
  81.7 11.3 %collective-permute-start.20 = (f32[2,256,256]{2,1,0:T(8,128)S(1)}, f32[2,256,256]{2,1,0:T(8,128)S(1)}, u32[]{:S(2)}, u32[]{:S(2)}) collective-permute-start(f32[2,256,256]{2,1,0:T(8,128)S(1)} %get-tuple-element.94), channel_id=1, source_target_pairs={{0,4},{1,5},{2,6},{3,7},{4,8},{5,9},{6,10},{7,11},{8,12},{9,13},{1... | collective-permute-start | bytes 1572872 | tf_op jit(solution)/shard_map/ppermute | solution.py:352
  82.4 14.7 %collective-permute-start.22 = (f32[2,256,256]{2,1,0:T(8,128)S(1)}, f32[2,256,256]{2,1,0:T(8,128)S(1)}, u32[]{:S(2)}, u32[]{:S(2)}) collective-permute-start(f32[2,256,256]{2,1,0:T(8,128)S(1)} %get-tuple-element.94), channel_id=1, source_target_pairs={{64,60},{65,61},{66,62},{67,63},{68,0},{69,1},{70,2},{71,3},{72,4}... | collective-permute-start | bytes 1572872 | tf_op jit(solution)/shard_map/ppermute | solution.py:352
  91.0 6.1 %collective-permute-start.19 = (f32[2,256,256]{2,1,0:T(8,128)S(1)}, f32[2,256,256]{2,1,0:T(8,128)S(1)}, u32[]{:S(2)}, u32[]{:S(2)}) collective-permute-start(f32[2,256,256]{2,1,0:T(8,128)S(1)} %get-tuple-element.93), channel_id=1, source_target_pairs={{0,1},{1,2},{2,3},{3,0},{4,5},{5,6},{6,7},{7,4},{8,9},{9,10},{10,1... | collective-permute-start | bytes 1572872 | tf_op jit(solution)/shard_map/ppermute | solution.py:352
  91.7 7.4 %collective-permute-start.21 = (f32[2,256,256]{2,1,0:T(8,128)S(1)}, f32[2,256,256]{2,1,0:T(8,128)S(1)}, u32[]{:S(2)}, u32[]{:S(2)}) collective-permute-start(f32[2,256,256]{2,1,0:T(8,128)S(1)} %get-tuple-element.93), channel_id=1, source_target_pairs={{64,3},{65,0},{66,1},{67,2},{68,7},{69,4},{70,5},{71,6},{72,11},{7... | collective-permute-start | bytes 1572872 | tf_op jit(solution)/shard_map/ppermute | solution.py:352

commit v2 on v1

--- a/solution.py
+++ b/solution.py
@@ -274,56 +274,64 @@
 def blend_kernel(by_rows, spots, own, near, mixed, inner):
     here = [spots[i] for i in range(3)]
     there = [spots[4 + i] for i in range(3)]
+    here_cols, there_cols = own_cols(here), own_cols(there)
     for sl, _, r0 in chunks():
-        for spot, out in ((there, mixed), (here, inner)):
-            mask = own_rows(spot, r0) if by_rows else own_cols(spot)
-            for c in range(2):
-                out[c, sl] = jnp.where(mask, own[c, sl], near[c, sl])
-
-
-def turn_kernel(p, spots, grad, came, sent, kept):
+        here_mask = own_rows(here, r0) if by_rows else here_cols
+        there_mask = own_rows(there, r0) if by_rows else there_cols
+        for c in range(2):
+            u, v = own[c, sl], near[c, sl]
+            mixed[c, sl] = jnp.where(there_mask, u, v)
+            inner[c, sl] = jnp.where(here_mask, u, v)
+
+
+def turn_kernel(parity, spots, *refs):
+    grads, came, outs = refs[0:2], refs[2:4], refs[4:8]
     here = [spots[i] for i in range(3)]
     there = [spots[4 + i] for i in range(3)]
     cols, there_cols = own_cols(here), own_cols(there)
+    upper = spots[2] == 1
     for sl, _, r0 in chunks():
         rows = own_rows(here, r0)
-        if p % 2 == 0:
+        if parity == 0:
             first, second, mask = rows, cols, there_cols
         else:
             first, second, mask = cols, rows, own_rows(there, r0)
         for c in range(2):
-            g = jnp.where(first, grad[c, sl], 0.0)
-            v = came[c, sl]
-            sent[c, sl] = jnp.where(second, 0.0, g) + jnp.where(mask, 0.0, v)
-            kept[c, sl] = jnp.where(second, g, 0.0) + jnp.where(mask, v, 0.0)
-
-
-def merge_kernel(spot, *refs):
-    kept, went, stay, leaving = refs[0:4], refs[4:6], refs[6], refs[7]
-    upper = spot[2] == 1
+            sent, kept = [], []
+            for grad, block in zip(grads, came):
+                g = jnp.where(first, grad[c, sl], 0.0)
+                v = block[c, sl]
+                sent.append(jnp.where(second, 0.0, g) + jnp.where(mask, 0.0, v))
+                kept.append(jnp.where(second, g, 0.0) + jnp.where(mask, v, 0.0))
+            outs[0][c, sl] = jnp.where(upper, sent[1], sent[0])
+            outs[1][c, sl] = jnp.where(upper, sent[0], sent[1])
+            outs[2][c, sl] = jnp.where(upper, kept[1], kept[0])
+            outs[3][c, sl] = jnp.where(upper, kept[0], kept[1])
+
+
+def final_kernel(spot, *refs):
+    out = refs[8]
     for q in range(2):
         for c in range(2):
             for sl, _, _ in chunks():
-                low = kept[q][c, sl]
-                high = kept[q + 2][c, sl] + went[q][c, sl]
-                stay[q, c, sl] = jnp.where(upper, high, low)
-                leaving[q, c, sl] = jnp.where(upper, low, high)
-
-
-def final_kernel(spot, stay, back, *refs):
-    out = refs[4]
-    for q in range(2):
+                a, b, x, y = (refs[4 * q + i][c, sl] for i in range(4))
+                out[q, c, sl] = (a + b) + (x + y)
+
+
+def load_kernel(spot, mine, *outs):
+    for k in range(2):
         for c in range(2):
             for sl, _, _ in chunks():
-                out[q, c, sl] = (stay[q, c, sl] + back[q, c, sl]) + (refs[q][c, sl] + refs[q + 2][c, sl])
-
-
-def order_kernel(spot, mine, other, *outs):
+                outs[k][c, sl] = mine[k, c, sl]
+
+
+def order_kernel(spot, *refs):
+    mine, other, outs = refs[0:2], refs[2], refs[3:7]
     upper = spot[2] == 1
     for k in range(4):
         for c in range(2):
             for sl, _, _ in chunks():
-                a, b = mine[k % 2, c, sl], other[k % 2, c, sl]
+                a, b = mine[k % 2][c, sl], other[k % 2, c, sl]
                 outs[k][c, sl] = jnp.where(upper, b, a) if k < 2 else jnp.where(upper, a, b)
 
 
@@ -342,8 +350,7 @@
 GATHER = (pairs_of((-1, 0), (1, 0)), pairs_of((0, -1), (0, 1)))
 SCATTER = (pairs_of((1, 0), (-1, 0)), pairs_of((0, 1), (0, -1)))
 INFO = (pairs_of((1, 0), (1, 0)), pairs_of((0, 1), (0, 1)))
-STRAIGHT = [[(a, b) for a, b in way if a < TILES] for way in SCATTER]
-CROSSED = [[(a, b - TILES) for a, b in way if a >= TILES] for way in SCATTER]
+CROSSED = [[(a, (b + TILES) % (2 * TILES)) for a, b in way] for way in SCATTER]
 DIAGONAL = pairs_of(None, (1, 1))
 SWAP = [(d * TILES + t, (1 - d) * TILES + t) for d in range(2) for t in range(TILES)]
 
@@ -366,13 +373,14 @@
     other = permute(mine, SWAP)
     alive = (core < counts[0]).astype(jnp.int32)
     info = jnp.concatenate([jnp.where(core == 0, offsets[0, 0], offsets[0, 1]), core[None], alive[None]])
+    loaded = call(load_kernel, [FIELD] * 2, info, [mine])
     left = permute(info, INFO[0])
-    above = permute(jnp.concatenate([info, left]), INFO[1])
-    up, upleft = above[:4], above[4:]
+    up = permute(info, INFO[1])
+    upleft = permute(info, DIAGONAL)
     here = jnp.where(core == 0, info, upleft)
     at_y = jnp.where(core == 0, up, left)
     at_x = jnp.where(core == 0, left, up)
-    own = call(order_kernel, [FIELD] * 4, info, [mine, other])
+    own = call(order_kernel, [FIELD] * 4, info, [*loaded, other])
 
     near = [permute(own[p], GATHER[p % 2]) for p in range(4)]
     shared = permute(intensity[0, 1], DIAGONAL)
@@ -402,18 +410,13 @@
         grads[p] = outs[0]
         came[p] = permute(outs[1], SCATTER[1 - p % 2])
         state = outs[2] if onward else None
-    kept, went = [None] * 4, [None] * 4
-    for p in (3, 2, 1, 0):
-        sent, kept[p] = call(functools.partial(turn_kernel, p), [FIELD] * 2, both[p % 2], [grads[p], came[p]])
-        if p > 1:
-            went[p] = permute(sent, SCATTER[p % 2])
-        else:
-            went[p] = [permute(sent, way[p % 2]) for way in (STRAIGHT, CROSSED)]
-    pair = jax.ShapeDtypeStruct((2, 2, N, N), F32)
-    stay, leaving = call(merge_kernel, [pair] * 2, here, [*kept, went[2], went[3]])
-    back = permute(leaving, SWAP)
-    last = [went[0][0], went[1][0], went[0][1], went[1][1]]
-    out, = call(final_kernel, [pair], here, [stay, back, *last])
+    parts = [None, None]
+    for q in (1, 0):
+        straight, cross, stay, leaving = call(
+            functools.partial(turn_kernel, q), [FIELD] * 4, both[q], [grads[q], grads[q + 2], came[q], came[q + 2]]
+        )
+        parts[q] = [stay, permute(leaving, SWAP), permute(straight, SCATTER[q]), permute(cross, CROSSED[q])]
+    out, = call(final_kernel, [jax.ShapeDtypeStruct((2, 2, N, N), F32)], here, parts[0] + parts[1])
     return out[:, :, None]
 
 

time: 101 us -> 99.2 us (0.982)
  waiting for transfers between devices: 35.3 us -> 30.6 us
  starting transfers between devices: 31.1 us -> 35.2 us
  Pallas kernels: 28.3 us -> 27.1 us
    ppermute x23, waiting for transfers between devices: 35.3 us -> 30.6 us  [permute(): return lax.ppermute(block, ('depth', 'tiles'), pairs)]
    ppermute x23, starting transfers between devices: 31.1 us -> 35.2 us  [permute(): return lax.ppermute(block, ('depth', 'tiles'), pairs)]
    pallas_call x17 -> x15, Pallas kernels: 25.6 us -> 24.4 us  [call(): pl.pallas_call(kernel, out_shape=outs, in_specs=[SS] + [VS] * len(args),...]
  transfers between devices with their start and end apart: 23 -> 23, of which waited for: 10 -> 5; matrix products, arithmetic and copies ran while one was open for 3% -> 3% of each run, Pallas kernels for 23% -> 20%
where the time goes in v2:
time: 99.2 us; the launch traced here: 98.9 us
  starting transfers between devices  35.2 us (35%)
  waiting for transfers between devices  30.6 us (31%)
  Pallas kernels  27.1 us (27%)
  local copies, waits for them, and re-layouts  2.95 us (3%)
  other arithmetic  2.18 us (2%)
    ppermute x23, starting transfers between devices, permute(): return lax.ppermute(block, ('depth', 'tiles'), pairs)  35.2 us
    ppermute x23, waiting for transfers between devices, permute(): return lax.ppermute(block, ('depth', 'tiles'), pairs)  30.6 us
    pallas_call x15, Pallas kernels, call(): pl.pallas_call(kernel, out_shape=outs, in_specs=[SS] + [VS] * len(args),...  24.4 us
    pallas_call x1, Pallas kernels, tables(): pl.pallas_call(tables_kernel, out_shape=[jax.ShapeDtypeStruct((4, 2 * N,...  2.74 us
    unnamed x12, local copies, waits for them, and re-layouts  2.04 us
  transfers between devices with their start and end apart: 23, of which 5 were waited for; matrix products, arithmetic and copies ran while one was open for 3% of the time, Pallas kernels for 20%

profile of v2, /device:TPU:1, one launch (start us, length us, event | category | flops | bytes accessed | tf_op | source)
XLA Modules:
  0.0 98.9 jit_solution(8847796698012076407)
XLA Ops:
  0.0 1.4 %collective-permute-start.3 = (f32[2,2,256,256]{3,2,1,0:T(8,128)}, f32[2,2,256,256]{3,2,1,0:T(8,128)S(1)}, u32[]{:S(2)}, u32[]{:S(2)}) collective-permute-start(f32[2,2,256,256]{3,2,1,0:T(8,128)} %bitcast.14), channel_id=1, source_target_pairs={{0,64},{1,65},{2,66},{3,67},{4,68},{5,69},{6,70},{7,71},{8,72},{9,... | collective-permute-start | bytes 3145736 | tf_op jit(solution)/shard_map/ppermute | solution.py:359
  2.0 0.8 fusion.6
  2.8 0.1 pad_add_fusion.spot
  2.9 4.2 %collective-permute-start = (s32[4]{0:T(128)S(1)}, s32[4]{0:T(128)S(1)}, u32[]{:S(2)}, u32[]{:S(2)}) collective-permute-start(s32[4]{0:T(128)S(1)} %pad_add_fusion.spot), channel_id=1, source_target_pairs={{64,69},{65,70},{66,71},{67,68},{68,73},{69,74},{70,75},{71,72},{7... | collective-permute-start | bytes 56 | tf_op jit(solution)/shard_map/ppermute | solution.py:359
  7.1 1.4 %collective-permute-start.1 = (s32[4]{0:T(128)S(1)}, s32[4]{0:T(128)S(1)}, u32[]{:S(2)}, u32[]{:S(2)}) collective-permute-start(s32[4]{0:T(128)S(1)} %pad_add_fusion.spot), channel_id=1, source_target_pairs={{0,4},{1,5},{2,6},{3,7},{4,8},{5,9},{6,10},{7,11},{8,12},{9,13},{1... | collective-permute-start | bytes 56 | tf_op jit(solution)/shard_map/ppermute | solution.py:359
  8.5 1.2 %copy-done = f32[2,2,1,256,256]{4,3,2,1,0:T(8,128)S(1)} copy-done((f32[2,2,1,256,256]{4,3,2,1,0:T(8,128)S(1)}, f32[2,2,1,256,256]{4,3,2,1,0:T(8,128)}, u32[]{:S(2)}) %copy-start) | copy-done | bytes 1048600
  9.7 0.6 shard_map.64
  10.3 0.0 collective-permute-done.3.refs_2_
  10.3 0.8 shard_map.65
  11.1 1.1 %collective-permute-start.9 = (f32[2,256,256]{2,1,0:T(8,128)S(1)}, f32[2,256,256]{2,1,0:T(8,128)S(1)}, u32[]{:S(2)}, u32[]{:S(2)}) collective-permute-start(f32[2,256,256]{2,1,0:T(8,128)S(1)} %get-tuple-element.60.own), channel_id=1, source_target_pairs={{0,60},{1,61},{2,62},{3,63},{4,0},{5,1},{6,2},{7,3},{8,4},{9,5},{1... | collective-permute-start | bytes 1572872 | tf_op jit(solution)/shard_map/ppermute | solution.py:359
  12.2 1.2 %collective-permute-start.8 = (f32[2,256,256]{2,1,0:T(8,128)S(1)}, f32[2,256,256]{2,1,0:T(8,128)S(1)}, u32[]{:S(2)}, u32[]{:S(2)}) collective-permute-start(f32[2,256,256]{2,1,0:T(8,128)S(1)} %get-tuple-element.58.own), channel_id=1, source_target_pairs={{0,3},{1,0},{2,1},{3,2},{4,7},{5,4},{6,5},{7,6},{8,11},{9,8},{10,9... | collective-permute-start | bytes 1572872 | tf_op jit(solution)/shard_map/ppermute | solution.py:359
  13.4 1.3 %collective-permute-start.5 = (f32[2,256,256]{2,1,0:T(8,128)S(1)}, f32[2,256,256]{2,1,0:T(8,128)S(1)}, u32[]{:S(2)}, u32[]{:S(2)}) collective-permute-start(f32[2,256,256]{2,1,0:T(8,128)S(1)} %get-tuple-element.54.own), channel_id=1, source_target_pairs={{0,60},{1,61},{2,62},{3,63},{4,0},{5,1},{6,2},{7,3},{8,4},{9,5},{1... | collective-permute-start | bytes 1572872 | tf_op jit(solution)/shard_map/ppermute | solution.py:359
  14.7 0.9 collective-permute-start.4
  15.6 0.1 broadcast_select_fusion.3.spot
  15.7 0.0 collective-permute-done.1
  15.7 0.2 collective-permute-start.2
  15.9 11.2 %collective-permute-done.2 = s32[4]{0:T(128)S(1)} collective-permute-done((s32[4]{0:T(128)S(1)}, s32[4]{0:T(128)S(1)}, u32[]{:S(2)}, u32[]{:S(2)}) %collective-permute-start.2) | collective-permute-done | bytes 48 | tf_op jit(solution)/shard_map/ppermute | solution.py:359
  27.1 0.1 pad_add_fusion.2
  27.2 1.4 %shard_map.69 = (f32[2,256,256]{2,1,0:T(8,128)}, f32[2,256,256]{2,1,0:T(8,128)S(1)}) custom-call(s32[8]{0:T(128)S(1)} %get-tuple-element.99.spots, f32[2,256,256]{2,1,0:T(8,128)S(1)} %get-tuple-element.60.own, f32[2,256,256]{2,1,0:T(8,128)S(1)} %collective-permute-done.9.near), custom_call_target="tpu_custom_call" | custom-call | tf_op jit(solution)/shard_map/pallas_call | solution.py:264
  28.7 0.2 collective-permute-start.11
  28.9 0.0 collective-permute-done.8.near
  28.9 1.5 %shard_map.68 = (f32[2,256,256]{2,1,0:T(8,128)}, f32[2,256,256]{2,1,0:T(8,128)S(1)}) custom-call(s32[8]{0:T(128)S(1)} %get-tuple-element.100.spots, f32[2,256,256]{2,1,0:T(8,128)S(1)} %get-tuple-element.58.own, f32[2,256,256]{2,1,0:T(8,128)S(1)} %collective-permute-done.8.near), custom_call_target="tpu_custom_call" | custom-call | tf_op jit(solution)/shard_map/pallas_call | solution.py:264
  30.4 1.3 %collective-permute-start.10 = (f32[2,256,256]{2,1,0:T(8,128)}, f32[2,256,256]{2,1,0:T(8,128)}, u32[]{:S(2)}, u32[]{:S(2)}) collective-permute-start(f32[2,256,256]{2,1,0:T(8,128)} %get-tuple-element.62), channel_id=1, source_target_pairs={{0,60},{1,61},{2,62},{3,63},{4,0},{5,1},{6,2},{7,3},{8,4},{9,5},{1... | collective-permute-start | bytes 1572872 | tf_op jit(solution)/shard_map/ppermute | solution.py:359
  31.7 0.0 collective-permute-done.5.near
  31.7 1.5 %shard_map.67 = (f32[2,256,256]{2,1,0:T(8,128)}, f32[2,256,256]{2,1,0:T(8,128)S(1)}) custom-call(s32[8]{0:T(128)S(1)} %get-tuple-element.99.spots, f32[2,256,256]{2,1,0:T(8,128)S(1)} %get-tuple-element.54.own, f32[2,256,256]{2,1,0:T(8,128)S(1)} %collective-permute-done.5.near), custom_call_target="tpu_custom_call" | custom-call | tf_op jit(solution)/shard_map/pallas_call | solution.py:264
  33.1 0.9 collective-permute-start.7
  34.0 0.0 collective-permute-done.4.near
  34.1 1.4 %shard_map.66 = (f32[2,256,256]{2,1,0:T(8,128)}, f32[2,256,256]{2,1,0:T(8,128)S(1)}) custom-call(s32[8]{0:T(128)S(1)} %get-tuple-element.100.spots, f32[2,256,256]{2,1,0:T(8,128)S(1)} %get-tuple-element.52.own, f32[2,256,256]{2,1,0:T(8,128)S(1)} %collective-permute-done.4.near), custom_call_target="tpu_custom_call" | custom-call | tf_op jit(solution)/shard_map/pallas_call | solution.py:264
  35.5 0.8 copy-done.2
  36.3 1.4 %collective-permute-start.6 = (f32[2,256,256]{2,1,0:T(8,128)}, f32[2,256,256]{2,1,0:T(8,128)}, u32[]{:S(2)}, u32[]{:S(2)}) collective-permute-start(f32[2,256,256]{2,1,0:T(8,128)} %get-tuple-element.56), channel_id=1, source_target_pairs={{0,60},{1,61},{2,62},{3,63},{4,0},{5,1},{6,2},{7,3},{8,4},{9,5},{1... | collective-permute-start | bytes 1572872 | tf_op jit(solution)/shard_map/ppermute | solution.py:359
  37.7 0.7 slice_bitcast_fusion
  38.4 3.2 %collective-permute-start.12 = (f32[256,256]{1,0:T(8,128)}, f32[256,256]{1,0:T(8,128)}, u32[]{:S(2)}, u32[]{:S(2)}) collective-permute-start(f32[256,256]{1,0:T(8,128)} %get-tuple-element.95), channel_id=1, source_target_pairs={{64,69},{65,70},{66,71},{67,68},{68,73},{69,74},{70,75},{71,72},{7... | collective-permute-start | bytes 786440 | tf_op jit(solution)/shard_map/ppermute | solution.py:359
  41.6 0.1 rev.3
  41.7 0.1 slice.26
  41.8 0.1 pad_maximum_fusion.1.taps
  41.9 1.1 %negate_multiply_fusion = (f32[1,256,256]{2,1,0:T(8,128)S(1)}, f32[1,256,256]{2,1,0:T(8,128)S(1)}) fusion(), kind=kLoop, calls=%fused_computation.9 | loop fusion | flops 1114112 | bytes 524288 | tf_op jit(solution)/shard_map/mul | solution.py:367
  43.0 2.7 %tables.1 = (bf16[4,512,512]{2,1,0:T(8,128)(2,1)S(1)}, bf16[4,512,512]{2,1,0:T(8,128)(2,1)S(1)}, bf16[4,512,256]{2,1,0:T(8,128)(2,1)S(1)}, bf16[4,512,256]{2,1,0:T(8,128)(2,1)S(1)}) custom-call(s32[4]{0:T(128)S(1)} %broadcast_select_fusion.3.spot, f32[8,256]{1,0:T(8,128)S(1)} %pad_maximum_fusion.1.taps, f32[2,256,256]{2,1,0:T(8,128)S(1)} %pad_maximum_fusion.dft), custom_call_target="tpu_custom_call" | custom-call | tf_op jit(solution)/shard_map/tables/pallas_call | solution.py:94
  45.8 3.5 %shard_map.70 = (f32[2,256,256]{2,1,0:T(8,128)}, f32[2,256,256]{2,1,0:T(8,128)S(1)}, f32[2,256,256]{2,1,0:T(8,128)S(1)}, f32[2,256,256]{2,1,0:T(8,128)S(1)}, f32[2,256,256]{2,1,0:T(8,128)S(1)}) custom-call(s32[4]{0:T(128)S(1)} %broadcast_select_fusion.3.spot, f32[2,256,256]{2,1,0:T(8,128)S(1)} %get-tuple-element.59.refs_0_, ...), custom_call_target="tpu_custom_call" | custom-call | tf_op jit(solution)/shard_map/pallas_call | solution.py:264
  49.3 0.0 collective-permute-done.7.refs_3_
  49.3 3.2 %shard_map.71 = (f32[2,256,256]{2,1,0:T(8,128)S(1)}, f32[2,256,256]{2,1,0:T(8,128)S(1)}, f32[2,256,256]{2,1,0:T(8,128)S(1)}, f32[2,256,256]{2,1,0:T(8,128)S(1)}) custom-call(s32[4]{0:T(128)S(1)} %broadcast_select_fusion.3.spot, f32[2,256,256]{2,1,0:T(8,128)S(1)} %copy-done.3, f32[2,256,256]{2,1,0:T(8,128)S(1)} %get-tuple-element.55.refs_1_, ...), custom_call_target="tpu_custom_call" | custom-call | tf_op jit(solution)/shard_map/pallas_call | solution.py:264
  52.5 0.0 collective-permute-done.12.refs_2_
  52.5 2.2 %shard_map.72 = (f32[2,256,256]{2,1,0:T(8,128)S(1)}, f32[2,256,256]{2,1,0:T(8,128)S(1)}, bf16[2,512,256]{2,1,0:T(8,128)(2,1)S(1)}) custom-call(s32[4]{0:T(128)S(1)} %broadcast_select_fusion.3.spot, f32[2,256,256]{2,1,0:T(8,128)S(1)} %get-tuple-element.69.refs_0_, f32[256,256]{1,0:T(8,128)S(1)} %get-tuple-element.96.refs_1_, ...), custom_call_target="tpu_custom_call" | custom-call | tf_op jit(solution)/shard_map/pallas_call | solution.py:264
  54.7 1.6 %shard_map.73 = (f32[2,256,256]{2,1,0:T(8,128)S(1)}, f32[2,256,256]{2,1,0:T(8,128)S(1)}, bf16[2,512,256]{2,1,0:T(8,128)(2,1)S(1)}) custom-call(s32[4]{0:T(128)S(1)} %broadcast_select_fusion.3.spot, bf16[2,512,256]{2,1,0:T(8,128)(2,1)S(1)} %get-tuple-element.72.refs_0_, f32[2,256,256]{2,1,0:T(8,128)S(1)} %get-tuple-element.68.refs_4_.refs_1_, ...), custom_call_target="tpu_custom_call" | custom-call | tf_op jit(solution)/shard_map/pallas_call | solution.py:264
  56.4 1.6 %shard_map.74 = (f32[2,256,256]{2,1,0:T(8,128)S(1)}, f32[2,256,256]{2,1,0:T(8,128)S(1)}, bf16[2,512,256]{2,1,0:T(8,128)(2,1)S(1)}) custom-call(s32[4]{0:T(128)S(1)} %broadcast_select_fusion.3.spot, bf16[2,512,256]{2,1,0:T(8,128)(2,1)S(1)} %get-tuple-element.74.refs_0_, f32[2,256,256]{2,1,0:T(8,128)S(1)} %get-tuple-element.75.refs_1_, ...), custom_call_target="tpu_custom_call" | custom-call | tf_op jit(solution)/shard_map/pallas_call | solution.py:264
  58.0 3.7 %collective-permute-start.18 = (f32[2,256,256]{2,1,0:T(8,128)S(1)}, f32[2,256,256]{2,1,0:T(8,128)S(1)}, u32[]{:S(2)}, u32[]{:S(2)}) collective-permute-start(f32[2,256,256]{2,1,0:T(8,128)S(1)} %get-tuple-element.89), channel_id=1, source_target_pairs={{0,1},{1,2},{2,3},{3,0},{4,5},{5,6},{6,7},{7,4},{8,9},{9,10},{10,1... | collective-permute-start | bytes 1572872 | tf_op jit(solution)/shard_map/ppermute | solution.py:359
  61.7 0.8 collective-permute-start.19
  62.5 1.6 %shard_map.75 = (f32[2,256,256]{2,1,0:T(8,128)S(1)}, f32[2,256,256]{2,1,0:T(8,128)S(1)}) custom-call(s32[4]{0:T(128)S(1)} %broadcast_select_fusion.3.spot, bf16[2,512,256]{2,1,0:T(8,128)(2,1)S(1)} %get-tuple-element.77.refs_0_, f32[2,256,256]{2,1,0:T(8,128)S(1)} %get-tuple-element.78.refs_1_, ...), custom_call_target="tpu_custom_call" | custom-call | tf_op jit(solution)/shard_map/pallas_call | solution.py:264
  64.1 2.2 %collective-permute-start.13 = (f32[2,256,256]{2,1,0:T(8,128)S(1)}, f32[2,256,256]{2,1,0:T(8,128)S(1)}, u32[]{:S(2)}, u32[]{:S(2)}) collective-permute-start(f32[2,256,256]{2,1,0:T(8,128)S(1)} %get-tuple-element.81), channel_id=1, source_target_pairs={{0,4},{1,5},{2,6},{3,7},{4,8},{5,9},{6,10},{7,11},{8,12},{9,13},{1... | collective-permute-start | bytes 1572872 | tf_op jit(solution)/shard_map/ppermute | solution.py:359
  66.3 0.3 collective-permute-start.14
  66.6 1.2 %collective-permute-done.18.refs_2_ = f32[2,256,256]{2,1,0:T(8,128)S(1)} collective-permute-done((f32[2,256,256]{2,1,0:T(8,128)S(1)}, f32[2,256,256]{2,1,0:T(8,128)S(1)}, u32[]{:S(2)}, u32[]{:S(2)}) %collective-permute-start.18) | collective-permute-done | bytes 524320 | tf_op jit(solution)/shard_map/ppermute | solution.py:359
  67.8 5.6 %collective-permute-done.19.refs_3_ = f32[2,256,256]{2,1,0:T(8,128)S(1)} collective-permute-done((f32[2,256,256]{2,1,0:T(8,128)S(1)}, f32[2,256,256]{2,1,0:T(8,128)S(1)}, u32[]{:S(2)}, u32[]{:S(2)}) %collective-permute-start.19) | collective-permute-done | bytes 524320 | tf_op jit(solution)/shard_map/ppermute | solution.py:359
  73.5 0.9 shard_map.77
  74.4 0.1 collective-permute-start.20
  74.5 2.6 %collective-permute-start.21 = (f32[2,256,256]{2,1,0:T(8,128)S(1)}, f32[2,256,256]{2,1,0:T(8,128)S(1)}, u32[]{:S(2)}, u32[]{:S(2)}) collective-permute-start(f32[2,256,256]{2,1,0:T(8,128)S(1)} %get-tuple-element.93), channel_id=1, source_target_pairs={{0,4},{1,5},{2,6},{3,7},{4,8},{5,9},{6,10},{7,11},{8,12},{9,13},{1... | collective-permute-start | bytes 1572872 | tf_op jit(solution)/shard_map/ppermute | solution.py:359
  77.0 2.9 %collective-permute-start.22 = (f32[2,256,256]{2,1,0:T(8,128)S(1)}, f32[2,256,256]{2,1,0:T(8,128)S(1)}, u32[]{:S(2)}, u32[]{:S(2)}) collective-permute-start(f32[2,256,256]{2,1,0:T(8,128)S(1)} %get-tuple-element.94), channel_id=1, source_target_pairs={{0,68},{1,69},{2,70},{3,71},{4,72},{5,73},{6,74},{7,75},{8,76},{9,... | collective-permute-start | bytes 1572872 | tf_op jit(solution)/shard_map/ppermute | solution.py:359
  79.9 0.0 collective-permute-done.13.refs_2_
  79.9 0.0 collective-permute-done.14.refs_3_
  79.9 0.9 shard_map.76
  80.8 0.1 collective-permute-start.15
  80.9 3.5 %collective-permute-start.16 = (f32[2,256,256]{2,1,0:T(8,128)S(1)}, f32[2,256,256]{2,1,0:T(8,128)S(1)}, u32[]{:S(2)}, u32[]{:S(2)}) collective-permute-start(f32[2,256,256]{2,1,0:T(8,128)S(1)} %get-tuple-element.85), channel_id=1, source_target_pairs={{0,1},{1,2},{2,3},{3,0},{4,5},{5,6},{6,7},{7,4},{8,9},{9,10},{10,1... | collective-permute-start | bytes 1572872 | tf_op jit(solution)/shard_map/ppermute | solution.py:359
  84.4 0.3 collective-permute-start.17
  84.7 7.7 %collective-permute-done.22.refs_7_ = f32[2,256,256]{2,1,0:T(8,128)S(1)} collective-permute-done((f32[2,256,256]{2,1,0:T(8,128)S(1)}, f32[2,256,256]{2,1,0:T(8,128)S(1)}, u32[]{:S(2)}, u32[]{:S(2)}) %collective-permute-start.22) | collective-permute-done | bytes 524320 | tf_op jit(solution)/shard_map/ppermute | solution.py:359
  92.4 4.8 %collective-permute-done.17.refs_3_ = f32[2,256,256]{2,1,0:T(8,128)S(1)} collective-permute-done((f32[2,256,256]{2,1,0:T(8,128)S(1)}, f32[2,256,256]{2,1,0:T(8,128)S(1)}, u32[]{:S(2)}, u32[]{:S(2)}) %collective-permute-start.17) | collective-permute-done | bytes 524320 | tf_op jit(solution)/shard_map/ppermute | solution.py:359
  97.2 1.7 %shard_map.78 = f32[2,2,256,256]{3,2,1,0:T(8,128)} custom-call(s32[4]{0:T(128)S(1)} %broadcast_select_fusion.3.spot, f32[2,256,256]{2,1,0:T(8,128)S(1)} %get-tuple-element.83.refs_0_, f32[2,256,256]{2,1,0:T(8,128)S(1)} %collective-permute-done.15.refs_1_, f32[2,256,256]{2,1,0:T(8,128)S(1)} %collective-permute-done.16.refs_2_, ...), custom_call_target="tpu_custom_call" | custom-call | tf_op jit(solution)/shard_map/pallas_call | solution.py:264
  (23 shorter events, 0.1 us)
Async XLA Ops:
  0.0 10.3 %collective-permute-start.3 = (f32[2,2,256,256]{3,2,1,0:T(8,128)}, f32[2,2,256,256]{3,2,1,0:T(8,128)S(1)}, u32[]{:S(2)}, u32[]{:S(2)}) collective-permute-start(f32[2,2,256,256]{3,2,1,0:T(8,128)} %bitcast.14), channel_id=1, source_target_pairs={{0,64},{1,65},{2,66},{3,67},{4,68},{5,69},{6,70},{7,71},{8,72},{9,... | collective-permute-start | bytes 3145736 | tf_op jit(solution)/shard_map/ppermute | solution.py:359
  2.9 11.8 %collective-permute-start = (s32[4]{0:T(128)S(1)}, s32[4]{0:T(128)S(1)}, u32[]{:S(2)}, u32[]{:S(2)}) collective-permute-start(s32[4]{0:T(128)S(1)} %pad_add_fusion.spot), channel_id=1, source_target_pairs={{64,69},{65,70},{66,71},{67,68},{68,73},{69,74},{70,75},{71,72},{7... | collective-permute-start | bytes 56 | tf_op jit(solution)/shard_map/ppermute | solution.py:359
  7.1 8.6 %collective-permute-start.1 = (s32[4]{0:T(128)S(1)}, s32[4]{0:T(128)S(1)}, u32[]{:S(2)}, u32[]{:S(2)}) collective-permute-start(s32[4]{0:T(128)S(1)} %pad_add_fusion.spot), channel_id=1, source_target_pairs={{0,4},{1,5},{2,6},{3,7},{4,8},{5,9},{6,10},{7,11},{8,12},{9,13},{1... | collective-permute-start | bytes 56 | tf_op jit(solution)/shard_map/ppermute | solution.py:359
  8.5 1.2 %copy-start = (f32[2,2,1,256,256]{4,3,2,1,0:T(8,128)S(1)}, f32[2,2,1,256,256]{4,3,2,1,0:T(8,128)}, u32[]{:S(2)}) copy-start(f32[2,2,1,256,256]{4,3,2,1,0:T(8,128)} %param.6) | copy-start | bytes 3145732
  11.1 16.1 %collective-permute-start.9 = (f32[2,256,256]{2,1,0:T(8,128)S(1)}, f32[2,256,256]{2,1,0:T(8,128)S(1)}, u32[]{:S(2)}, u32[]{:S(2)}) collective-permute-start(f32[2,256,256]{2,1,0:T(8,128)S(1)} %get-tuple-element.60.own), channel_id=1, source_target_pairs={{0,60},{1,61},{2,62},{3,63},{4,0},{5,1},{6,2},{7,3},{8,4},{9,5},{1... | collective-permute-start | bytes 1572872 | tf_op jit(solution)/shard_map/ppermute | solution.py:359
  12.2 16.7 %collective-permute-start.8 = (f32[2,256,256]{2,1,0:T(8,128)S(1)}, f32[2,256,256]{2,1,0:T(8,128)S(1)}, u32[]{:S(2)}, u32[]{:S(2)}) collective-permute-start(f32[2,256,256]{2,1,0:T(8,128)S(1)} %get-tuple-element.58.own), channel_id=1, source_target_pairs={{0,3},{1,0},{2,1},{3,2},{4,7},{5,4},{6,5},{7,6},{8,11},{9,8},{10,9... | collective-permute-start | bytes 1572872 | tf_op jit(solution)/shard_map/ppermute | solution.py:359
  13.4 18.3 %collective-permute-start.5 = (f32[2,256,256]{2,1,0:T(8,128)S(1)}, f32[2,256,256]{2,1,0:T(8,128)S(1)}, u32[]{:S(2)}, u32[]{:S(2)}) collective-permute-start(f32[2,256,256]{2,1,0:T(8,128)S(1)} %get-tuple-element.54.own), channel_id=1, source_target_pairs={{0,60},{1,61},{2,62},{3,63},{4,0},{5,1},{6,2},{7,3},{8,4},{9,5},{1... | collective-permute-start | bytes 1572872 | tf_op jit(solution)/shard_map/ppermute | solution.py:359
  14.7 19.4 %collective-permute-start.4 = (f32[2,256,256]{2,1,0:T(8,128)S(1)}, f32[2,256,256]{2,1,0:T(8,128)S(1)}, u32[]{:S(2)}, u32[]{:S(2)}) collective-permute-start(f32[2,256,256]{2,1,0:T(8,128)S(1)} %get-tuple-element.52.own), channel_id=1, source_target_pairs={{0,3},{1,0},{2,1},{3,2},{4,7},{5,4},{6,5},{7,6},{8,11},{9,8},{10,9... | collective-permute-start | bytes 1572872 | tf_op jit(solution)/shard_map/ppermute | solution.py:359
  15.7 11.4 %collective-permute-start.2 = (s32[4]{0:T(128)S(1)}, s32[4]{0:T(128)S(1)}, u32[]{:S(2)}, u32[]{:S(2)}) collective-permute-start(s32[4]{0:T(128)S(1)} %pad_add_fusion.spot), channel_id=1, source_target_pairs={{0,1},{1,2},{2,3},{3,0},{4,5},{5,6},{6,7},{7,4},{8,9},{9,10},{10,1... | collective-permute-start | bytes 56 | tf_op jit(solution)/shard_map/ppermute | solution.py:359
  27.2 10.4 %copy-start.4 = (f32[1,2,256,256]{3,2,1,0:T(8,128)S(1)}, f32[1,2,256,256]{3,2,1,0:T(8,128)}, u32[]{:S(2)}) copy-start(f32[1,2,256,256]{3,2,1,0:T(8,128)} %param.9) | copy-start | bytes 1572868
  28.7 17.1 %collective-permute-start.11 = (f32[2,256,256]{2,1,0:T(8,128)}, f32[2,256,256]{2,1,0:T(8,128)S(1)}, u32[]{:S(2)}, u32[]{:S(2)}) collective-permute-start(f32[2,256,256]{2,1,0:T(8,128)} %get-tuple-element.63), channel_id=1, source_target_pairs={{0,3},{1,0},{2,1},{3,2},{4,7},{5,4},{6,5},{7,6},{8,11},{9,8},{10,9... | collective-permute-start | bytes 1572872 | tf_op jit(solution)/shard_map/ppermute | solution.py:359
  28.9 12.7 %copy-start.5 = (f32[2,31]{1,0:T(2,128)S(1)}, f32[2,31]{1,0:T(2,128)}, u32[]{:S(2)}) copy-start(f32[2,31]{1,0:T(2,128)} %param.8) | copy-start | bytes 748
  30.4 15.4 %collective-permute-start.10 = (f32[2,256,256]{2,1,0:T(8,128)}, f32[2,256,256]{2,1,0:T(8,128)}, u32[]{:S(2)}, u32[]{:S(2)}) collective-permute-start(f32[2,256,256]{2,1,0:T(8,128)} %get-tuple-element.62), channel_id=1, source_target_pairs={{0,60},{1,61},{2,62},{3,63},{4,0},{5,1},{6,2},{7,3},{8,4},{9,5},{1... | collective-permute-start | bytes 1572872 | tf_op jit(solution)/shard_map/ppermute | solution.py:359
  33.1 12.6 %copy-start.1 = (f32[2,256,256]{2,1,0:T(8,128)S(1)}, f32[2,256,256]{2,1,0:T(8,128)}, u32[]{:S(2)}) copy-start(f32[2,256,256]{2,1,0:T(8,128)} %refs_4_.1) | copy-start | bytes 1572868
  33.1 16.1 %collective-permute-start.7 = (f32[2,256,256]{2,1,0:T(8,128)}, f32[2,256,256]{2,1,0:T(8,128)S(1)}, u32[]{:S(2)}, u32[]{:S(2)}) collective-permute-start(f32[2,256,256]{2,1,0:T(8,128)} %get-tuple-element.57), channel_id=1, source_target_pairs={{0,3},{1,0},{2,1},{3,2},{4,7},{5,4},{6,5},{7,6},{8,11},{9,8},{10,9... | collective-permute-start | bytes 1572872 | tf_op jit(solution)/shard_map/ppermute | solution.py:359
  35.5 0.8 copy-start.2
  36.3 13.0 %collective-permute-start.6 = (f32[2,256,256]{2,1,0:T(8,128)}, f32[2,256,256]{2,1,0:T(8,128)}, u32[]{:S(2)}, u32[]{:S(2)}) collective-permute-start(f32[2,256,256]{2,1,0:T(8,128)} %get-tuple-element.56), channel_id=1, source_target_pairs={{0,60},{1,61},{2,62},{3,63},{4,0},{5,1},{6,2},{7,3},{8,4},{9,5},{1... | collective-permute-start | bytes 1572872 | tf_op jit(solution)/shard_map/ppermute | solution.py:359
  38.4 14.1 %collective-permute-start.12 = (f32[256,256]{1,0:T(8,128)}, f32[256,256]{1,0:T(8,128)}, u32[]{:S(2)}, u32[]{:S(2)}) collective-permute-start(f32[256,256]{1,0:T(8,128)} %get-tuple-element.95), channel_id=1, source_target_pairs={{64,69},{65,70},{66,71},{67,68},{68,73},{69,74},{70,75},{71,72},{7... | collective-permute-start | bytes 786440 | tf_op jit(solution)/shard_map/ppermute | solution.py:359
  45.8 3.5 %copy-start.3 = (f32[2,256,256]{2,1,0:T(8,128)S(1)}, f32[2,256,256]{2,1,0:T(8,128)}, u32[]{:S(2)}) copy-start(f32[2,256,256]{2,1,0:T(8,128)} %copy-done.2) | copy-start | bytes 1572868
  58.0 9.8 %collective-permute-start.18 = (f32[2,256,256]{2,1,0:T(8,128)S(1)}, f32[2,256,256]{2,1,0:T(8,128)S(1)}, u32[]{:S(2)}, u32[]{:S(2)}) collective-permute-start(f32[2,256,256]{2,1,0:T(8,128)S(1)} %get-tuple-element.89), channel_id=1, source_target_pairs={{0,1},{1,2},{2,3},{3,0},{4,5},{5,6},{6,7},{7,4},{8,9},{9,10},{10,1... | collective-permute-start | bytes 1572872 | tf_op jit(solution)/shard_map/ppermute | solution.py:359
  61.7 11.7 %collective-permute-start.19 = (f32[2,256,256]{2,1,0:T(8,128)S(1)}, f32[2,256,256]{2,1,0:T(8,128)S(1)}, u32[]{:S(2)}, u32[]{:S(2)}) collective-permute-start(f32[2,256,256]{2,1,0:T(8,128)S(1)} %get-tuple-element.90), channel_id=1, source_target_pairs={{0,1},{1,2},{2,3},{3,0},{4,5},{5,6},{6,7},{7,4},{8,9},{9,10},{10,1... | collective-permute-start | bytes 1572872 | tf_op jit(solution)/shard_map/ppermute | solution.py:359
  64.1 15.8 %collective-permute-start.13 = (f32[2,256,256]{2,1,0:T(8,128)S(1)}, f32[2,256,256]{2,1,0:T(8,128)S(1)}, u32[]{:S(2)}, u32[]{:S(2)}) collective-permute-start(f32[2,256,256]{2,1,0:T(8,128)S(1)} %get-tuple-element.81), channel_id=1, source_target_pairs={{0,4},{1,5},{2,6},{3,7},{4,8},{5,9},{6,10},{7,11},{8,12},{9,13},{1... | collective-permute-start | bytes 1572872 | tf_op jit(solution)/shard_map/ppermute | solution.py:359
  66.3 13.6 %collective-permute-start.14 = (f32[2,256,256]{2,1,0:T(8,128)S(1)}, f32[2,256,256]{2,1,0:T(8,128)S(1)}, u32[]{:S(2)}, u32[]{:S(2)}) collective-permute-start(f32[2,256,256]{2,1,0:T(8,128)S(1)} %get-tuple-element.82), channel_id=1, source_target_pairs={{0,4},{1,5},{2,6},{3,7},{4,8},{5,9},{6,10},{7,11},{8,12},{9,13},{1... | collective-permute-start | bytes 1572872 | tf_op jit(solution)/shard_map/ppermute | solution.py:359
  74.4 10.0 %collective-permute-start.20 = (f32[2,256,256]{2,1,0:T(8,128)S(1)}, f32[2,256,256]{2,1,0:T(8,128)S(1)}, u32[]{:S(2)}, u32[]{:S(2)}) collective-permute-start(f32[2,256,256]{2,1,0:T(8,128)S(1)} %get-tuple-element.92), channel_id=1, source_target_pairs={{0,64},{1,65},{2,66},{3,67},{4,68},{5,69},{6,70},{7,71},{8,72},{9,... | collective-permute-start | bytes 1572872 | tf_op jit(solution)/shard_map/ppermute | solution.py:359
  74.5 10.2 %collective-permute-start.21 = (f32[2,256,256]{2,1,0:T(8,128)S(1)}, f32[2,256,256]{2,1,0:T(8,128)S(1)}, u32[]{:S(2)}, u32[]{:S(2)}) collective-permute-start(f32[2,256,256]{2,1,0:T(8,128)S(1)} %get-tuple-element.93), channel_id=1, source_target_pairs={{0,4},{1,5},{2,6},{3,7},{4,8},{5,9},{6,10},{7,11},{8,12},{9,13},{1... | collective-permute-start | bytes 1572872 | tf_op jit(solution)/shard_map/ppermute | solution.py:359
  77.0 15.3 %collective-permute-start.22 = (f32[2,256,256]{2,1,0:T(8,128)S(1)}, f32[2,256,256]{2,1,0:T(8,128)S(1)}, u32[]{:S(2)}, u32[]{:S(2)}) collective-permute-start(f32[2,256,256]{2,1,0:T(8,128)S(1)} %get-tuple-element.94), channel_id=1, source_target_pairs={{0,68},{1,69},{2,70},{3,71},{4,72},{5,73},{6,74},{7,75},{8,76},{9,... | collective-permute-start | bytes 1572872 | tf_op jit(solution)/shard_map/ppermute | solution.py:359
  80.8 11.6 %collective-permute-start.15 = (f32[2,256,256]{2,1,0:T(8,128)S(1)}, f32[2,256,256]{2,1,0:T(8,128)S(1)}, u32[]{:S(2)}, u32[]{:S(2)}) collective-permute-start(f32[2,256,256]{2,1,0:T(8,128)S(1)} %get-tuple-element.84), channel_id=1, source_target_pairs={{0,64},{1,65},{2,66},{3,67},{4,68},{5,69},{6,70},{7,71},{8,72},{9,... | collective-permute-start | bytes 1572872 | tf_op jit(solution)/shard_map/ppermute | solution.py:359
  80.9 11.5 %collective-permute-start.16 = (f32[2,256,256]{2,1,0:T(8,128)S(1)}, f32[2,256,256]{2,1,0:T(8,128)S(1)}, u32[]{:S(2)}, u32[]{:S(2)}) collective-permute-start(f32[2,256,256]{2,1,0:T(8,128)S(1)} %get-tuple-element.85), channel_id=1, source_target_pairs={{0,1},{1,2},{2,3},{3,0},{4,5},{5,6},{6,7},{7,4},{8,9},{9,10},{10,1... | collective-permute-start | bytes 1572872 | tf_op jit(solution)/shard_map/ppermute | solution.py:359
  84.4 12.8 %collective-permute-start.17 = (f32[2,256,256]{2,1,0:T(8,128)S(1)}, f32[2,256,256]{2,1,0:T(8,128)S(1)}, u32[]{:S(2)}, u32[]{:S(2)}) collective-permute-start(f32[2,256,256]{2,1,0:T(8,128)S(1)} %get-tuple-element.86), channel_id=1, source_target_pairs={{0,65},{1,66},{2,67},{3,64},{4,69},{5,70},{6,71},{7,68},{8,73},{9,... | collective-permute-start | bytes 1572872 | tf_op jit(solution)/shard_map/ppermute | solution.py:359

commit v3 on v2

--- a/solution.py
+++ b/solution.py
@@ -16,6 +16,8 @@
 BF = jnp.bfloat16
 F32 = jnp.float32
 FIELD = jax.ShapeDtypeStruct((2, N, N), F32)
+PAIR = jax.ShapeDtypeStruct((2, 2, N, N), F32)
+ALL = jax.ShapeDtypeStruct((4, 2, N, N), F32)
 VS = pl.BlockSpec(memory_space=pltpu.VMEM)
 SS = pl.BlockSpec(memory_space=pltpu.SMEM)
 
@@ -155,14 +157,6 @@
             acc[part] = dot3(y_high[part], y_low[part], right_high[index], right_low[index])
 
 
-def gather_patch(spot, p, inner, far, out):
-    mine_cols = own_cols(spot)
-    for sl, _, r0 in chunks():
-        mask = own_rows(spot, r0) if p % 2 == 0 else mine_cols
-        for c in range(2):
-            out[c, sl] = jnp.where(mask, inner[c, sl], far[c, sl])
-
-
 def enter_slice(work, patch, wave):
     for sl, _, r0 in chunks():
         pr, pi, wr, wi = wave[0, sl], wave[1, sl], patch[0, sl], patch[1, sl]
@@ -176,53 +170,54 @@
         wave[1, sl] = acc[s2]
 
 
-def leave_slice(work, spot, p, patch, wave, grad, sent, onward):
+def leave_slice(work, spot, patch, wave, grad, sent_x, sent_y, onward):
     acc = work[4]
     mine_cols = own_cols(spot)
     for sl, s2, r0 in chunks():
         mr, mi, pr, pi = acc[sl], acc[s2], wave[0, sl], wave[1, sl]
-        keep = own_rows(spot, r0) if p % 2 == 0 else mine_cols
-        for c, g in enumerate((pr * mr + pi * mi, pr * mi - pi * mr)):
-            grad[c, sl] = g
-            sent[c, sl] = jnp.where(keep, 0.0, g)
+        re = pr * mr + pi * mi
+        im = pr * mi - pi * mr
+        grad[0, sl] = re
+        grad[1, sl] = im
+        sent_x[sl] = jnp.where(mine_cols, 0.0, re)
+        sent_y[sl] = jnp.where(own_rows(spot, r0), 0.0, im)
         if onward:
             wr, wi = patch[0, sl], patch[1, sl]
             put_field(work, r0, wr * mr + wi * mi, wr * mi - wi * mr)
 
 
-def first_kernel(spot, *refs):
-    inner, far = refs[0:2], refs[2:4]
-    probe, tabs = refs[4], refs[5:9]
-    patches, waves = refs[9:11], refs[11:14]
-    work = refs[14:]
+def down_kernel(spot, *refs):
+    mine, near_x, far_y, other, near_y, far_x = refs[0], refs[1], refs[2], refs[3], refs[4:6], refs[6:8]
+    probe, tabs = refs[8], refs[9:13]
+    patches, waves, spectrum = refs[13:16]
+    work = refs[16:]
+    core = spot[2]
+    cols = own_cols(spot)
+    for q in range(2):
+        for sl, _, r0 in chunks():
+            rows = own_rows(spot, r0)
+            for c in range(2):
+                inner = jnp.where(cols, mine[q, c, sl], near_x[q, c, sl])
+                patches[2 * core + q, c, sl] = jnp.where(rows, inner, far_y[q, c, sl])
+                inner = jnp.where(rows, other[q, c, sl], near_y[q][c, sl])
+                patches[2 - 2 * core + q, c, sl] = jnp.where(cols, inner, far_x[q][c, sl])
     for c in range(2):
-        waves[0][c] = pltpu.roll(pltpu.roll(probe[c], spot[0], 0), spot[1], 1)
-    for p in range(2):
-        gather_patch(spot, p, inner[p], far[p], patches[p])
-        enter_slice(work, patches[p], waves[p])
-        propagate(work, tabs, 0)
-        leave(work, waves[p + 1])
-
-
-def second_kernel(spot, *refs):
-    inner, far = refs[0:2], refs[2:4]
-    wave, tabs = refs[4], refs[5:9]
-    patches, middle, spectrum = refs[9:11], refs[11], refs[12]
+        waves[0, c] = pltpu.roll(pltpu.roll(probe[c], spot[0], 0), spot[1], 1)
+    for k in range(4):
+        enter_slice(work, patches.at[k], waves.at[k])
+        propagate(work, tabs, 0 if k < 3 else 2)
+        leave(work, waves.at[k + 1] if k < 3 else spectrum)
+
+
+def save(work, state):
+    state[0] = work[0][...]
+    state[1] = work[1][...]
+
+
+def turn_up_kernel(spot, *refs):
+    spectrum, measured, shared, waves, patches, tabs = refs[0], refs[1], refs[2], refs[3], refs[4], refs[5:9]
+    grad, sent_x, sent_y, state = refs[9:13]
     work = refs[13:]
-    for p in range(2):
-        gather_patch(spot, p, inner[p], far[p], patches[p])
-    enter_slice(work, patches[0], wave)
-    propagate(work, tabs, 0)
-    leave(work, middle)
-    enter_slice(work, patches[1], middle)
-    propagate(work, tabs, 2)
-    leave(work, spectrum)
-
-
-def third_kernel(spot, *refs):
-    spectrum, measured, shared, wave, patch, tabs = refs[0], refs[1], refs[2], refs[3], refs[4], refs[5:9]
-    grad, sent, state = refs[9:12]
-    work = refs[12:]
     upper = spot[2] == 1
     scale = 2.0 * spot[3].astype(F32)
     for sl, _, r0 in chunks():
@@ -230,30 +225,21 @@
         target = jnp.where(upper, shared[sl], measured[sl])
         misfit = (sr * sr + si * si - target) * scale
         put_field(work, r0, misfit * sr, misfit * si)
-    propagate(work, tabs, 3)
-    leave_slice(work, spot, 3, patch, wave, grad, sent, True)
-    state[0] = work[0][...]
-    state[1] = work[1][...]
-
-
-def back_kernel(p, onward, spot, *refs):
-    state, wave = refs[0], refs[1]
-    n = 2
-    patch = None
-    if onward:
-        patch = refs[2]
-        n = 3
-    tabs = refs[n : n + 4]
-    outs = refs[n + 4 :]
-    grad, sent = outs[0], outs[1]
-    work = outs[3:] if onward else outs[2:]
+    for k in (3, 2):
+        propagate(work, tabs, 3 if k == 3 else 1)
+        leave_slice(work, spot, patches.at[k], waves.at[k], grad.at[k - 2], sent_x.at[k - 2], sent_y.at[k - 2], True)
+    save(work, state)
+
+
+def up_kernel(spot, *refs):
+    state, waves, patches, tabs = refs[0], refs[1], refs[2], refs[3:7]
+    grad, sent_x, sent_y = refs[7:10]
+    work = refs[10:]
     work[0][...] = state[0]
     work[1][...] = state[1]
-    propagate(work, tabs, 1)
-    leave_slice(work, spot, p, patch, wave, grad, sent, onward)
-    if onward:
-        outs[2][0] = work[0][...]
-        outs[2][1] = work[1][...]
+    for k in (1, 0):
+        propagate(work, tabs, 1)
+        leave_slice(work, spot, patches.at[k], waves.at[k], grad.at[k], sent_x.at[k], sent_y.at[k], k > 0)
 
 
 STATE = jax.ShapeDtypeStruct((2, 2 * N, N), BF)
@@ -271,20 +257,16 @@
     )(spot, *args)
 
 
-def blend_kernel(by_rows, spots, own, near, mixed, inner):
-    here = [spots[i] for i in range(3)]
-    there = [spots[4 + i] for i in range(3)]
-    here_cols, there_cols = own_cols(here), own_cols(there)
+def blend_kernel(by_rows, leads, spot, own, near, mixed):
+    cols = own_cols(spot)
     for sl, _, r0 in chunks():
-        here_mask = own_rows(here, r0) if by_rows else here_cols
-        there_mask = own_rows(there, r0) if by_rows else there_cols
-        for c in range(2):
-            u, v = own[c, sl], near[c, sl]
-            mixed[c, sl] = jnp.where(there_mask, u, v)
-            inner[c, sl] = jnp.where(here_mask, u, v)
-
-
-def turn_kernel(parity, spots, *refs):
+        mask = own_rows(spot, r0) if by_rows else cols
+        for lead in leads:
+            at = (*lead, sl)
+            mixed[at] = jnp.where(mask, own[at], near[at])
+
+
+def turn_kernel(channel, spots, *refs):
     grads, came, outs = refs[0:2], refs[2:4], refs[4:8]
     here = [spots[i] for i in range(3)]
     there = [spots[4 + i] for i in range(3)]
@@ -292,21 +274,21 @@
     upper = spots[2] == 1
     for sl, _, r0 in chunks():
         rows = own_rows(here, r0)
-        if parity == 0:
+        if channel == 1:
             first, second, mask = rows, cols, there_cols
         else:
             first, second, mask = cols, rows, own_rows(there, r0)
-        for c in range(2):
+        for q in range(2):
             sent, kept = [], []
             for grad, block in zip(grads, came):
-                g = jnp.where(first, grad[c, sl], 0.0)
-                v = block[c, sl]
+                g = jnp.where(first, grad[q, channel, sl], 0.0)
+                v = block[q, sl]
                 sent.append(jnp.where(second, 0.0, g) + jnp.where(mask, 0.0, v))
                 kept.append(jnp.where(second, g, 0.0) + jnp.where(mask, v, 0.0))
-            outs[0][c, sl] = jnp.where(upper, sent[1], sent[0])
-            outs[1][c, sl] = jnp.where(upper, sent[0], sent[1])
-            outs[2][c, sl] = jnp.where(upper, kept[1], kept[0])
-            outs[3][c, sl] = jnp.where(upper, kept[0], kept[1])
+            outs[0][q, sl] = jnp.where(upper, sent[1], sent[0])
+            outs[1][q, sl] = jnp.where(upper, sent[0], sent[1])
+            outs[2][q, sl] = jnp.where(upper, kept[1], kept[0])
+            outs[3][q, sl] = jnp.where(upper, kept[0], kept[1])
 
 
 def final_kernel(spot, *refs):
@@ -314,25 +296,8 @@
     for q in range(2):
         for c in range(2):
             for sl, _, _ in chunks():
-                a, b, x, y = (refs[4 * q + i][c, sl] for i in range(4))
+                a, b, x, y = (refs[4 * c + i][q, sl] for i in range(4))
                 out[q, c, sl] = (a + b) + (x + y)
-
-
-def load_kernel(spot, mine, *outs):
-    for k in range(2):
-        for c in range(2):
-            for sl, _, _ in chunks():
-                outs[k][c, sl] = mine[k, c, sl]
-
-
-def order_kernel(spot, *refs):
-    mine, other, outs = refs[0:2], refs[2], refs[3:7]
-    upper = spot[2] == 1
-    for k in range(4):
-        for c in range(2):
-            for sl, _, _ in chunks():
-                a, b = mine[k % 2][c, sl], other[k % 2, c, sl]
-                outs[k][c, sl] = jnp.where(upper, b, a) if k < 2 else jnp.where(upper, a, b)
 
 
 def moved(t, dx, dy):
@@ -371,52 +336,47 @@
     core = lax.axis_index("depth").astype(jnp.int32)
     mine = transmission[:, :, 0]
     other = permute(mine, SWAP)
+    near_x = permute(mine, GATHER[0])
     alive = (core < counts[0]).astype(jnp.int32)
     info = jnp.concatenate([jnp.where(core == 0, offsets[0, 0], offsets[0, 1]), core[None], alive[None]])
-    loaded = call(load_kernel, [FIELD] * 2, info, [mine])
     left = permute(info, INFO[0])
     up = permute(info, INFO[1])
     upleft = permute(info, DIAGONAL)
     here = jnp.where(core == 0, info, upleft)
     at_y = jnp.where(core == 0, up, left)
     at_x = jnp.where(core == 0, left, up)
-    own = call(order_kernel, [FIELD] * 4, info, [*loaded, other])
-
-    near = [permute(own[p], GATHER[p % 2]) for p in range(4)]
+    near_y = [permute(other[q], GATHER[1]) for q in range(2)]
+
+    leads = tuple((q, c) for q in range(2) for c in range(2))
+    mixed, = call(functools.partial(blend_kernel, False, leads), [PAIR], at_y, [mine, near_x])
+    far_y = permute(mixed, GATHER[1])
+    far_x = []
+    for q in range(2):
+        mixed, = call(functools.partial(blend_kernel, True, ((0,), (1,))), [FIELD], at_x, [other[q], near_y[q]])
+        far_x.append(permute(mixed, GATHER[0]))
     shared = permute(intensity[0, 1], DIAGONAL)
-    far, inner = [], []
-    both = [jnp.concatenate([here, spot]) for spot in (at_y, at_x)]
-    for p in range(4):
-        mixed, kept = call(functools.partial(blend_kernel, p % 2 == 1), [FIELD] * 2, both[p % 2], [own[p], near[p]])
-        inner.append(kept)
-        far.append(permute(mixed, GATHER[1 - p % 2]))
 
     tabs = tables(here, tap_rows(fresnel_taps), fourier())
-    _, patch1, wave0, wave1, wave2 = call(
-        first_kernel, [FIELD] * 5, here, [*inner[:2], *far[:2], illumination, *tabs], WORK
+    patches, waves, spectrum = call(
+        down_kernel, [ALL, ALL, FIELD], here,
+        [mine, near_x, far_y, other, *near_y, *far_x, illumination, *tabs], WORK
     )
-    patch2, patch3, wave3, spectrum = call(second_kernel, [FIELD] * 4, here, [*inner[2:], *far[2:], wave2, *tabs], WORK)
-    grad3, sent3, state = call(
-        third_kernel, [FIELD] * 2 + [STATE], here, [spectrum, intensity[0, 0], shared, wave3, patch3, *tabs], WORK
+    grad_high, x_high, y_high, state = call(
+        turn_up_kernel, [PAIR, FIELD, FIELD, STATE], here,
+        [spectrum, intensity[0, 0], shared, waves, patches, *tabs], WORK
     )
-    grads = [None, None, None, grad3]
-    came = [None, None, None, permute(sent3, SCATTER[0])]
-    for p, wave, patch in ((2, wave2, patch2), (1, wave1, patch1), (0, wave0, None)):
-        onward = p > 0
-        outs = call(
-            functools.partial(back_kernel, p, onward), [FIELD] * 2 + [STATE] * onward, here,
-            [state, wave] + [patch] * onward + list(tabs), WORK
+    came_high = [permute(x_high, SCATTER[0]), permute(y_high, SCATTER[1])]
+    grad_low, x_low, y_low = call(up_kernel, [PAIR, FIELD, FIELD], here, [state, waves, patches, *tabs], WORK)
+    came_low = [permute(x_low, SCATTER[0]), permute(y_low, SCATTER[1])]
+    parts = []
+    for channel, there in ((0, at_x), (1, at_y)):
+        straight, cross, stay, leaving = call(
+            functools.partial(turn_kernel, channel), [FIELD] * 4, jnp.concatenate([here, there]),
+            [grad_low, grad_high, came_low[channel], came_high[channel]]
         )
-        grads[p] = outs[0]
-        came[p] = permute(outs[1], SCATTER[1 - p % 2])
-        state = outs[2] if onward else None
-    parts = [None, None]
-    for q in (1, 0):
-        straight, cross, stay, leaving = call(
-            functools.partial(turn_kernel, q), [FIELD] * 4, both[q], [grads[q], grads[q + 2], came[q], came[q + 2]]
-        )
-        parts[q] = [stay, permute(leaving, SWAP), permute(straight, SCATTER[q]), permute(cross, CROSSED[q])]
-    out, = call(final_kernel, [jax.ShapeDtypeStruct((2, 2, N, N), F32)], here, parts[0] + parts[1])
+        way = 1 - channel
+        parts += [stay, permute(leaving, SWAP), permute(straight, SCATTER[way]), permute(cross, CROSSED[way])]
+    out, = call(final_kernel, [PAIR], here, parts)
     return out[:, :, None]
 
 

time: 99.2 us -> 102 us (1.028)
  waiting for transfers between devices: 30.6 us -> 37 us
  Pallas kernels: 27.1 us -> 22.5 us
  starting transfers between devices: 35.2 us -> 37.2 us
    ppermute x23 -> x21, waiting for transfers between devices: 30.6 us -> 37 us  [permute(): return lax.ppermute(block, ('depth', 'tiles'), pairs)]
    pallas_call x15 -> x9, Pallas kernels: 24.4 us -> 19.7 us  [call(): pl.pallas_call(kernel, out_shape=outs, in_specs=[SS] + [VS] * len(args),...]
    unnamed x12 -> x8, local copies, waits for them, and re-layouts: 2.04 us -> 0.02 us
    ppermute x23 -> x21, starting transfers between devices: 35.2 us -> 37.2 us  [permute(): return lax.ppermute(block, ('depth', 'tiles'), pairs)]
    squeeze x0 -> x1, local copies, waits for them, and re-layouts: none -> 1.06 us  [step(): near_y = [permute(other[q], GATHER[1]) for q in range(2)]]
  transfers between devices with their start and end apart: 23 -> 21, of which waited for: 5 -> 7; matrix products, arithmetic and copies ran while one was open for 3% -> 4% of each run, Pallas kernels for 20% -> 15%
where the time goes in v3:
time: 102 us
  starting transfers between devices  37.2 us (36%)
  waiting for transfers between devices  37 us (36%)
  Pallas kernels  22.5 us (22%)
  other arithmetic  2.17 us (2%)
  local copies, waits for them, and re-layouts  1.98 us (2%)
    ppermute x21, starting transfers between devices, permute(): return lax.ppermute(block, ('depth', 'tiles'), pairs)  37.2 us
    ppermute x21, waiting for transfers between devices, permute(): return lax.ppermute(block, ('depth', 'tiles'), pairs)  37 us
    pallas_call x9, Pallas kernels, call(): pl.pallas_call(kernel, out_shape=outs, in_specs=[SS] + [VS] * len(args),...  19.7 us
    pallas_call x1, Pallas kernels, tables(): pl.pallas_call(tables_kernel, out_shape=[jax.ShapeDtypeStruct((4, 2 * N,...  2.74 us
  transfers between devices with their start and end apart: 21, of which 7 were waited for; matrix products, arithmetic and copies ran while one was open for 4% of the time, Pallas kernels for 15%

profile of v3, /device:TPU:1, one launch (start us, length us, event | category | flops | bytes accessed | tf_op | source)
XLA Modules:
  0.0 101.6 jit_solution(11194204710792151682)
XLA Ops:
  0.0 1.4 %collective-permute-start.5 = (f32[2,2,256,256]{3,2,1,0:T(8,128)}, f32[2,2,256,256]{3,2,1,0:T(8,128)S(1)}, u32[]{:S(2)}, u32[]{:S(2)}) collective-permute-start(f32[2,2,256,256]{3,2,1,0:T(8,128)} %bitcast.18), channel_id=1, source_target_pairs={{0,64},{1,65},{2,66},{3,67},{4,68},{5,69},{6,70},{7,71},{8,72},{9,... | collective-permute-start | bytes 3145736 | tf_op jit(solution)/shard_map/ppermute | solution.py:324
  1.4 1.3 %collective-permute-start.3 = (f32[2,2,256,256]{3,2,1,0:T(8,128)}, f32[2,2,256,256]{3,2,1,0:T(8,128)S(1)}, u32[]{:S(2)}, u32[]{:S(2)}) collective-permute-start(f32[2,2,256,256]{3,2,1,0:T(8,128)} %bitcast.19), channel_id=1, source_target_pairs={{0,3},{1,0},{2,1},{3,2},{4,7},{5,4},{6,5},{7,6},{8,11},{9,8},{10,9... | collective-permute-start | bytes 3145736 | tf_op jit(solution)/shard_map/ppermute | solution.py:324
  3.4 0.8 fusion.6
  4.1 0.1 pad_add_fusion
  4.2 1.2 %collective-permute-start.1 = (s32[4]{0:T(128)S(1)}, s32[4]{0:T(128)S(1)}, u32[]{:S(2)}, u32[]{:S(2)}) collective-permute-start(s32[4]{0:T(128)S(1)} %pad_add_fusion), channel_id=1, source_target_pairs={{0,1},{1,2},{2,3},{3,0},{4,5},{5,6},{6,7},{7,4},{8,9},{9,10},{10,1... | collective-permute-start | bytes 56 | tf_op jit(solution)/shard_map/ppermute | solution.py:324
  5.4 1.3 %collective-permute-start.2 = (s32[4]{0:T(128)S(1)}, s32[4]{0:T(128)S(1)}, u32[]{:S(2)}, u32[]{:S(2)}) collective-permute-start(s32[4]{0:T(128)S(1)} %pad_add_fusion), channel_id=1, source_target_pairs={{0,4},{1,5},{2,6},{3,7},{4,8},{5,9},{6,10},{7,11},{8,12},{9,13},{1... | collective-permute-start | bytes 56 | tf_op jit(solution)/shard_map/ppermute | solution.py:324
  6.7 0.0 collective-permute-done.5.refs_3_
  6.7 1.1 %slice_bitcast_fusion = (f32[2,256,256]{2,1,0:T(8,128)}, f32[2,256,256]{2,1,0:T(8,128)}) fusion(f32[2,2,256,256]{3,2,1,0:T(8,128)S(1)} %collective-permute-done.5.refs_3_), kind=kLoop, calls=%fused_computation | loop fusion | bytes 2097152 | tf_op jit(solution)/shard_map/squeeze | solution.py:348
  7.8 1.3 %collective-permute-start.6 = (f32[2,256,256]{2,1,0:T(8,128)}, f32[2,256,256]{2,1,0:T(8,128)}, u32[]{:S(2)}, u32[]{:S(2)}) collective-permute-start(f32[2,256,256]{2,1,0:T(8,128)} %get-tuple-element.50.own), channel_id=1, source_target_pairs={{0,60},{1,61},{2,62},{3,63},{4,0},{5,1},{6,2},{7,3},{8,4},{9,5},{1... | collective-permute-start | bytes 1572872 | tf_op jit(solution)/shard_map/ppermute | solution.py:324
  9.1 1.0 collective-permute-start.7
  10.1 6.5 %collective-permute-done.1 = s32[4]{0:T(128)S(1)} collective-permute-done((s32[4]{0:T(128)S(1)}, s32[4]{0:T(128)S(1)}, u32[]{:S(2)}, u32[]{:S(2)}) %collective-permute-start.1) | collective-permute-done | bytes 48 | tf_op jit(solution)/shard_map/ppermute | solution.py:324
  16.6 0.0 collective-permute-done.2
  16.6 0.0 collective-permute-done.3.near.refs_1_
  16.6 0.0 copy-start.3
  16.6 1.6 %shard_map.64 = f32[2,2,256,256]{3,2,1,0:T(8,128)} custom-call(s32[4]{0:T(128)S(1)} %get-tuple-element.53.spot, f32[2,2,256,256]{3,2,1,0:T(8,128)S(1)} %bitcast.20, f32[2,2,256,256]{3,2,1,0:T(8,128)S(1)} %collective-permute-done.3.near.refs_1_), custom_call_target="tpu_custom_call" | custom-call | tf_op jit(solution)/shard_map/pallas_call | solution.py:250
  18.2 1.4 %collective-permute-start.4 = (f32[2,2,256,256]{3,2,1,0:T(8,128)}, f32[2,2,256,256]{3,2,1,0:T(8,128)}, u32[]{:S(2)}, u32[]{:S(2)}) collective-permute-start(f32[2,2,256,256]{3,2,1,0:T(8,128)} %shard_map.64), channel_id=1, source_target_pairs={{0,60},{1,61},{2,62},{3,63},{4,0},{5,1},{6,2},{7,3},{8,4},{9,5},{1... | collective-permute-start | bytes 3145736 | tf_op jit(solution)/shard_map/ppermute | solution.py:324
  19.6 3.2 %collective-permute-start = (s32[4]{0:T(128)S(1)}, s32[4]{0:T(128)S(1)}, u32[]{:S(2)}, u32[]{:S(2)}) collective-permute-start(s32[4]{0:T(128)S(1)} %pad_add_fusion), channel_id=1, source_target_pairs={{64,69},{65,70},{66,71},{67,68},{68,73},{69,74},{70,75},{71,72},{7... | collective-permute-start | bytes 56 | tf_op jit(solution)/shard_map/ppermute | solution.py:324
  22.9 0.7 slice_bitcast_fusion.2
  23.6 3.8 %collective-permute-start.10 = (f32[256,256]{1,0:T(8,128)}, f32[256,256]{1,0:T(8,128)}, u32[]{:S(2)}, u32[]{:S(2)}) collective-permute-start(f32[256,256]{1,0:T(8,128)} %get-tuple-element.51), channel_id=1, source_target_pairs={{64,69},{65,70},{66,71},{67,68},{68,73},{69,74},{70,75},{71,72},{7... | collective-permute-start | bytes 786440 | tf_op jit(solution)/shard_map/ppermute | solution.py:324
  27.4 0.1 rev.3
  27.5 1.1 %negate_multiply_fusion = (f32[1,256,256]{2,1,0:T(8,128)S(1)}, f32[1,256,256]{2,1,0:T(8,128)S(1)}) fusion(), kind=kLoop, calls=%fused_computation.11 | loop fusion | flops 1114112 | bytes 524288 | tf_op jit(solution)/shard_map/mul | solution.py:332
  28.6 0.0 collective-permute-done.6.near.refs_4_
  28.6 0.0 copy-start.1
  28.6 1.3 %shard_map.65 = f32[2,256,256]{2,1,0:T(8,128)S(1)} custom-call(s32[4]{0:T(128)S(1)} %get-tuple-element.54.spot, f32[2,256,256]{2,1,0:T(8,128)} %get-tuple-element.50.own, f32[2,256,256]{2,1,0:T(8,128)} %collective-permute-done.6.near.refs_4_), custom_call_target="tpu_custom_call" | custom-call | tf_op jit(solution)/shard_map/pallas_call | solution.py:250
  29.9 1.0 collective-permute-start.8
  30.9 0.0 collective-permute-done.7.near.refs_5_
  30.9 1.3 %shard_map.66 = f32[2,256,256]{2,1,0:T(8,128)S(1)} custom-call(s32[4]{0:T(128)S(1)} %get-tuple-element.54.spot, f32[2,256,256]{2,1,0:T(8,128)} %get-tuple-element.49.own, f32[2,256,256]{2,1,0:T(8,128)} %collective-permute-done.7.near.refs_5_), custom_call_target="tpu_custom_call" | custom-call | tf_op jit(solution)/shard_map/pallas_call | solution.py:250
  32.2 1.7 %collective-permute-start.9 = (f32[2,256,256]{2,1,0:T(8,128)S(1)}, f32[2,256,256]{2,1,0:T(8,128)S(1)}, u32[]{:S(2)}, u32[]{:S(2)}) collective-permute-start(f32[2,256,256]{2,1,0:T(8,128)S(1)} %shard_map.66), channel_id=1, source_target_pairs={{0,3},{1,0},{2,1},{3,2},{4,7},{5,4},{6,5},{7,6},{8,11},{9,8},{10,9... | collective-permute-start | bytes 1572872 | tf_op jit(solution)/shard_map/ppermute | solution.py:324
  33.9 0.1 slice.38
  34.0 0.1 pad_maximum_fusion.1.taps
  34.1 0.0 collective-permute-done
  34.1 0.1 broadcast_select_fusion.3.spot
  34.1 2.7 %tables.1 = (bf16[4,512,512]{2,1,0:T(8,128)(2,1)S(1)}, bf16[4,512,512]{2,1,0:T(8,128)(2,1)S(1)}, bf16[4,512,256]{2,1,0:T(8,128)(2,1)S(1)}, bf16[4,512,256]{2,1,0:T(8,128)(2,1)S(1)}) custom-call(s32[4]{0:T(128)S(1)} %broadcast_select_fusion.3.spot, f32[8,256]{1,0:T(8,128)S(1)} %pad_maximum_fusion.1.taps, f32[2,256,256]{2,1,0:T(8,128)S(1)} %pad_maximum_fusion.dft), custom_call_target="tpu_custom_call" | custom-call | tf_op jit(solution)/shard_map/tables/pallas_call | solution.py:96
  36.9 2.4 %collective-permute-done.8.refs_6_ = f32[2,256,256]{2,1,0:T(8,128)S(1)} collective-permute-done((f32[2,256,256]{2,1,0:T(8,128)S(1)}, f32[2,256,256]{2,1,0:T(8,128)S(1)}, u32[]{:S(2)}, u32[]{:S(2)}) %collective-permute-start.8) | collective-permute-done | bytes 524320 | tf_op jit(solution)/shard_map/ppermute | solution.py:324
  39.3 5.6 %collective-permute-done.9.refs_7_ = f32[2,256,256]{2,1,0:T(8,128)S(1)} collective-permute-done((f32[2,256,256]{2,1,0:T(8,128)S(1)}, f32[2,256,256]{2,1,0:T(8,128)S(1)}, u32[]{:S(2)}, u32[]{:S(2)}) %collective-permute-start.9) | collective-permute-done | bytes 524320 | tf_op jit(solution)/shard_map/ppermute | solution.py:324
  44.9 0.0 collective-permute-done.4.refs_2_
  44.9 6.2 %shard_map.67 = (f32[4,2,256,256]{3,2,1,0:T(8,128)S(1)}, f32[4,2,256,256]{3,2,1,0:T(8,128)S(1)}, f32[2,256,256]{2,1,0:T(8,128)S(1)}) custom-call(s32[4]{0:T(128)S(1)} %broadcast_select_fusion.3.spot, f32[2,2,256,256]{3,2,1,0:T(8,128)S(1)} %bitcast.21, f32[2,2,256,256]{3,2,1,0:T(8,128)S(1)} %collective-permute-done.3.near.refs_1_, ...), custom_call_target="tpu_custom_call" | custom-call | tf_op jit(solution)/shard_map/pallas_call | solution.py:250
  51.0 0.0 collective-permute-done.10.refs_2_
  51.0 3.2 %shard_map.68 = (f32[2,2,256,256]{3,2,1,0:T(8,128)S(1)}, f32[2,256,256]{2,1,0:T(8,128)S(1)}, f32[2,256,256]{2,1,0:T(8,128)S(1)}, bf16[2,512,256]{2,1,0:T(8,128)(2,1)S(1)}) custom-call(s32[4]{0:T(128)S(1)} %broadcast_select_fusion.3.spot, f32[2,256,256]{2,1,0:T(8,128)S(1)} %get-tuple-element.31.refs_0_, f32[256,256]{1,0:T(8,128)S(1)} %get-tuple-element.52.refs_1_, ...), custom_call_target="tpu_custom_call" | custom-call | tf_op jit(solution)/shard_map/pallas_call | solution.py:250
  54.3 2.6 %shard_map.69 = (f32[2,2,256,256]{3,2,1,0:T(8,128)S(1)}, f32[2,256,256]{2,1,0:T(8,128)S(1)}, f32[2,256,256]{2,1,0:T(8,128)S(1)}) custom-call(s32[4]{0:T(128)S(1)} %broadcast_select_fusion.3.spot, bf16[2,512,256]{2,1,0:T(8,128)(2,1)S(1)} %get-tuple-element.34.refs_0_, f32[4,2,256,256]{3,2,1,0:T(8,128)S(1)} %get-tuple-element.32.refs_3_.refs_1_, ...), custom_call_target="tpu_custom_call" | custom-call | tf_op jit(solution)/shard_map/pallas_call | solution.py:250
  56.9 3.9 %collective-permute-start.16 = (f32[2,256,256]{2,1,0:T(8,128)S(1)}, f32[2,256,256]{2,1,0:T(8,128)S(1)}, u32[]{:S(2)}, u32[]{:S(2)}) collective-permute-start(f32[2,256,256]{2,1,0:T(8,128)S(1)} %get-tuple-element.43), channel_id=1, source_target_pairs={{0,4},{1,5},{2,6},{3,7},{4,8},{5,9},{6,10},{7,11},{8,12},{9,13},{1... | collective-permute-start | bytes 1572872 | tf_op jit(solution)/shard_map/ppermute | solution.py:324
  60.8 0.2 collective-permute-start.17
  61.0 0.1 pad_add_fusion.2
  61.0 1.0 collective-permute-start.11
  62.0 0.4 collective-permute-start.12
  62.4 4.5 %collective-permute-done.16.refs_2_ = f32[2,256,256]{2,1,0:T(8,128)S(1)} collective-permute-done((f32[2,256,256]{2,1,0:T(8,128)S(1)}, f32[2,256,256]{2,1,0:T(8,128)S(1)}, u32[]{:S(2)}, u32[]{:S(2)}) %collective-permute-start.16) | collective-permute-done | bytes 524320 | tf_op jit(solution)/shard_map/ppermute | solution.py:324
  66.9 5.6 %collective-permute-done.17.refs_3_ = f32[2,256,256]{2,1,0:T(8,128)S(1)} collective-permute-done((f32[2,256,256]{2,1,0:T(8,128)S(1)}, f32[2,256,256]{2,1,0:T(8,128)S(1)}, u32[]{:S(2)}, u32[]{:S(2)}) %collective-permute-start.17) | collective-permute-done | bytes 524320 | tf_op jit(solution)/shard_map/ppermute | solution.py:324
  72.5 0.9 shard_map.71
  73.4 4.1 %collective-permute-start.18 = (f32[2,256,256]{2,1,0:T(8,128)S(1)}, f32[2,256,256]{2,1,0:T(8,128)S(1)}, u32[]{:S(2)}, u32[]{:S(2)}) collective-permute-start(f32[2,256,256]{2,1,0:T(8,128)S(1)} %get-tuple-element.46), channel_id=1, source_target_pairs={{0,64},{1,65},{2,66},{3,67},{4,68},{5,69},{6,70},{7,71},{8,72},{9,... | collective-permute-start | bytes 1572872 | tf_op jit(solution)/shard_map/ppermute | solution.py:324
  77.5 3.4 %collective-permute-start.19 = (f32[2,256,256]{2,1,0:T(8,128)S(1)}, f32[2,256,256]{2,1,0:T(8,128)S(1)}, u32[]{:S(2)}, u32[]{:S(2)}) collective-permute-start(f32[2,256,256]{2,1,0:T(8,128)S(1)} %get-tuple-element.47), channel_id=1, source_target_pairs={{0,1},{1,2},{2,3},{3,0},{4,5},{5,6},{6,7},{7,4},{8,9},{9,10},{10,1... | collective-permute-start | bytes 1572872 | tf_op jit(solution)/shard_map/ppermute | solution.py:324
  80.9 0.1 collective-permute-start.20
  81.0 0.0 collective-permute-done.11.refs_2_
  81.0 0.0 collective-permute-done.12.refs_3_
  81.0 0.9 shard_map.70
  81.9 0.1 collective-permute-start.13
  82.0 1.1 %collective-permute-start.14 = (f32[2,256,256]{2,1,0:T(8,128)S(1)}, f32[2,256,256]{2,1,0:T(8,128)S(1)}, u32[]{:S(2)}, u32[]{:S(2)}) collective-permute-start(f32[2,256,256]{2,1,0:T(8,128)S(1)} %get-tuple-element.41), channel_id=1, source_target_pairs={{0,4},{1,5},{2,6},{3,7},{4,8},{5,9},{6,10},{7,11},{8,12},{9,13},{1... | collective-permute-start | bytes 1572872 | tf_op jit(solution)/shard_map/ppermute | solution.py:324
  83.1 0.0 collective-permute-done.18.refs_5_
  83.1 4.3 %collective-permute-start.15 = (f32[2,256,256]{2,1,0:T(8,128)S(1)}, f32[2,256,256]{2,1,0:T(8,128)S(1)}, u32[]{:S(2)}, u32[]{:S(2)}) collective-permute-start(f32[2,256,256]{2,1,0:T(8,128)S(1)} %get-tuple-element.42), channel_id=1, source_target_pairs={{0,68},{1,69},{2,70},{3,71},{4,72},{5,73},{6,74},{7,75},{8,76},{9,... | collective-permute-start | bytes 1572872 | tf_op jit(solution)/shard_map/ppermute | solution.py:324
  87.4 0.0 collective-permute-done.19.refs_6_
  87.4 6.2 %collective-permute-done.20.refs_7_ = f32[2,256,256]{2,1,0:T(8,128)S(1)} collective-permute-done((f32[2,256,256]{2,1,0:T(8,128)S(1)}, f32[2,256,256]{2,1,0:T(8,128)S(1)}, u32[]{:S(2)}, u32[]{:S(2)}) %collective-permute-start.20) | collective-permute-done | bytes 524320 | tf_op jit(solution)/shard_map/ppermute | solution.py:324
  93.7 0.0 collective-permute-done.13.refs_1_
  93.7 0.0 collective-permute-done.14.refs_2_
  93.7 6.2 %collective-permute-done.15.refs_3_ = f32[2,256,256]{2,1,0:T(8,128)S(1)} collective-permute-done((f32[2,256,256]{2,1,0:T(8,128)S(1)}, f32[2,256,256]{2,1,0:T(8,128)S(1)}, u32[]{:S(2)}, u32[]{:S(2)}) %collective-permute-start.15) | collective-permute-done | bytes 524320 | tf_op jit(solution)/shard_map/ppermute | solution.py:324
  99.9 1.7 %shard_map.72 = f32[2,2,256,256]{3,2,1,0:T(8,128)} custom-call(s32[4]{0:T(128)S(1)} %broadcast_select_fusion.3.spot, f32[2,256,256]{2,1,0:T(8,128)S(1)} %get-tuple-element.39.refs_0_, f32[2,256,256]{2,1,0:T(8,128)S(1)} %collective-permute-done.13.refs_1_, f32[2,256,256]{2,1,0:T(8,128)S(1)} %collective-permute-done.14.refs_2_, ...), custom_call_target="tpu_custom_call" | custom-call | tf_op jit(solution)/shard_map/pallas_call | solution.py:250
  (10 shorter events, 0.1 us)
Async XLA Ops:
  0.0 16.6 %copy-start = (f32[2,2,1,256,256]{4,3,2,1,0:T(8,128)S(1)}, f32[2,2,1,256,256]{4,3,2,1,0:T(8,128)}, u32[]{:S(2)}) copy-start(f32[2,2,1,256,256]{4,3,2,1,0:T(8,128)} %param.6) | copy-start | bytes 3145732
  0.0 6.7 %collective-permute-start.5 = (f32[2,2,256,256]{3,2,1,0:T(8,128)}, f32[2,2,256,256]{3,2,1,0:T(8,128)S(1)}, u32[]{:S(2)}, u32[]{:S(2)}) collective-permute-start(f32[2,2,256,256]{3,2,1,0:T(8,128)} %bitcast.18), channel_id=1, source_target_pairs={{0,64},{1,65},{2,66},{3,67},{4,68},{5,69},{6,70},{7,71},{8,72},{9,... | collective-permute-start | bytes 3145736 | tf_op jit(solution)/shard_map/ppermute | solution.py:324
  1.4 15.2 %collective-permute-start.3 = (f32[2,2,256,256]{3,2,1,0:T(8,128)}, f32[2,2,256,256]{3,2,1,0:T(8,128)S(1)}, u32[]{:S(2)}, u32[]{:S(2)}) collective-permute-start(f32[2,2,256,256]{3,2,1,0:T(8,128)} %bitcast.19), channel_id=1, source_target_pairs={{0,3},{1,0},{2,1},{3,2},{4,7},{5,4},{6,5},{7,6},{8,11},{9,8},{10,9... | collective-permute-start | bytes 3145736 | tf_op jit(solution)/shard_map/ppermute | solution.py:324
  4.2 12.3 %collective-permute-start.1 = (s32[4]{0:T(128)S(1)}, s32[4]{0:T(128)S(1)}, u32[]{:S(2)}, u32[]{:S(2)}) collective-permute-start(s32[4]{0:T(128)S(1)} %pad_add_fusion), channel_id=1, source_target_pairs={{0,1},{1,2},{2,3},{3,0},{4,5},{5,6},{6,7},{7,4},{8,9},{9,10},{10,1... | collective-permute-start | bytes 56 | tf_op jit(solution)/shard_map/ppermute | solution.py:324
  5.4 11.1 %collective-permute-start.2 = (s32[4]{0:T(128)S(1)}, s32[4]{0:T(128)S(1)}, u32[]{:S(2)}, u32[]{:S(2)}) collective-permute-start(s32[4]{0:T(128)S(1)} %pad_add_fusion), channel_id=1, source_target_pairs={{0,4},{1,5},{2,6},{3,7},{4,8},{5,9},{6,10},{7,11},{8,12},{9,13},{1... | collective-permute-start | bytes 56 | tf_op jit(solution)/shard_map/ppermute | solution.py:324
  7.8 15.1 %copy-start.2 = (f32[1,2,256,256]{3,2,1,0:T(8,128)S(1)}, f32[1,2,256,256]{3,2,1,0:T(8,128)}, u32[]{:S(2)}) copy-start(f32[1,2,256,256]{3,2,1,0:T(8,128)} %param.9) | copy-start | bytes 1572868
  7.8 20.8 %collective-permute-start.6 = (f32[2,256,256]{2,1,0:T(8,128)}, f32[2,256,256]{2,1,0:T(8,128)}, u32[]{:S(2)}, u32[]{:S(2)}) collective-permute-start(f32[2,256,256]{2,1,0:T(8,128)} %get-tuple-element.50.own), channel_id=1, source_target_pairs={{0,60},{1,61},{2,62},{3,63},{4,0},{5,1},{6,2},{7,3},{8,4},{9,5},{1... | collective-permute-start | bytes 1572872 | tf_op jit(solution)/shard_map/ppermute | solution.py:324
  9.1 21.9 %collective-permute-start.7 = (f32[2,256,256]{2,1,0:T(8,128)}, f32[2,256,256]{2,1,0:T(8,128)}, u32[]{:S(2)}, u32[]{:S(2)}) collective-permute-start(f32[2,256,256]{2,1,0:T(8,128)} %get-tuple-element.49.own), channel_id=1, source_target_pairs={{0,60},{1,61},{2,62},{3,63},{4,0},{5,1},{6,2},{7,3},{8,4},{9,5},{1... | collective-permute-start | bytes 1572872 | tf_op jit(solution)/shard_map/ppermute | solution.py:324
  16.6 10.9 %copy-start.3 = (f32[2,31]{1,0:T(2,128)S(1)}, f32[2,31]{1,0:T(2,128)}, u32[]{:S(2)}) copy-start(f32[2,31]{1,0:T(2,128)} %param.8) | copy-start | bytes 748
  18.2 26.7 %collective-permute-start.4 = (f32[2,2,256,256]{3,2,1,0:T(8,128)}, f32[2,2,256,256]{3,2,1,0:T(8,128)}, u32[]{:S(2)}, u32[]{:S(2)}) collective-permute-start(f32[2,2,256,256]{3,2,1,0:T(8,128)} %shard_map.64), channel_id=1, source_target_pairs={{0,60},{1,61},{2,62},{3,63},{4,0},{5,1},{6,2},{7,3},{8,4},{9,5},{1... | collective-permute-start | bytes 3145736 | tf_op jit(solution)/shard_map/ppermute | solution.py:324
  19.6 14.5 %collective-permute-start = (s32[4]{0:T(128)S(1)}, s32[4]{0:T(128)S(1)}, u32[]{:S(2)}, u32[]{:S(2)}) collective-permute-start(s32[4]{0:T(128)S(1)} %pad_add_fusion), channel_id=1, source_target_pairs={{64,69},{65,70},{66,71},{67,68},{68,73},{69,74},{70,75},{71,72},{7... | collective-permute-start | bytes 56 | tf_op jit(solution)/shard_map/ppermute | solution.py:324
  23.6 27.4 %collective-permute-start.10 = (f32[256,256]{1,0:T(8,128)}, f32[256,256]{1,0:T(8,128)}, u32[]{:S(2)}, u32[]{:S(2)}) collective-permute-start(f32[256,256]{1,0:T(8,128)} %get-tuple-element.51), channel_id=1, source_target_pairs={{64,69},{65,70},{66,71},{67,68},{68,73},{69,74},{70,75},{71,72},{7... | collective-permute-start | bytes 786440 | tf_op jit(solution)/shard_map/ppermute | solution.py:324
  28.6 16.3 %copy-start.1 = (f32[2,256,256]{2,1,0:T(8,128)S(1)}, f32[2,256,256]{2,1,0:T(8,128)}, u32[]{:S(2)}) copy-start(f32[2,256,256]{2,1,0:T(8,128)} %refs_8_.1) | copy-start | bytes 1572868
  29.9 9.3 %collective-permute-start.8 = (f32[2,256,256]{2,1,0:T(8,128)S(1)}, f32[2,256,256]{2,1,0:T(8,128)S(1)}, u32[]{:S(2)}, u32[]{:S(2)}) collective-permute-start(f32[2,256,256]{2,1,0:T(8,128)S(1)} %shard_map.65), channel_id=1, source_target_pairs={{0,3},{1,0},{2,1},{3,2},{4,7},{5,4},{6,5},{7,6},{8,11},{9,8},{10,9... | collective-permute-start | bytes 1572872 | tf_op jit(solution)/shard_map/ppermute | solution.py:324
  32.2 12.7 %collective-permute-start.9 = (f32[2,256,256]{2,1,0:T(8,128)S(1)}, f32[2,256,256]{2,1,0:T(8,128)S(1)}, u32[]{:S(2)}, u32[]{:S(2)}) collective-permute-start(f32[2,256,256]{2,1,0:T(8,128)S(1)} %shard_map.66), channel_id=1, source_target_pairs={{0,3},{1,0},{2,1},{3,2},{4,7},{5,4},{6,5},{7,6},{8,11},{9,8},{10,9... | collective-permute-start | bytes 1572872 | tf_op jit(solution)/shard_map/ppermute | solution.py:324
  56.9 10.0 %collective-permute-start.16 = (f32[2,256,256]{2,1,0:T(8,128)S(1)}, f32[2,256,256]{2,1,0:T(8,128)S(1)}, u32[]{:S(2)}, u32[]{:S(2)}) collective-permute-start(f32[2,256,256]{2,1,0:T(8,128)S(1)} %get-tuple-element.43), channel_id=1, source_target_pairs={{0,4},{1,5},{2,6},{3,7},{4,8},{5,9},{6,10},{7,11},{8,12},{9,13},{1... | collective-permute-start | bytes 1572872 | tf_op jit(solution)/shard_map/ppermute | solution.py:324
  60.8 11.7 %collective-permute-start.17 = (f32[2,256,256]{2,1,0:T(8,128)S(1)}, f32[2,256,256]{2,1,0:T(8,128)S(1)}, u32[]{:S(2)}, u32[]{:S(2)}) collective-permute-start(f32[2,256,256]{2,1,0:T(8,128)S(1)} %get-tuple-element.44), channel_id=1, source_target_pairs={{0,4},{1,5},{2,6},{3,7},{4,8},{5,9},{6,10},{7,11},{8,12},{9,13},{1... | collective-permute-start | bytes 1572872 | tf_op jit(solution)/shard_map/ppermute | solution.py:324
  61.0 20.0 %collective-permute-start.11 = (f32[2,256,256]{2,1,0:T(8,128)S(1)}, f32[2,256,256]{2,1,0:T(8,128)S(1)}, u32[]{:S(2)}, u32[]{:S(2)}) collective-permute-start(f32[2,256,256]{2,1,0:T(8,128)S(1)} %get-tuple-element.37), channel_id=1, source_target_pairs={{0,1},{1,2},{2,3},{3,0},{4,5},{5,6},{6,7},{7,4},{8,9},{9,10},{10,1... | collective-permute-start | bytes 1572872 | tf_op jit(solution)/shard_map/ppermute | solution.py:324
  62.0 19.0 %collective-permute-start.12 = (f32[2,256,256]{2,1,0:T(8,128)S(1)}, f32[2,256,256]{2,1,0:T(8,128)S(1)}, u32[]{:S(2)}, u32[]{:S(2)}) collective-permute-start(f32[2,256,256]{2,1,0:T(8,128)S(1)} %get-tuple-element.38), channel_id=1, source_target_pairs={{0,1},{1,2},{2,3},{3,0},{4,5},{5,6},{6,7},{7,4},{8,9},{9,10},{10,1... | collective-permute-start | bytes 1572872 | tf_op jit(solution)/shard_map/ppermute | solution.py:324
  73.4 9.7 %collective-permute-start.18 = (f32[2,256,256]{2,1,0:T(8,128)S(1)}, f32[2,256,256]{2,1,0:T(8,128)S(1)}, u32[]{:S(2)}, u32[]{:S(2)}) collective-permute-start(f32[2,256,256]{2,1,0:T(8,128)S(1)} %get-tuple-element.46), channel_id=1, source_target_pairs={{0,64},{1,65},{2,66},{3,67},{4,68},{5,69},{6,70},{7,71},{8,72},{9,... | collective-permute-start | bytes 1572872 | tf_op jit(solution)/shard_map/ppermute | solution.py:324
  77.5 9.9 %collective-permute-start.19 = (f32[2,256,256]{2,1,0:T(8,128)S(1)}, f32[2,256,256]{2,1,0:T(8,128)S(1)}, u32[]{:S(2)}, u32[]{:S(2)}) collective-permute-start(f32[2,256,256]{2,1,0:T(8,128)S(1)} %get-tuple-element.47), channel_id=1, source_target_pairs={{0,1},{1,2},{2,3},{3,0},{4,5},{5,6},{6,7},{7,4},{8,9},{9,10},{10,1... | collective-permute-start | bytes 1572872 | tf_op jit(solution)/shard_map/ppermute | solution.py:324
  80.9 12.7 %collective-permute-start.20 = (f32[2,256,256]{2,1,0:T(8,128)S(1)}, f32[2,256,256]{2,1,0:T(8,128)S(1)}, u32[]{:S(2)}, u32[]{:S(2)}) collective-permute-start(f32[2,256,256]{2,1,0:T(8,128)S(1)} %get-tuple-element.48), channel_id=1, source_target_pairs={{0,65},{1,66},{2,67},{3,64},{4,69},{5,70},{6,71},{7,68},{8,73},{9,... | collective-permute-start | bytes 1572872 | tf_op jit(solution)/shard_map/ppermute | solution.py:324
  81.9 11.8 %collective-permute-start.13 = (f32[2,256,256]{2,1,0:T(8,128)S(1)}, f32[2,256,256]{2,1,0:T(8,128)S(1)}, u32[]{:S(2)}, u32[]{:S(2)}) collective-permute-start(f32[2,256,256]{2,1,0:T(8,128)S(1)} %get-tuple-element.40), channel_id=1, source_target_pairs={{0,64},{1,65},{2,66},{3,67},{4,68},{5,69},{6,70},{7,71},{8,72},{9,... | collective-permute-start | bytes 1572872 | tf_op jit(solution)/shard_map/ppermute | solution.py:324
  82.0 11.7 %collective-permute-start.14 = (f32[2,256,256]{2,1,0:T(8,128)S(1)}, f32[2,256,256]{2,1,0:T(8,128)S(1)}, u32[]{:S(2)}, u32[]{:S(2)}) collective-permute-start(f32[2,256,256]{2,1,0:T(8,128)S(1)} %get-tuple-element.41), channel_id=1, source_target_pairs={{0,4},{1,5},{2,6},{3,7},{4,8},{5,9},{6,10},{7,11},{8,12},{9,13},{1... | collective-permute-start | bytes 1572872 | tf_op jit(solution)/shard_map/ppermute | solution.py:324
  83.1 16.8 %collective-permute-start.15 = (f32[2,256,256]{2,1,0:T(8,128)S(1)}, f32[2,256,256]{2,1,0:T(8,128)S(1)}, u32[]{:S(2)}, u32[]{:S(2)}) collective-permute-start(f32[2,256,256]{2,1,0:T(8,128)S(1)} %get-tuple-element.42), channel_id=1, source_target_pairs={{0,68},{1,69},{2,70},{3,71},{4,72},{5,73},{6,74},{7,75},{8,76},{9,... | collective-permute-start | bytes 1572872 | tf_op jit(solution)/shard_map/ppermute | solution.py:324

commit v4 on v3

--- a/solution.py
+++ b/solution.py
@@ -58,7 +58,8 @@
         base = jnp.broadcast_to(taps[k : k + 1, :], (N, N))
         return pltpu.roll(base, 0, 1, stride=1, stride_axis=0)
 
-    rings = [circulant(k) for k in range(4)]
+    rings = [circulant(0), circulant(1)]
+    rings += [ring.T for ring in rings]
     fr, fi = dft[0], dft[1]
 
     def bands(shift):
@@ -106,8 +107,7 @@
 
 
 def tap_rows(taps):
-    rows = jnp.concatenate([taps, taps[:, ::-1]], 0)
-    rows = jnp.pad(rows, ((0, 4), (0, N - rows.shape[1])))
+    rows = jnp.pad(taps, ((0, 6), (0, N - taps.shape[1])))
     return jnp.roll(rows, -15, 1)
 
 
@@ -187,10 +187,10 @@
 
 
 def down_kernel(spot, *refs):
-    mine, near_x, far_y, other, near_y, far_x = refs[0], refs[1], refs[2], refs[3], refs[4:6], refs[6:8]
-    probe, tabs = refs[8], refs[9:13]
-    patches, waves, spectrum = refs[13:16]
-    work = refs[16:]
+    mine, near_x, far_y, other, near_y, far_x = refs[0:6]
+    probe, tabs = refs[6], refs[7:11]
+    patches, waves, spectrum = refs[11:14]
+    work = refs[14:]
     core = spot[2]
     cols = own_cols(spot)
     for q in range(2):
@@ -199,8 +199,8 @@
             for c in range(2):
                 inner = jnp.where(cols, mine[q, c, sl], near_x[q, c, sl])
                 patches[2 * core + q, c, sl] = jnp.where(rows, inner, far_y[q, c, sl])
-                inner = jnp.where(rows, other[q, c, sl], near_y[q][c, sl])
-                patches[2 - 2 * core + q, c, sl] = jnp.where(cols, inner, far_x[q][c, sl])
+                inner = jnp.where(rows, other[q, c, sl], near_y[q, c, sl])
+                patches[2 - 2 * core + q, c, sl] = jnp.where(cols, inner, far_x[q, c, sl])
     for c in range(2):
         waves[0, c] = pltpu.roll(pltpu.roll(probe[c], spot[0], 0), spot[1], 1)
     for k in range(4):
@@ -257,13 +257,20 @@
     )(spot, *args)
 
 
-def blend_kernel(by_rows, leads, spot, own, near, mixed):
+def load_kernel(spot, block, out):
+    for q in range(2):
+        for c in range(2):
+            for sl, _, _ in chunks():
+                out[q, c, sl] = block[q, c, sl]
+
+
+def blend_kernel(by_rows, spot, own, near, mixed):
     cols = own_cols(spot)
     for sl, _, r0 in chunks():
         mask = own_rows(spot, r0) if by_rows else cols
-        for lead in leads:
-            at = (*lead, sl)
-            mixed[at] = jnp.where(mask, own[at], near[at])
+        for q in range(2):
+            for c in range(2):
+                mixed[q, c, sl] = jnp.where(mask, own[q, c, sl], near[q, c, sl])
 
 
 def turn_kernel(channel, spots, *refs):
@@ -345,21 +352,20 @@
     here = jnp.where(core == 0, info, upleft)
     at_y = jnp.where(core == 0, up, left)
     at_x = jnp.where(core == 0, left, up)
-    near_y = [permute(other[q], GATHER[1]) for q in range(2)]
-
-    leads = tuple((q, c) for q in range(2) for c in range(2))
-    mixed, = call(functools.partial(blend_kernel, False, leads), [PAIR], at_y, [mine, near_x])
+    near_y = permute(other, GATHER[1])
+
+    mine, = call(load_kernel, [PAIR], info, [mine])
+    mixed, = call(functools.partial(blend_kernel, False), [PAIR], at_y, [mine, near_x])
     far_y = permute(mixed, GATHER[1])
-    far_x = []
-    for q in range(2):
-        mixed, = call(functools.partial(blend_kernel, True, ((0,), (1,))), [FIELD], at_x, [other[q], near_y[q]])
-        far_x.append(permute(mixed, GATHER[0]))
-    shared = permute(intensity[0, 1], DIAGONAL)
+    mixed, = call(functools.partial(blend_kernel, True), [PAIR], at_x, [other, near_y])
+    far_x = permute(mixed, GATHER[0])
+    second_slot = intensity[0, 1]
+    shared = permute(second_slot, DIAGONAL)
 
     tabs = tables(here, tap_rows(fresnel_taps), fourier())
     patches, waves, spectrum = call(
         down_kernel, [ALL, ALL, FIELD], here,
-        [mine, near_x, far_y, other, *near_y, *far_x, illumination, *tabs], WORK
+        [mine, near_x, far_y, other, near_y, far_x, illumination, *tabs], WORK
     )
     grad_high, x_high, y_high, state = call(
         turn_up_kernel, [PAIR, FIELD, FIELD, STATE], here,

time: 102 us -> 95 us (0.931)
  starting transfers between devices: 37.2 us -> 31.5 us
  Pallas kernels: 22.5 us -> 18.8 us
  waiting for transfers between devices: 37 us -> 40.1 us
    ppermute x21 -> x19, starting transfers between devices: 37.2 us -> 31.5 us  [permute(): return lax.ppermute(block, ('depth', 'tiles'), pairs)]
    pallas_call x9, Pallas kernels: 19.7 us -> 16.1 us  [call(): pl.pallas_call(kernel, out_shape=outs, in_specs=[SS] + [VS] * len(args),...]
    ppermute x21 -> x19, waiting for transfers between devices: 37 us -> 40.1 us  [permute(): return lax.ppermute(block, ('depth', 'tiles'), pairs)]
    squeeze x2 -> x1, local copies, waits for them, and re-layouts: 1.79 us -> 0.03 us  [step(): second_slot = intensity[0, 1]]
    unnamed x8, local copies, waits for them, and re-layouts: 0.02 us -> 1.24 us
  transfers between devices with their start and end apart: 21 -> 19, of which waited for: 7 -> 9; matrix products, arithmetic and copies ran while one was open for 4% -> 2% of each run, Pallas kernels for 15% -> 12%
where the time goes in v4:
time: 95 us; the launch traced here: 94.8 us
  waiting for transfers between devices  40.1 us (42%)
  starting transfers between devices  31.5 us (33%)
  Pallas kernels  18.8 us (20%)
  other arithmetic  2.16 us (2%)
  local copies, waits for them, and re-layouts  1.35 us (1%)
    ppermute x19, waiting for transfers between devices, permute(): return lax.ppermute(block, ('depth', 'tiles'), pairs)  40.1 us
    ppermute x19, starting transfers between devices, permute(): return lax.ppermute(block, ('depth', 'tiles'), pairs)  31.5 us
    pallas_call x9, Pallas kernels, call(): pl.pallas_call(kernel, out_shape=outs, in_specs=[SS] + [VS] * len(args),...  16.1 us
    pallas_call x1, Pallas kernels, tables(): pl.pallas_call(tables_kernel, out_shape=[jax.ShapeDtypeStruct((4, 2 * N,...  2.7 us
  transfers between devices with their start and end apart: 19, of which 9 were waited for; matrix products, arithmetic and copies ran while one was open for 2% of the time, Pallas kernels for 12%

profile of v4, /device:TPU:1, one launch (start us, length us, event | category | flops | bytes accessed | tf_op | source)
XLA Modules:
  0.0 94.8 jit_solution(14354162618734216368)
XLA Ops:
  0.0 1.4 %collective-permute-start.5 = (f32[2,2,256,256]{3,2,1,0:T(8,128)}, f32[2,2,256,256]{3,2,1,0:T(8,128)S(1)}, u32[]{:S(2)}, u32[]{:S(2)}) collective-permute-start(f32[2,2,256,256]{3,2,1,0:T(8,128)} %bitcast.14), channel_id=1, source_target_pairs={{0,64},{1,65},{2,66},{3,67},{4,68},{5,69},{6,70},{7,71},{8,72},{9,... | collective-permute-start | bytes 3145736 | tf_op jit(solution)/shard_map/ppermute | solution.py:331
  1.4 1.3 %collective-permute-start.3 = (f32[2,2,256,256]{3,2,1,0:T(8,128)}, f32[2,2,256,256]{3,2,1,0:T(8,128)S(1)}, u32[]{:S(2)}, u32[]{:S(2)}) collective-permute-start(f32[2,2,256,256]{3,2,1,0:T(8,128)} %bitcast.15), channel_id=1, source_target_pairs={{0,3},{1,0},{2,1},{3,2},{4,7},{5,4},{6,5},{7,6},{8,11},{9,8},{10,9... | collective-permute-start | bytes 3145736 | tf_op jit(solution)/shard_map/ppermute | solution.py:331
  2.7 1.2 %collective-permute-done.5.own.refs_3_ = f32[2,2,256,256]{3,2,1,0:T(8,128)S(1)} collective-permute-done((f32[2,2,256,256]{3,2,1,0:T(8,128)}, f32[2,2,256,256]{3,2,1,0:T(8,128)S(1)}, u32[]{:S(2)}, u32[]{:S(2)}) %collective-permute-start.5) | collective-permute-done | bytes 1048608 | tf_op jit(solution)/shard_map/ppermute | solution.py:331
  3.9 1.4 %collective-permute-start.6 = (f32[2,2,256,256]{3,2,1,0:T(8,128)S(1)}, f32[2,2,256,256]{3,2,1,0:T(8,128)S(1)}, u32[]{:S(2)}, u32[]{:S(2)}) collective-permute-start(f32[2,2,256,256]{3,2,1,0:T(8,128)S(1)} %collective-permute-done.5.own.refs_3_), channel_id=1, source_target_pairs={{0,60},{1,61},{2,62},{3,63},{4,0},{5,1},{6,2},{7,3},{8,4},{9,5},{1... | collective-permute-start | bytes 3145736 | tf_op jit(solution)/shard_map/ppermute | solution.py:331
  5.9 0.8 fusion.6
  6.7 0.1 pad_add_fusion.spot
  6.8 1.2 %collective-permute-start.1 = (s32[4]{0:T(128)S(1)}, s32[4]{0:T(128)S(1)}, u32[]{:S(2)}, u32[]{:S(2)}) collective-permute-start(s32[4]{0:T(128)S(1)} %pad_add_fusion.spot), channel_id=1, source_target_pairs={{0,1},{1,2},{2,3},{3,0},{4,5},{5,6},{6,7},{7,4},{8,9},{9,10},{10,1... | collective-permute-start | bytes 56 | tf_op jit(solution)/shard_map/ppermute | solution.py:331
  8.0 1.3 %collective-permute-start.2 = (s32[4]{0:T(128)S(1)}, s32[4]{0:T(128)S(1)}, u32[]{:S(2)}, u32[]{:S(2)}) collective-permute-start(s32[4]{0:T(128)S(1)} %pad_add_fusion.spot), channel_id=1, source_target_pairs={{0,4},{1,5},{2,6},{3,7},{4,8},{5,9},{6,10},{7,11},{8,12},{9,13},{1... | collective-permute-start | bytes 56 | tf_op jit(solution)/shard_map/ppermute | solution.py:331
  9.3 3.8 %collective-permute-start = (s32[4]{0:T(128)S(1)}, s32[4]{0:T(128)S(1)}, u32[]{:S(2)}, u32[]{:S(2)}) collective-permute-start(s32[4]{0:T(128)S(1)} %pad_add_fusion.spot), channel_id=1, source_target_pairs={{64,69},{65,70},{66,71},{67,68},{68,73},{69,74},{70,75},{71,72},{7... | collective-permute-start | bytes 56 | tf_op jit(solution)/shard_map/ppermute | solution.py:331
  13.1 0.0 copy-start
  13.1 1.2 %copy-done = f32[2,2,1,256,256]{4,3,2,1,0:T(8,128)S(1)} copy-done((f32[2,2,1,256,256]{4,3,2,1,0:T(8,128)S(1)}, f32[2,2,1,256,256]{4,3,2,1,0:T(8,128)}, u32[]{:S(2)}) %copy-start) | copy-done | bytes 1048600
  14.4 0.6 shard_map.64.own.refs_0_
  15.0 1.8 %collective-permute-done.1 = s32[4]{0:T(128)S(1)} collective-permute-done((s32[4]{0:T(128)S(1)}, s32[4]{0:T(128)S(1)}, u32[]{:S(2)}, u32[]{:S(2)}) %collective-permute-start.1) | collective-permute-done | bytes 48 | tf_op jit(solution)/shard_map/ppermute | solution.py:331
  16.7 5.7 %collective-permute-done.2 = s32[4]{0:T(128)S(1)} collective-permute-done((s32[4]{0:T(128)S(1)}, s32[4]{0:T(128)S(1)}, u32[]{:S(2)}, u32[]{:S(2)}) %collective-permute-start.2) | collective-permute-done | bytes 48 | tf_op jit(solution)/shard_map/ppermute | solution.py:331
  22.5 0.0 collective-permute-done.3.near.refs_1_
  22.5 0.7 shard_map.65
  23.2 0.0 copy-start.2
  23.2 0.1 collective-permute-start.4
  23.3 0.0 collective-permute-done.6.near.refs_4_
  23.3 0.0 copy-start.3
  23.3 0.7 shard_map.66
  23.9 0.0 copy-start.1
  24.0 1.3 %collective-permute-start.7 = (f32[2,2,256,256]{3,2,1,0:T(8,128)S(1)}, f32[2,2,256,256]{3,2,1,0:T(8,128)S(1)}, u32[]{:S(2)}, u32[]{:S(2)}) collective-permute-start(f32[2,2,256,256]{3,2,1,0:T(8,128)S(1)} %shard_map.66), channel_id=1, source_target_pairs={{0,3},{1,0},{2,1},{3,2},{4,7},{5,4},{6,5},{7,6},{8,11},{9,8},{10,9... | collective-permute-start | bytes 3145736 | tf_op jit(solution)/shard_map/ppermute | solution.py:331
  25.2 0.0 copy-done.2
  25.3 2.1 %collective-permute-start.8 = (f32[256,256]{1,0:T(8,128)S(1)}, f32[256,256]{1,0:T(8,128)S(1)}, u32[]{:S(2)}, u32[]{:S(2)}) collective-permute-start(f32[256,256]{1,0:T(8,128)S(1)} %get-tuple-element.49), channel_id=1, source_target_pairs={{64,69},{65,70},{66,71},{67,68},{68,73},{69,74},{70,75},{71,72},{7... | collective-permute-start | bytes 786440 | tf_op jit(solution)/shard_map/ppermute | solution.py:331
  27.4 0.0 copy-done.3
  27.4 0.1 pad_slice_fusion.1
  27.5 1.1 %negate_multiply_fusion = (f32[1,256,256]{2,1,0:T(8,128)S(1)}, f32[1,256,256]{2,1,0:T(8,128)S(1)}) fusion(), kind=kLoop, calls=%fused_computation.9 | loop fusion | flops 1114112 | bytes 524288 | tf_op jit(solution)/shard_map/mul | solution.py:339
  28.6 0.1 pad_maximum_fusion.1.taps
  28.7 0.0 collective-permute-done
  28.7 0.1 broadcast_select_fusion.3.spot
  28.7 2.7 %tables.1 = (bf16[4,512,512]{2,1,0:T(8,128)(2,1)S(1)}, bf16[4,512,512]{2,1,0:T(8,128)(2,1)S(1)}, bf16[4,512,256]{2,1,0:T(8,128)(2,1)S(1)}, bf16[4,512,256]{2,1,0:T(8,128)(2,1)S(1)}) custom-call(s32[4]{0:T(128)S(1)} %broadcast_select_fusion.3.spot, f32[8,256]{1,0:T(8,128)S(1)} %pad_maximum_fusion.1.taps, f32[2,256,256]{2,1,0:T(8,128)S(1)} %pad_maximum_fusion.dft), custom_call_target="tpu_custom_call" | custom-call | tf_op jit(solution)/shard_map/tables/pallas_call | solution.py:97
  31.5 8.8 %collective-permute-done.4.refs_2_ = f32[2,2,256,256]{3,2,1,0:T(8,128)S(1)} collective-permute-done((f32[2,2,256,256]{3,2,1,0:T(8,128)S(1)}, f32[2,2,256,256]{3,2,1,0:T(8,128)S(1)}, u32[]{:S(2)}, u32[]{:S(2)}) %collective-permute-start.4) | collective-permute-done | bytes 1048608 | tf_op jit(solution)/shard_map/ppermute | solution.py:331
  40.2 0.0 collective-permute-done.7.refs_5_
  40.2 0.0 copy-done.1
  40.2 5.2 %shard_map.67 = (f32[4,2,256,256]{3,2,1,0:T(8,128)S(1)}, f32[4,2,256,256]{3,2,1,0:T(8,128)S(1)}, f32[2,256,256]{2,1,0:T(8,128)S(1)}) custom-call(s32[4]{0:T(128)S(1)} %broadcast_select_fusion.3.spot, f32[2,2,256,256]{3,2,1,0:T(8,128)S(1)} %shard_map.64.own.refs_0_, f32[2,2,256,256]{3,2,1,0:T(8,128)S(1)} %collective-permute-done.3.near.refs_1_, ...), custom_call_target="tpu_custom_call" | custom-call | tf_op jit(solution)/shard_map/pallas_call | solution.py:250
  45.4 0.7 collective-permute-done.8.refs_2_
  46.2 2.8 %shard_map.68 = (f32[2,2,256,256]{3,2,1,0:T(8,128)S(1)}, f32[2,256,256]{2,1,0:T(8,128)S(1)}, f32[2,256,256]{2,1,0:T(8,128)S(1)}, bf16[2,512,256]{2,1,0:T(8,128)(2,1)S(1)}) custom-call(s32[4]{0:T(128)S(1)} %broadcast_select_fusion.3.spot, f32[2,256,256]{2,1,0:T(8,128)S(1)} %get-tuple-element.31.refs_0_, f32[256,256]{1,0:T(8,128)S(1)} %get-tuple-element.50.refs_1_, ...), custom_call_target="tpu_custom_call" | custom-call | tf_op jit(solution)/shard_map/pallas_call | solution.py:250
  49.0 2.6 %shard_map.69 = (f32[2,2,256,256]{3,2,1,0:T(8,128)S(1)}, f32[2,256,256]{2,1,0:T(8,128)S(1)}, f32[2,256,256]{2,1,0:T(8,128)S(1)}) custom-call(s32[4]{0:T(128)S(1)} %broadcast_select_fusion.3.spot, bf16[2,512,256]{2,1,0:T(8,128)(2,1)S(1)} %get-tuple-element.34.refs_0_, f32[4,2,256,256]{3,2,1,0:T(8,128)S(1)} %get-tuple-element.32.refs_3_.refs_1_, ...), custom_call_target="tpu_custom_call" | custom-call | tf_op jit(solution)/shard_map/pallas_call | solution.py:250
  51.6 2.8 %collective-permute-start.14 = (f32[2,256,256]{2,1,0:T(8,128)S(1)}, f32[2,256,256]{2,1,0:T(8,128)S(1)}, u32[]{:S(2)}, u32[]{:S(2)}) collective-permute-start(f32[2,256,256]{2,1,0:T(8,128)S(1)} %get-tuple-element.43), channel_id=1, source_target_pairs={{0,4},{1,5},{2,6},{3,7},{4,8},{5,9},{6,10},{7,11},{8,12},{9,13},{1... | collective-permute-start | bytes 1572872 | tf_op jit(solution)/shard_map/ppermute | solution.py:331
  54.4 0.1 collective-permute-start.15
  54.5 0.1 pad_add_fusion.2
  54.6 1.6 %collective-permute-start.9 = (f32[2,256,256]{2,1,0:T(8,128)S(1)}, f32[2,256,256]{2,1,0:T(8,128)S(1)}, u32[]{:S(2)}, u32[]{:S(2)}) collective-permute-start(f32[2,256,256]{2,1,0:T(8,128)S(1)} %get-tuple-element.37), channel_id=1, source_target_pairs={{0,1},{1,2},{2,3},{3,0},{4,5},{5,6},{6,7},{7,4},{8,9},{9,10},{10,1... | collective-permute-start | bytes 1572872 | tf_op jit(solution)/shard_map/ppermute | solution.py:331
  56.1 0.6 collective-permute-start.10
  56.7 3.9 %collective-permute-done.14.refs_2_ = f32[2,256,256]{2,1,0:T(8,128)S(1)} collective-permute-done((f32[2,256,256]{2,1,0:T(8,128)S(1)}, f32[2,256,256]{2,1,0:T(8,128)S(1)}, u32[]{:S(2)}, u32[]{:S(2)}) %collective-permute-start.14) | collective-permute-done | bytes 524320 | tf_op jit(solution)/shard_map/ppermute | solution.py:331
  60.5 5.6 %collective-permute-done.15.refs_3_ = f32[2,256,256]{2,1,0:T(8,128)S(1)} collective-permute-done((f32[2,256,256]{2,1,0:T(8,128)S(1)}, f32[2,256,256]{2,1,0:T(8,128)S(1)}, u32[]{:S(2)}, u32[]{:S(2)}) %collective-permute-start.15) | collective-permute-done | bytes 524320 | tf_op jit(solution)/shard_map/ppermute | solution.py:331
  66.2 0.9 shard_map.71
  67.0 3.6 %collective-permute-start.16 = (f32[2,256,256]{2,1,0:T(8,128)S(1)}, f32[2,256,256]{2,1,0:T(8,128)S(1)}, u32[]{:S(2)}, u32[]{:S(2)}) collective-permute-start(f32[2,256,256]{2,1,0:T(8,128)S(1)} %get-tuple-element.46), channel_id=1, source_target_pairs={{0,64},{1,65},{2,66},{3,67},{4,68},{5,69},{6,70},{7,71},{8,72},{9,... | collective-permute-start | bytes 1572872 | tf_op jit(solution)/shard_map/ppermute | solution.py:331
  70.6 3.4 %collective-permute-start.17 = (f32[2,256,256]{2,1,0:T(8,128)S(1)}, f32[2,256,256]{2,1,0:T(8,128)S(1)}, u32[]{:S(2)}, u32[]{:S(2)}) collective-permute-start(f32[2,256,256]{2,1,0:T(8,128)S(1)} %get-tuple-element.47), channel_id=1, source_target_pairs={{0,1},{1,2},{2,3},{3,0},{4,5},{5,6},{6,7},{7,4},{8,9},{9,10},{10,1... | collective-permute-start | bytes 1572872 | tf_op jit(solution)/shard_map/ppermute | solution.py:331
  74.0 0.1 collective-permute-start.18
  74.1 0.0 collective-permute-done.9.refs_2_
  74.1 0.0 collective-permute-done.10.refs_3_
  74.1 0.9 shard_map.70
  75.0 0.1 collective-permute-start.11
  75.1 1.7 %collective-permute-start.12 = (f32[2,256,256]{2,1,0:T(8,128)S(1)}, f32[2,256,256]{2,1,0:T(8,128)S(1)}, u32[]{:S(2)}, u32[]{:S(2)}) collective-permute-start(f32[2,256,256]{2,1,0:T(8,128)S(1)} %get-tuple-element.41), channel_id=1, source_target_pairs={{0,4},{1,5},{2,6},{3,7},{4,8},{5,9},{6,10},{7,11},{8,12},{9,13},{1... | collective-permute-start | bytes 1572872 | tf_op jit(solution)/shard_map/ppermute | solution.py:331
  76.8 0.0 collective-permute-done.16.refs_5_
  76.8 3.8 %collective-permute-start.13 = (f32[2,256,256]{2,1,0:T(8,128)S(1)}, f32[2,256,256]{2,1,0:T(8,128)S(1)}, u32[]{:S(2)}, u32[]{:S(2)}) collective-permute-start(f32[2,256,256]{2,1,0:T(8,128)S(1)} %get-tuple-element.42), channel_id=1, source_target_pairs={{0,68},{1,69},{2,70},{3,71},{4,72},{5,73},{6,74},{7,75},{8,76},{9,... | collective-permute-start | bytes 1572872 | tf_op jit(solution)/shard_map/ppermute | solution.py:331
  80.6 0.0 collective-permute-done.17.refs_6_
  80.6 6.2 %collective-permute-done.18.refs_7_ = f32[2,256,256]{2,1,0:T(8,128)S(1)} collective-permute-done((f32[2,256,256]{2,1,0:T(8,128)S(1)}, f32[2,256,256]{2,1,0:T(8,128)S(1)}, u32[]{:S(2)}, u32[]{:S(2)}) %collective-permute-start.18) | collective-permute-done | bytes 524320 | tf_op jit(solution)/shard_map/ppermute | solution.py:331
  86.8 0.0 collective-permute-done.11.refs_1_
  86.8 0.0 collective-permute-done.12.refs_2_
  86.8 6.2 %collective-permute-done.13.refs_3_ = f32[2,256,256]{2,1,0:T(8,128)S(1)} collective-permute-done((f32[2,256,256]{2,1,0:T(8,128)S(1)}, f32[2,256,256]{2,1,0:T(8,128)S(1)}, u32[]{:S(2)}, u32[]{:S(2)}) %collective-permute-start.13) | collective-permute-done | bytes 524320 | tf_op jit(solution)/shard_map/ppermute | solution.py:331
  93.0 1.7 %shard_map.72 = f32[2,2,256,256]{3,2,1,0:T(8,128)} custom-call(s32[4]{0:T(128)S(1)} %broadcast_select_fusion.3.spot, f32[2,256,256]{2,1,0:T(8,128)S(1)} %get-tuple-element.39.refs_0_, f32[2,256,256]{2,1,0:T(8,128)S(1)} %collective-permute-done.11.refs_1_, f32[2,256,256]{2,1,0:T(8,128)S(1)} %collective-permute-done.12.refs_2_, ...), custom_call_target="tpu_custom_call" | custom-call | tf_op jit(solution)/shard_map/pallas_call | solution.py:250
  (4 shorter events, 0.1 us)
Async XLA Ops:
  0.0 3.9 %collective-permute-start.5 = (f32[2,2,256,256]{3,2,1,0:T(8,128)}, f32[2,2,256,256]{3,2,1,0:T(8,128)S(1)}, u32[]{:S(2)}, u32[]{:S(2)}) collective-permute-start(f32[2,2,256,256]{3,2,1,0:T(8,128)} %bitcast.14), channel_id=1, source_target_pairs={{0,64},{1,65},{2,66},{3,67},{4,68},{5,69},{6,70},{7,71},{8,72},{9,... | collective-permute-start | bytes 3145736 | tf_op jit(solution)/shard_map/ppermute | solution.py:331
  1.4 21.1 %collective-permute-start.3 = (f32[2,2,256,256]{3,2,1,0:T(8,128)}, f32[2,2,256,256]{3,2,1,0:T(8,128)S(1)}, u32[]{:S(2)}, u32[]{:S(2)}) collective-permute-start(f32[2,2,256,256]{3,2,1,0:T(8,128)} %bitcast.15), channel_id=1, source_target_pairs={{0,3},{1,0},{2,1},{3,2},{4,7},{5,4},{6,5},{7,6},{8,11},{9,8},{10,9... | collective-permute-start | bytes 3145736 | tf_op jit(solution)/shard_map/ppermute | solution.py:331
  3.9 19.4 %collective-permute-start.6 = (f32[2,2,256,256]{3,2,1,0:T(8,128)S(1)}, f32[2,2,256,256]{3,2,1,0:T(8,128)S(1)}, u32[]{:S(2)}, u32[]{:S(2)}) collective-permute-start(f32[2,2,256,256]{3,2,1,0:T(8,128)S(1)} %collective-permute-done.5.own.refs_3_), channel_id=1, source_target_pairs={{0,60},{1,61},{2,62},{3,63},{4,0},{5,1},{6,2},{7,3},{8,4},{9,5},{1... | collective-permute-start | bytes 3145736 | tf_op jit(solution)/shard_map/ppermute | solution.py:331
  6.8 10.0 %collective-permute-start.1 = (s32[4]{0:T(128)S(1)}, s32[4]{0:T(128)S(1)}, u32[]{:S(2)}, u32[]{:S(2)}) collective-permute-start(s32[4]{0:T(128)S(1)} %pad_add_fusion.spot), channel_id=1, source_target_pairs={{0,1},{1,2},{2,3},{3,0},{4,5},{5,6},{6,7},{7,4},{8,9},{9,10},{10,1... | collective-permute-start | bytes 56 | tf_op jit(solution)/shard_map/ppermute | solution.py:331
  8.0 14.5 %collective-permute-start.2 = (s32[4]{0:T(128)S(1)}, s32[4]{0:T(128)S(1)}, u32[]{:S(2)}, u32[]{:S(2)}) collective-permute-start(s32[4]{0:T(128)S(1)} %pad_add_fusion.spot), channel_id=1, source_target_pairs={{0,4},{1,5},{2,6},{3,7},{4,8},{5,9},{6,10},{7,11},{8,12},{9,13},{1... | collective-permute-start | bytes 56 | tf_op jit(solution)/shard_map/ppermute | solution.py:331
  9.3 19.4 %collective-permute-start = (s32[4]{0:T(128)S(1)}, s32[4]{0:T(128)S(1)}, u32[]{:S(2)}, u32[]{:S(2)}) collective-permute-start(s32[4]{0:T(128)S(1)} %pad_add_fusion.spot), channel_id=1, source_target_pairs={{64,69},{65,70},{66,71},{67,68},{68,73},{69,74},{70,75},{71,72},{7... | collective-permute-start | bytes 56 | tf_op jit(solution)/shard_map/ppermute | solution.py:331
  13.1 1.2 %copy-start = (f32[2,2,1,256,256]{4,3,2,1,0:T(8,128)S(1)}, f32[2,2,1,256,256]{4,3,2,1,0:T(8,128)}, u32[]{:S(2)}) copy-start(f32[2,2,1,256,256]{4,3,2,1,0:T(8,128)} %param.6) | copy-start | bytes 3145732
  23.2 2.1 %copy-start.2 = (f32[1,2,256,256]{3,2,1,0:T(8,128)S(1)}, f32[1,2,256,256]{3,2,1,0:T(8,128)}, u32[]{:S(2)}) copy-start(f32[1,2,256,256]{3,2,1,0:T(8,128)} %param.9) | copy-start | bytes 1572868
  23.2 17.0 %collective-permute-start.4 = (f32[2,2,256,256]{3,2,1,0:T(8,128)S(1)}, f32[2,2,256,256]{3,2,1,0:T(8,128)S(1)}, u32[]{:S(2)}, u32[]{:S(2)}) collective-permute-start(f32[2,2,256,256]{3,2,1,0:T(8,128)S(1)} %shard_map.65), channel_id=1, source_target_pairs={{0,60},{1,61},{2,62},{3,63},{4,0},{5,1},{6,2},{7,3},{8,4},{9,5},{1... | collective-permute-start | bytes 3145736 | tf_op jit(solution)/shard_map/ppermute | solution.py:331
  23.3 4.1 %copy-start.3 = (f32[2,31]{1,0:T(2,128)S(1)}, f32[2,31]{1,0:T(2,128)}, u32[]{:S(2)}) copy-start(f32[2,31]{1,0:T(2,128)} %param.8) | copy-start | bytes 748
  23.9 16.3 %copy-start.1 = (f32[2,256,256]{2,1,0:T(8,128)S(1)}, f32[2,256,256]{2,1,0:T(8,128)}, u32[]{:S(2)}) copy-start(f32[2,256,256]{2,1,0:T(8,128)} %refs_6_.1) | copy-start | bytes 1572868
  24.0 16.3 %collective-permute-start.7 = (f32[2,2,256,256]{3,2,1,0:T(8,128)S(1)}, f32[2,2,256,256]{3,2,1,0:T(8,128)S(1)}, u32[]{:S(2)}, u32[]{:S(2)}) collective-permute-start(f32[2,2,256,256]{3,2,1,0:T(8,128)S(1)} %shard_map.66), channel_id=1, source_target_pairs={{0,3},{1,0},{2,1},{3,2},{4,7},{5,4},{6,5},{7,6},{8,11},{9,8},{10,9... | collective-permute-start | bytes 3145736 | tf_op jit(solution)/shard_map/ppermute | solution.py:331
  25.3 20.9 %collective-permute-start.8 = (f32[256,256]{1,0:T(8,128)S(1)}, f32[256,256]{1,0:T(8,128)S(1)}, u32[]{:S(2)}, u32[]{:S(2)}) collective-permute-start(f32[256,256]{1,0:T(8,128)S(1)} %get-tuple-element.49), channel_id=1, source_target_pairs={{64,69},{65,70},{66,71},{67,68},{68,73},{69,74},{70,75},{71,72},{7... | collective-permute-start | bytes 786440 | tf_op jit(solution)/shard_map/ppermute | solution.py:331
  51.6 8.9 %collective-permute-start.14 = (f32[2,256,256]{2,1,0:T(8,128)S(1)}, f32[2,256,256]{2,1,0:T(8,128)S(1)}, u32[]{:S(2)}, u32[]{:S(2)}) collective-permute-start(f32[2,256,256]{2,1,0:T(8,128)S(1)} %get-tuple-element.43), channel_id=1, source_target_pairs={{0,4},{1,5},{2,6},{3,7},{4,8},{5,9},{6,10},{7,11},{8,12},{9,13},{1... | collective-permute-start | bytes 1572872 | tf_op jit(solution)/shard_map/ppermute | solution.py:331
  54.4 11.7 %collective-permute-start.15 = (f32[2,256,256]{2,1,0:T(8,128)S(1)}, f32[2,256,256]{2,1,0:T(8,128)S(1)}, u32[]{:S(2)}, u32[]{:S(2)}) collective-permute-start(f32[2,256,256]{2,1,0:T(8,128)S(1)} %get-tuple-element.44), channel_id=1, source_target_pairs={{0,4},{1,5},{2,6},{3,7},{4,8},{5,9},{6,10},{7,11},{8,12},{9,13},{1... | collective-permute-start | bytes 1572872 | tf_op jit(solution)/shard_map/ppermute | solution.py:331
  54.6 19.5 %collective-permute-start.9 = (f32[2,256,256]{2,1,0:T(8,128)S(1)}, f32[2,256,256]{2,1,0:T(8,128)S(1)}, u32[]{:S(2)}, u32[]{:S(2)}) collective-permute-start(f32[2,256,256]{2,1,0:T(8,128)S(1)} %get-tuple-element.37), channel_id=1, source_target_pairs={{0,1},{1,2},{2,3},{3,0},{4,5},{5,6},{6,7},{7,4},{8,9},{9,10},{10,1... | collective-permute-start | bytes 1572872 | tf_op jit(solution)/shard_map/ppermute | solution.py:331
  56.1 18.0 %collective-permute-start.10 = (f32[2,256,256]{2,1,0:T(8,128)S(1)}, f32[2,256,256]{2,1,0:T(8,128)S(1)}, u32[]{:S(2)}, u32[]{:S(2)}) collective-permute-start(f32[2,256,256]{2,1,0:T(8,128)S(1)} %get-tuple-element.38), channel_id=1, source_target_pairs={{0,1},{1,2},{2,3},{3,0},{4,5},{5,6},{6,7},{7,4},{8,9},{9,10},{10,1... | collective-permute-start | bytes 1572872 | tf_op jit(solution)/shard_map/ppermute | solution.py:331
  67.0 9.7 %collective-permute-start.16 = (f32[2,256,256]{2,1,0:T(8,128)S(1)}, f32[2,256,256]{2,1,0:T(8,128)S(1)}, u32[]{:S(2)}, u32[]{:S(2)}) collective-permute-start(f32[2,256,256]{2,1,0:T(8,128)S(1)} %get-tuple-element.46), channel_id=1, source_target_pairs={{0,64},{1,65},{2,66},{3,67},{4,68},{5,69},{6,70},{7,71},{8,72},{9,... | collective-permute-start | bytes 1572872 | tf_op jit(solution)/shard_map/ppermute | solution.py:331
  70.6 10.0 %collective-permute-start.17 = (f32[2,256,256]{2,1,0:T(8,128)S(1)}, f32[2,256,256]{2,1,0:T(8,128)S(1)}, u32[]{:S(2)}, u32[]{:S(2)}) collective-permute-start(f32[2,256,256]{2,1,0:T(8,128)S(1)} %get-tuple-element.47), channel_id=1, source_target_pairs={{0,1},{1,2},{2,3},{3,0},{4,5},{5,6},{6,7},{7,4},{8,9},{9,10},{10,1... | collective-permute-start | bytes 1572872 | tf_op jit(solution)/shard_map/ppermute | solution.py:331
  74.0 12.7 %collective-permute-start.18 = (f32[2,256,256]{2,1,0:T(8,128)S(1)}, f32[2,256,256]{2,1,0:T(8,128)S(1)}, u32[]{:S(2)}, u32[]{:S(2)}) collective-permute-start(f32[2,256,256]{2,1,0:T(8,128)S(1)} %get-tuple-element.48), channel_id=1, source_target_pairs={{0,65},{1,66},{2,67},{3,64},{4,69},{5,70},{6,71},{7,68},{8,73},{9,... | collective-permute-start | bytes 1572872 | tf_op jit(solution)/shard_map/ppermute | solution.py:331
  75.0 11.8 %collective-permute-start.11 = (f32[2,256,256]{2,1,0:T(8,128)S(1)}, f32[2,256,256]{2,1,0:T(8,128)S(1)}, u32[]{:S(2)}, u32[]{:S(2)}) collective-permute-start(f32[2,256,256]{2,1,0:T(8,128)S(1)} %get-tuple-element.40), channel_id=1, source_target_pairs={{0,64},{1,65},{2,66},{3,67},{4,68},{5,69},{6,70},{7,71},{8,72},{9,... | collective-permute-start | bytes 1572872 | tf_op jit(solution)/shard_map/ppermute | solution.py:331
  75.1 11.7 %collective-permute-start.12 = (f32[2,256,256]{2,1,0:T(8,128)S(1)}, f32[2,256,256]{2,1,0:T(8,128)S(1)}, u32[]{:S(2)}, u32[]{:S(2)}) collective-permute-start(f32[2,256,256]{2,1,0:T(8,128)S(1)} %get-tuple-element.41), channel_id=1, source_target_pairs={{0,4},{1,5},{2,6},{3,7},{4,8},{5,9},{6,10},{7,11},{8,12},{9,13},{1... | collective-permute-start | bytes 1572872 | tf_op jit(solution)/shard_map/ppermute | solution.py:331
  76.8 16.3 %collective-permute-start.13 = (f32[2,256,256]{2,1,0:T(8,128)S(1)}, f32[2,256,256]{2,1,0:T(8,128)S(1)}, u32[]{:S(2)}, u32[]{:S(2)}) collective-permute-start(f32[2,256,256]{2,1,0:T(8,128)S(1)} %get-tuple-element.42), channel_id=1, source_target_pairs={{0,68},{1,69},{2,70},{3,71},{4,72},{5,73},{6,74},{7,75},{8,76},{9,... | collective-permute-start | bytes 1572872 | tf_op jit(solution)/shard_map/ppermute | solution.py:331

commit v5 on v4

--- a/solution.py
+++ b/solution.py
@@ -245,13 +245,13 @@
 STATE = jax.ShapeDtypeStruct((2, 2 * N, N), BF)
 
 
-def call(kernel, outs, spot, args, scratch=()):
+def call(kernel, outs, spot, args, scratch=(), where=VS):
     room = (12 if scratch else 6) << 20
     return pl.pallas_call(
         kernel,
         out_shape=outs,
         in_specs=[SS] + [VS] * len(args),
-        out_specs=[VS] * len(outs),
+        out_specs=[where] * len(outs),
         scratch_shapes=list(scratch),
         compiler_params=pltpu.CompilerParams(vmem_limit_bytes=room),
     )(spot, *args)
@@ -299,12 +299,17 @@
 
 
 def final_kernel(spot, *refs):
-    out = refs[8]
+    out, buffer, done = refs[8], refs[9], refs[10]
+    copies = []
     for q in range(2):
         for c in range(2):
             for sl, _, _ in chunks():
                 a, b, x, y = (refs[4 * c + i][q, sl] for i in range(4))
-                out[q, c, sl] = (a + b) + (x + y)
+                buffer[q, c, sl] = (a + b) + (x + y)
+            copies.append(pltpu.make_async_copy(buffer.at[q, c], out.at[q, c], done.at[2 * q + c]))
+            copies[-1].start()
+    for copy in copies:
+        copy.wait()
 
 
 def moved(t, dx, dy):
@@ -382,7 +387,8 @@
         )
         way = 1 - channel
         parts += [stay, permute(leaving, SWAP), permute(straight, SCATTER[way]), permute(cross, CROSSED[way])]
-    out, = call(final_kernel, [PAIR], here, parts)
+    scratch = [pltpu.VMEM((2, 2, N, N), F32), pltpu.SemaphoreType.DMA((4,))]
+    out, = call(final_kernel, [PAIR], here, parts, scratch, pl.BlockSpec(memory_space=pl.ANY))
     return out[:, :, None]
 
 

time: 95 us -> 95 us (level)
  no operation moved by 1% of the time
where the time goes in v5:
time: 95 us; the launch traced here: 94.8 us
  waiting for transfers between devices  40.1 us (42%)
  starting transfers between devices  31.5 us (33%)
  Pallas kernels  18.7 us (20%)
  other arithmetic  2.16 us (2%)
  local copies, waits for them, and re-layouts  1.35 us (1%)
  between operations  1.02 us (1%)
    ppermute x19, waiting for transfers between devices, permute(): return lax.ppermute(block, ('depth', 'tiles'), pairs)  40.1 us
    ppermute x19, starting transfers between devices, permute(): return lax.ppermute(block, ('depth', 'tiles'), pairs)  31.5 us
    pallas_call x9, Pallas kernels, call(): pl.pallas_call(kernel, out_shape=outs, in_specs=[SS] + [VS] * len(args),...  16 us
    pallas_call x1, Pallas kernels, tables(): pl.pallas_call(tables_kernel, out_shape=[jax.ShapeDtypeStruct((4, 2 * N,...  2.7 us
  transfers between devices with their start and end apart: 19, of which 9 were waited for; matrix products, arithmetic and copies ran while one was open for 2% of the time, Pallas kernels for 12%

profile of v5, /device:TPU:1, one launch (start us, length us, event | category | flops | bytes accessed | tf_op | source)
XLA Modules:
  0.0 94.8 jit_solution(16037298798351631615)
XLA Ops:
  0.0 1.4 %collective-permute-start.5 = (f32[2,2,256,256]{3,2,1,0:T(8,128)}, f32[2,2,256,256]{3,2,1,0:T(8,128)S(1)}, u32[]{:S(2)}, u32[]{:S(2)}) collective-permute-start(f32[2,2,256,256]{3,2,1,0:T(8,128)} %bitcast.14), channel_id=1, source_target_pairs={{0,64},{1,65},{2,66},{3,67},{4,68},{5,69},{6,70},{7,71},{8,72},{9,... | collective-permute-start | bytes 3145736 | tf_op jit(solution)/shard_map/ppermute | solution.py:336
  1.4 1.3 %collective-permute-start.3 = (f32[2,2,256,256]{3,2,1,0:T(8,128)}, f32[2,2,256,256]{3,2,1,0:T(8,128)S(1)}, u32[]{:S(2)}, u32[]{:S(2)}) collective-permute-start(f32[2,2,256,256]{3,2,1,0:T(8,128)} %bitcast.15), channel_id=1, source_target_pairs={{0,3},{1,0},{2,1},{3,2},{4,7},{5,4},{6,5},{7,6},{8,11},{9,8},{10,9... | collective-permute-start | bytes 3145736 | tf_op jit(solution)/shard_map/ppermute | solution.py:336
  2.7 1.2 %collective-permute-done.5.own.refs_3_ = f32[2,2,256,256]{3,2,1,0:T(8,128)S(1)} collective-permute-done((f32[2,2,256,256]{3,2,1,0:T(8,128)}, f32[2,2,256,256]{3,2,1,0:T(8,128)S(1)}, u32[]{:S(2)}, u32[]{:S(2)}) %collective-permute-start.5) | collective-permute-done | bytes 1048608 | tf_op jit(solution)/shard_map/ppermute | solution.py:336
  3.9 1.4 %collective-permute-start.6 = (f32[2,2,256,256]{3,2,1,0:T(8,128)S(1)}, f32[2,2,256,256]{3,2,1,0:T(8,128)S(1)}, u32[]{:S(2)}, u32[]{:S(2)}) collective-permute-start(f32[2,2,256,256]{3,2,1,0:T(8,128)S(1)} %collective-permute-done.5.own.refs_3_), channel_id=1, source_target_pairs={{0,60},{1,61},{2,62},{3,63},{4,0},{5,1},{6,2},{7,3},{8,4},{9,5},{1... | collective-permute-start | bytes 3145736 | tf_op jit(solution)/shard_map/ppermute | solution.py:336
  5.9 0.8 fusion.6
  6.7 0.1 pad_add_fusion.spot
  6.8 1.2 %collective-permute-start.1 = (s32[4]{0:T(128)S(1)}, s32[4]{0:T(128)S(1)}, u32[]{:S(2)}, u32[]{:S(2)}) collective-permute-start(s32[4]{0:T(128)S(1)} %pad_add_fusion.spot), channel_id=1, source_target_pairs={{0,1},{1,2},{2,3},{3,0},{4,5},{5,6},{6,7},{7,4},{8,9},{9,10},{10,1... | collective-permute-start | bytes 56 | tf_op jit(solution)/shard_map/ppermute | solution.py:336
  8.0 1.3 %collective-permute-start.2 = (s32[4]{0:T(128)S(1)}, s32[4]{0:T(128)S(1)}, u32[]{:S(2)}, u32[]{:S(2)}) collective-permute-start(s32[4]{0:T(128)S(1)} %pad_add_fusion.spot), channel_id=1, source_target_pairs={{0,4},{1,5},{2,6},{3,7},{4,8},{5,9},{6,10},{7,11},{8,12},{9,13},{1... | collective-permute-start | bytes 56 | tf_op jit(solution)/shard_map/ppermute | solution.py:336
  9.3 3.8 %collective-permute-start = (s32[4]{0:T(128)S(1)}, s32[4]{0:T(128)S(1)}, u32[]{:S(2)}, u32[]{:S(2)}) collective-permute-start(s32[4]{0:T(128)S(1)} %pad_add_fusion.spot), channel_id=1, source_target_pairs={{64,69},{65,70},{66,71},{67,68},{68,73},{69,74},{70,75},{71,72},{7... | collective-permute-start | bytes 56 | tf_op jit(solution)/shard_map/ppermute | solution.py:336
  13.1 0.0 copy-start
  13.1 1.2 %copy-done = f32[2,2,1,256,256]{4,3,2,1,0:T(8,128)S(1)} copy-done((f32[2,2,1,256,256]{4,3,2,1,0:T(8,128)S(1)}, f32[2,2,1,256,256]{4,3,2,1,0:T(8,128)}, u32[]{:S(2)}) %copy-start) | copy-done | bytes 1048600
  14.4 0.6 shard_map.64.own.refs_0_
  15.0 1.8 %collective-permute-done.1 = s32[4]{0:T(128)S(1)} collective-permute-done((s32[4]{0:T(128)S(1)}, s32[4]{0:T(128)S(1)}, u32[]{:S(2)}, u32[]{:S(2)}) %collective-permute-start.1) | collective-permute-done | bytes 48 | tf_op jit(solution)/shard_map/ppermute | solution.py:336
  16.7 5.7 %collective-permute-done.2 = s32[4]{0:T(128)S(1)} collective-permute-done((s32[4]{0:T(128)S(1)}, s32[4]{0:T(128)S(1)}, u32[]{:S(2)}, u32[]{:S(2)}) %collective-permute-start.2) | collective-permute-done | bytes 48 | tf_op jit(solution)/shard_map/ppermute | solution.py:336
  22.5 0.0 collective-permute-done.3.near.refs_1_
  22.5 0.7 shard_map.65
  23.2 0.0 copy-start.2
  23.2 0.1 collective-permute-start.4
  23.3 0.0 collective-permute-done.6.near.refs_4_
  23.3 0.0 copy-start.3
  23.3 0.7 shard_map.66
  23.9 0.0 copy-start.1
  24.0 1.3 %collective-permute-start.7 = (f32[2,2,256,256]{3,2,1,0:T(8,128)S(1)}, f32[2,2,256,256]{3,2,1,0:T(8,128)S(1)}, u32[]{:S(2)}, u32[]{:S(2)}) collective-permute-start(f32[2,2,256,256]{3,2,1,0:T(8,128)S(1)} %shard_map.66), channel_id=1, source_target_pairs={{0,3},{1,0},{2,1},{3,2},{4,7},{5,4},{6,5},{7,6},{8,11},{9,8},{10,9... | collective-permute-start | bytes 3145736 | tf_op jit(solution)/shard_map/ppermute | solution.py:336
  25.2 0.0 copy-done.2
  25.3 2.1 %collective-permute-start.8 = (f32[256,256]{1,0:T(8,128)S(1)}, f32[256,256]{1,0:T(8,128)S(1)}, u32[]{:S(2)}, u32[]{:S(2)}) collective-permute-start(f32[256,256]{1,0:T(8,128)S(1)} %get-tuple-element.49), channel_id=1, source_target_pairs={{64,69},{65,70},{66,71},{67,68},{68,73},{69,74},{70,75},{71,72},{7... | collective-permute-start | bytes 786440 | tf_op jit(solution)/shard_map/ppermute | solution.py:336
  27.4 0.0 copy-done.3
  27.4 0.1 pad_slice_fusion.1
  27.5 1.1 %negate_multiply_fusion = (f32[1,256,256]{2,1,0:T(8,128)S(1)}, f32[1,256,256]{2,1,0:T(8,128)S(1)}) fusion(), kind=kLoop, calls=%fused_computation.9 | loop fusion | flops 1114112 | bytes 524288 | tf_op jit(solution)/shard_map/mul | solution.py:344
  28.6 0.1 pad_maximum_fusion.1.taps
  28.7 0.0 collective-permute-done
  28.7 0.1 broadcast_select_fusion.3.spot
  28.7 2.7 %tables.1 = (bf16[4,512,512]{2,1,0:T(8,128)(2,1)S(1)}, bf16[4,512,512]{2,1,0:T(8,128)(2,1)S(1)}, bf16[4,512,256]{2,1,0:T(8,128)(2,1)S(1)}, bf16[4,512,256]{2,1,0:T(8,128)(2,1)S(1)}) custom-call(s32[4]{0:T(128)S(1)} %broadcast_select_fusion.3.spot, f32[8,256]{1,0:T(8,128)S(1)} %pad_maximum_fusion.1.taps, f32[2,256,256]{2,1,0:T(8,128)S(1)} %pad_maximum_fusion.dft), custom_call_target="tpu_custom_call" | custom-call | tf_op jit(solution)/shard_map/tables/pallas_call | solution.py:97
  31.5 8.8 %collective-permute-done.4.refs_2_ = f32[2,2,256,256]{3,2,1,0:T(8,128)S(1)} collective-permute-done((f32[2,2,256,256]{3,2,1,0:T(8,128)S(1)}, f32[2,2,256,256]{3,2,1,0:T(8,128)S(1)}, u32[]{:S(2)}, u32[]{:S(2)}) %collective-permute-start.4) | collective-permute-done | bytes 1048608 | tf_op jit(solution)/shard_map/ppermute | solution.py:336
  40.2 0.0 collective-permute-done.7.refs_5_
  40.2 0.0 copy-done.1
  40.2 5.2 %shard_map.67 = (f32[4,2,256,256]{3,2,1,0:T(8,128)S(1)}, f32[4,2,256,256]{3,2,1,0:T(8,128)S(1)}, f32[2,256,256]{2,1,0:T(8,128)S(1)}) custom-call(s32[4]{0:T(128)S(1)} %broadcast_select_fusion.3.spot, f32[2,2,256,256]{3,2,1,0:T(8,128)S(1)} %shard_map.64.own.refs_0_, f32[2,2,256,256]{3,2,1,0:T(8,128)S(1)} %collective-permute-done.3.near.refs_1_, ...), custom_call_target="tpu_custom_call" | custom-call | tf_op jit(solution)/shard_map/pallas_call | solution.py:250
  45.4 0.7 collective-permute-done.8.refs_2_
  46.2 2.8 %shard_map.68 = (f32[2,2,256,256]{3,2,1,0:T(8,128)S(1)}, f32[2,256,256]{2,1,0:T(8,128)S(1)}, f32[2,256,256]{2,1,0:T(8,128)S(1)}, bf16[2,512,256]{2,1,0:T(8,128)(2,1)S(1)}) custom-call(s32[4]{0:T(128)S(1)} %broadcast_select_fusion.3.spot, f32[2,256,256]{2,1,0:T(8,128)S(1)} %get-tuple-element.31.refs_0_, f32[256,256]{1,0:T(8,128)S(1)} %get-tuple-element.50.refs_1_, ...), custom_call_target="tpu_custom_call" | custom-call | tf_op jit(solution)/shard_map/pallas_call | solution.py:250
  49.0 2.6 %shard_map.69 = (f32[2,2,256,256]{3,2,1,0:T(8,128)S(1)}, f32[2,256,256]{2,1,0:T(8,128)S(1)}, f32[2,256,256]{2,1,0:T(8,128)S(1)}) custom-call(s32[4]{0:T(128)S(1)} %broadcast_select_fusion.3.spot, bf16[2,512,256]{2,1,0:T(8,128)(2,1)S(1)} %get-tuple-element.34.refs_0_, f32[4,2,256,256]{3,2,1,0:T(8,128)S(1)} %get-tuple-element.32.refs_3_.refs_1_, ...), custom_call_target="tpu_custom_call" | custom-call | tf_op jit(solution)/shard_map/pallas_call | solution.py:250
  51.6 2.8 %collective-permute-start.14 = (f32[2,256,256]{2,1,0:T(8,128)S(1)}, f32[2,256,256]{2,1,0:T(8,128)S(1)}, u32[]{:S(2)}, u32[]{:S(2)}) collective-permute-start(f32[2,256,256]{2,1,0:T(8,128)S(1)} %get-tuple-element.43), channel_id=1, source_target_pairs={{0,4},{1,5},{2,6},{3,7},{4,8},{5,9},{6,10},{7,11},{8,12},{9,13},{1... | collective-permute-start | bytes 1572872 | tf_op jit(solution)/shard_map/ppermute | solution.py:336
  54.4 0.1 collective-permute-start.15
  54.5 0.1 pad_add_fusion.2
  54.6 1.6 %collective-permute-start.9 = (f32[2,256,256]{2,1,0:T(8,128)S(1)}, f32[2,256,256]{2,1,0:T(8,128)S(1)}, u32[]{:S(2)}, u32[]{:S(2)}) collective-permute-start(f32[2,256,256]{2,1,0:T(8,128)S(1)} %get-tuple-element.37), channel_id=1, source_target_pairs={{0,1},{1,2},{2,3},{3,0},{4,5},{5,6},{6,7},{7,4},{8,9},{9,10},{10,1... | collective-permute-start | bytes 1572872 | tf_op jit(solution)/shard_map/ppermute | solution.py:336
  56.1 0.6 collective-permute-start.10
  56.7 3.9 %collective-permute-done.14.refs_2_ = f32[2,256,256]{2,1,0:T(8,128)S(1)} collective-permute-done((f32[2,256,256]{2,1,0:T(8,128)S(1)}, f32[2,256,256]{2,1,0:T(8,128)S(1)}, u32[]{:S(2)}, u32[]{:S(2)}) %collective-permute-start.14) | collective-permute-done | bytes 524320 | tf_op jit(solution)/shard_map/ppermute | solution.py:336
  60.5 5.6 %collective-permute-done.15.refs_3_ = f32[2,256,256]{2,1,0:T(8,128)S(1)} collective-permute-done((f32[2,256,256]{2,1,0:T(8,128)S(1)}, f32[2,256,256]{2,1,0:T(8,128)S(1)}, u32[]{:S(2)}, u32[]{:S(2)}) %collective-permute-start.15) | collective-permute-done | bytes 524320 | tf_op jit(solution)/shard_map/ppermute | solution.py:336
  66.2 0.9 shard_map.71
  67.0 3.6 %collective-permute-start.16 = (f32[2,256,256]{2,1,0:T(8,128)S(1)}, f32[2,256,256]{2,1,0:T(8,128)S(1)}, u32[]{:S(2)}, u32[]{:S(2)}) collective-permute-start(f32[2,256,256]{2,1,0:T(8,128)S(1)} %get-tuple-element.46), channel_id=1, source_target_pairs={{0,64},{1,65},{2,66},{3,67},{4,68},{5,69},{6,70},{7,71},{8,72},{9,... | collective-permute-start | bytes 1572872 | tf_op jit(solution)/shard_map/ppermute | solution.py:336
  70.6 3.4 %collective-permute-start.17 = (f32[2,256,256]{2,1,0:T(8,128)S(1)}, f32[2,256,256]{2,1,0:T(8,128)S(1)}, u32[]{:S(2)}, u32[]{:S(2)}) collective-permute-start(f32[2,256,256]{2,1,0:T(8,128)S(1)} %get-tuple-element.47), channel_id=1, source_target_pairs={{0,1},{1,2},{2,3},{3,0},{4,5},{5,6},{6,7},{7,4},{8,9},{9,10},{10,1... | collective-permute-start | bytes 1572872 | tf_op jit(solution)/shard_map/ppermute | solution.py:336
  74.0 0.1 collective-permute-start.18
  74.1 0.0 collective-permute-done.9.refs_2_
  74.1 0.0 collective-permute-done.10.refs_3_
  74.1 0.9 shard_map.70
  75.0 0.1 collective-permute-start.11
  75.1 1.7 %collective-permute-start.12 = (f32[2,256,256]{2,1,0:T(8,128)S(1)}, f32[2,256,256]{2,1,0:T(8,128)S(1)}, u32[]{:S(2)}, u32[]{:S(2)}) collective-permute-start(f32[2,256,256]{2,1,0:T(8,128)S(1)} %get-tuple-element.41), channel_id=1, source_target_pairs={{0,4},{1,5},{2,6},{3,7},{4,8},{5,9},{6,10},{7,11},{8,12},{9,13},{1... | collective-permute-start | bytes 1572872 | tf_op jit(solution)/shard_map/ppermute | solution.py:336
  76.8 0.0 collective-permute-done.16.refs_5_
  76.8 3.8 %collective-permute-start.13 = (f32[2,256,256]{2,1,0:T(8,128)S(1)}, f32[2,256,256]{2,1,0:T(8,128)S(1)}, u32[]{:S(2)}, u32[]{:S(2)}) collective-permute-start(f32[2,256,256]{2,1,0:T(8,128)S(1)} %get-tuple-element.42), channel_id=1, source_target_pairs={{0,68},{1,69},{2,70},{3,71},{4,72},{5,73},{6,74},{7,75},{8,76},{9,... | collective-permute-start | bytes 1572872 | tf_op jit(solution)/shard_map/ppermute | solution.py:336
  80.6 0.0 collective-permute-done.17.refs_6_
  80.6 6.2 %collective-permute-done.18.refs_7_ = f32[2,256,256]{2,1,0:T(8,128)S(1)} collective-permute-done((f32[2,256,256]{2,1,0:T(8,128)S(1)}, f32[2,256,256]{2,1,0:T(8,128)S(1)}, u32[]{:S(2)}, u32[]{:S(2)}) %collective-permute-start.18) | collective-permute-done | bytes 524320 | tf_op jit(solution)/shard_map/ppermute | solution.py:336
  86.8 0.0 collective-permute-done.11.refs_1_
  86.8 0.0 collective-permute-done.12.refs_2_
  86.8 6.2 %collective-permute-done.13.refs_3_ = f32[2,256,256]{2,1,0:T(8,128)S(1)} collective-permute-done((f32[2,256,256]{2,1,0:T(8,128)S(1)}, f32[2,256,256]{2,1,0:T(8,128)S(1)}, u32[]{:S(2)}, u32[]{:S(2)}) %collective-permute-start.13) | collective-permute-done | bytes 524320 | tf_op jit(solution)/shard_map/ppermute | solution.py:336
  93.0 1.6 %shard_map.72 = f32[2,2,256,256]{3,2,1,0:T(8,128)} custom-call(s32[4]{0:T(128)S(1)} %broadcast_select_fusion.3.spot, f32[2,256,256]{2,1,0:T(8,128)S(1)} %get-tuple-element.39.refs_0_, f32[2,256,256]{2,1,0:T(8,128)S(1)} %collective-permute-done.11.refs_1_, f32[2,256,256]{2,1,0:T(8,128)S(1)} %collective-permute-done.12.refs_2_, ...), custom_call_target="tpu_custom_call" | custom-call | tf_op jit(solution)/shard_map/pallas_call | solution.py:250
  (4 shorter events, 0.1 us)
Async XLA Ops:
  0.0 3.9 %collective-permute-start.5 = (f32[2,2,256,256]{3,2,1,0:T(8,128)}, f32[2,2,256,256]{3,2,1,0:T(8,128)S(1)}, u32[]{:S(2)}, u32[]{:S(2)}) collective-permute-start(f32[2,2,256,256]{3,2,1,0:T(8,128)} %bitcast.14), channel_id=1, source_target_pairs={{0,64},{1,65},{2,66},{3,67},{4,68},{5,69},{6,70},{7,71},{8,72},{9,... | collective-permute-start | bytes 3145736 | tf_op jit(solution)/shard_map/ppermute | solution.py:336
  1.4 21.1 %collective-permute-start.3 = (f32[2,2,256,256]{3,2,1,0:T(8,128)}, f32[2,2,256,256]{3,2,1,0:T(8,128)S(1)}, u32[]{:S(2)}, u32[]{:S(2)}) collective-permute-start(f32[2,2,256,256]{3,2,1,0:T(8,128)} %bitcast.15), channel_id=1, source_target_pairs={{0,3},{1,0},{2,1},{3,2},{4,7},{5,4},{6,5},{7,6},{8,11},{9,8},{10,9... | collective-permute-start | bytes 3145736 | tf_op jit(solution)/shard_map/ppermute | solution.py:336
  3.9 19.4 %collective-permute-start.6 = (f32[2,2,256,256]{3,2,1,0:T(8,128)S(1)}, f32[2,2,256,256]{3,2,1,0:T(8,128)S(1)}, u32[]{:S(2)}, u32[]{:S(2)}) collective-permute-start(f32[2,2,256,256]{3,2,1,0:T(8,128)S(1)} %collective-permute-done.5.own.refs_3_), channel_id=1, source_target_pairs={{0,60},{1,61},{2,62},{3,63},{4,0},{5,1},{6,2},{7,3},{8,4},{9,5},{1... | collective-permute-start | bytes 3145736 | tf_op jit(solution)/shard_map/ppermute | solution.py:336
  6.8 10.0 %collective-permute-start.1 = (s32[4]{0:T(128)S(1)}, s32[4]{0:T(128)S(1)}, u32[]{:S(2)}, u32[]{:S(2)}) collective-permute-start(s32[4]{0:T(128)S(1)} %pad_add_fusion.spot), channel_id=1, source_target_pairs={{0,1},{1,2},{2,3},{3,0},{4,5},{5,6},{6,7},{7,4},{8,9},{9,10},{10,1... | collective-permute-start | bytes 56 | tf_op jit(solution)/shard_map/ppermute | solution.py:336
  8.0 14.5 %collective-permute-start.2 = (s32[4]{0:T(128)S(1)}, s32[4]{0:T(128)S(1)}, u32[]{:S(2)}, u32[]{:S(2)}) collective-permute-start(s32[4]{0:T(128)S(1)} %pad_add_fusion.spot), channel_id=1, source_target_pairs={{0,4},{1,5},{2,6},{3,7},{4,8},{5,9},{6,10},{7,11},{8,12},{9,13},{1... | collective-permute-start | bytes 56 | tf_op jit(solution)/shard_map/ppermute | solution.py:336
  9.3 19.4 %collective-permute-start = (s32[4]{0:T(128)S(1)}, s32[4]{0:T(128)S(1)}, u32[]{:S(2)}, u32[]{:S(2)}) collective-permute-start(s32[4]{0:T(128)S(1)} %pad_add_fusion.spot), channel_id=1, source_target_pairs={{64,69},{65,70},{66,71},{67,68},{68,73},{69,74},{70,75},{71,72},{7... | collective-permute-start | bytes 56 | tf_op jit(solution)/shard_map/ppermute | solution.py:336
  13.1 1.2 %copy-start = (f32[2,2,1,256,256]{4,3,2,1,0:T(8,128)S(1)}, f32[2,2,1,256,256]{4,3,2,1,0:T(8,128)}, u32[]{:S(2)}) copy-start(f32[2,2,1,256,256]{4,3,2,1,0:T(8,128)} %param.6) | copy-start | bytes 3145732
  23.2 2.1 %copy-start.2 = (f32[1,2,256,256]{3,2,1,0:T(8,128)S(1)}, f32[1,2,256,256]{3,2,1,0:T(8,128)}, u32[]{:S(2)}) copy-start(f32[1,2,256,256]{3,2,1,0:T(8,128)} %param.9) | copy-start | bytes 1572868
  23.2 17.0 %collective-permute-start.4 = (f32[2,2,256,256]{3,2,1,0:T(8,128)S(1)}, f32[2,2,256,256]{3,2,1,0:T(8,128)S(1)}, u32[]{:S(2)}, u32[]{:S(2)}) collective-permute-start(f32[2,2,256,256]{3,2,1,0:T(8,128)S(1)} %shard_map.65), channel_id=1, source_target_pairs={{0,60},{1,61},{2,62},{3,63},{4,0},{5,1},{6,2},{7,3},{8,4},{9,5},{1... | collective-permute-start | bytes 3145736 | tf_op jit(solution)/shard_map/ppermute | solution.py:336
  23.3 4.1 %copy-start.3 = (f32[2,31]{1,0:T(2,128)S(1)}, f32[2,31]{1,0:T(2,128)}, u32[]{:S(2)}) copy-start(f32[2,31]{1,0:T(2,128)} %param.8) | copy-start | bytes 748
  23.9 16.3 %copy-start.1 = (f32[2,256,256]{2,1,0:T(8,128)S(1)}, f32[2,256,256]{2,1,0:T(8,128)}, u32[]{:S(2)}) copy-start(f32[2,256,256]{2,1,0:T(8,128)} %refs_6_.1) | copy-start | bytes 1572868
  24.0 16.3 %collective-permute-start.7 = (f32[2,2,256,256]{3,2,1,0:T(8,128)S(1)}, f32[2,2,256,256]{3,2,1,0:T(8,128)S(1)}, u32[]{:S(2)}, u32[]{:S(2)}) collective-permute-start(f32[2,2,256,256]{3,2,1,0:T(8,128)S(1)} %shard_map.66), channel_id=1, source_target_pairs={{0,3},{1,0},{2,1},{3,2},{4,7},{5,4},{6,5},{7,6},{8,11},{9,8},{10,9... | collective-permute-start | bytes 3145736 | tf_op jit(solution)/shard_map/ppermute | solution.py:336
  25.3 20.9 %collective-permute-start.8 = (f32[256,256]{1,0:T(8,128)S(1)}, f32[256,256]{1,0:T(8,128)S(1)}, u32[]{:S(2)}, u32[]{:S(2)}) collective-permute-start(f32[256,256]{1,0:T(8,128)S(1)} %get-tuple-element.49), channel_id=1, source_target_pairs={{64,69},{65,70},{66,71},{67,68},{68,73},{69,74},{70,75},{71,72},{7... | collective-permute-start | bytes 786440 | tf_op jit(solution)/shard_map/ppermute | solution.py:336
  51.6 8.9 %collective-permute-start.14 = (f32[2,256,256]{2,1,0:T(8,128)S(1)}, f32[2,256,256]{2,1,0:T(8,128)S(1)}, u32[]{:S(2)}, u32[]{:S(2)}) collective-permute-start(f32[2,256,256]{2,1,0:T(8,128)S(1)} %get-tuple-element.43), channel_id=1, source_target_pairs={{0,4},{1,5},{2,6},{3,7},{4,8},{5,9},{6,10},{7,11},{8,12},{9,13},{1... | collective-permute-start | bytes 1572872 | tf_op jit(solution)/shard_map/ppermute | solution.py:336
  54.4 11.7 %collective-permute-start.15 = (f32[2,256,256]{2,1,0:T(8,128)S(1)}, f32[2,256,256]{2,1,0:T(8,128)S(1)}, u32[]{:S(2)}, u32[]{:S(2)}) collective-permute-start(f32[2,256,256]{2,1,0:T(8,128)S(1)} %get-tuple-element.44), channel_id=1, source_target_pairs={{0,4},{1,5},{2,6},{3,7},{4,8},{5,9},{6,10},{7,11},{8,12},{9,13},{1... | collective-permute-start | bytes 1572872 | tf_op jit(solution)/shard_map/ppermute | solution.py:336
  54.6 19.5 %collective-permute-start.9 = (f32[2,256,256]{2,1,0:T(8,128)S(1)}, f32[2,256,256]{2,1,0:T(8,128)S(1)}, u32[]{:S(2)}, u32[]{:S(2)}) collective-permute-start(f32[2,256,256]{2,1,0:T(8,128)S(1)} %get-tuple-element.37), channel_id=1, source_target_pairs={{0,1},{1,2},{2,3},{3,0},{4,5},{5,6},{6,7},{7,4},{8,9},{9,10},{10,1... | collective-permute-start | bytes 1572872 | tf_op jit(solution)/shard_map/ppermute | solution.py:336
  56.1 18.0 %collective-permute-start.10 = (f32[2,256,256]{2,1,0:T(8,128)S(1)}, f32[2,256,256]{2,1,0:T(8,128)S(1)}, u32[]{:S(2)}, u32[]{:S(2)}) collective-permute-start(f32[2,256,256]{2,1,0:T(8,128)S(1)} %get-tuple-element.38), channel_id=1, source_target_pairs={{0,1},{1,2},{2,3},{3,0},{4,5},{5,6},{6,7},{7,4},{8,9},{9,10},{10,1... | collective-permute-start | bytes 1572872 | tf_op jit(solution)/shard_map/ppermute | solution.py:336
  67.0 9.7 %collective-permute-start.16 = (f32[2,256,256]{2,1,0:T(8,128)S(1)}, f32[2,256,256]{2,1,0:T(8,128)S(1)}, u32[]{:S(2)}, u32[]{:S(2)}) collective-permute-start(f32[2,256,256]{2,1,0:T(8,128)S(1)} %get-tuple-element.46), channel_id=1, source_target_pairs={{0,64},{1,65},{2,66},{3,67},{4,68},{5,69},{6,70},{7,71},{8,72},{9,... | collective-permute-start | bytes 1572872 | tf_op jit(solution)/shard_map/ppermute | solution.py:336
  70.6 10.0 %collective-permute-start.17 = (f32[2,256,256]{2,1,0:T(8,128)S(1)}, f32[2,256,256]{2,1,0:T(8,128)S(1)}, u32[]{:S(2)}, u32[]{:S(2)}) collective-permute-start(f32[2,256,256]{2,1,0:T(8,128)S(1)} %get-tuple-element.47), channel_id=1, source_target_pairs={{0,1},{1,2},{2,3},{3,0},{4,5},{5,6},{6,7},{7,4},{8,9},{9,10},{10,1... | collective-permute-start | bytes 1572872 | tf_op jit(solution)/shard_map/ppermute | solution.py:336
  74.0 12.7 %collective-permute-start.18 = (f32[2,256,256]{2,1,0:T(8,128)S(1)}, f32[2,256,256]{2,1,0:T(8,128)S(1)}, u32[]{:S(2)}, u32[]{:S(2)}) collective-permute-start(f32[2,256,256]{2,1,0:T(8,128)S(1)} %get-tuple-element.48), channel_id=1, source_target_pairs={{0,65},{1,66},{2,67},{3,64},{4,69},{5,70},{6,71},{7,68},{8,73},{9,... | collective-permute-start | bytes 1572872 | tf_op jit(solution)/shard_map/ppermute | solution.py:336
  75.0 11.8 %collective-permute-start.11 = (f32[2,256,256]{2,1,0:T(8,128)S(1)}, f32[2,256,256]{2,1,0:T(8,128)S(1)}, u32[]{:S(2)}, u32[]{:S(2)}) collective-permute-start(f32[2,256,256]{2,1,0:T(8,128)S(1)} %get-tuple-element.40), channel_id=1, source_target_pairs={{0,64},{1,65},{2,66},{3,67},{4,68},{5,69},{6,70},{7,71},{8,72},{9,... | collective-permute-start | bytes 1572872 | tf_op jit(solution)/shard_map/ppermute | solution.py:336
  75.1 11.7 %collective-permute-start.12 = (f32[2,256,256]{2,1,0:T(8,128)S(1)}, f32[2,256,256]{2,1,0:T(8,128)S(1)}, u32[]{:S(2)}, u32[]{:S(2)}) collective-permute-start(f32[2,256,256]{2,1,0:T(8,128)S(1)} %get-tuple-element.41), channel_id=1, source_target_pairs={{0,4},{1,5},{2,6},{3,7},{4,8},{5,9},{6,10},{7,11},{8,12},{9,13},{1... | collective-permute-start | bytes 1572872 | tf_op jit(solution)/shard_map/ppermute | solution.py:336
  76.8 16.3 %collective-permute-start.13 = (f32[2,256,256]{2,1,0:T(8,128)S(1)}, f32[2,256,256]{2,1,0:T(8,128)S(1)}, u32[]{:S(2)}, u32[]{:S(2)}) collective-permute-start(f32[2,256,256]{2,1,0:T(8,128)S(1)} %get-tuple-element.42), channel_id=1, source_target_pairs={{0,68},{1,69},{2,70},{3,71},{4,72},{5,73},{6,74},{7,75},{8,76},{9,... | collective-permute-start | bytes 1572872 | tf_op jit(solution)/shard_map/ppermute | solution.py:336

commit v6 on v5

--- a/solution.py
+++ b/solution.py
@@ -231,17 +231,19 @@
     save(work, state)
 
 
-def up_kernel(spot, *refs):
+def up_kernel(k, spot, *refs):
     state, waves, patches, tabs = refs[0], refs[1], refs[2], refs[3:7]
     grad, sent_x, sent_y = refs[7:10]
-    work = refs[10:]
+    work = refs[11:] if k > 0 else refs[10:]
     work[0][...] = state[0]
     work[1][...] = state[1]
-    for k in (1, 0):
-        propagate(work, tabs, 1)
-        leave_slice(work, spot, patches.at[k], waves.at[k], grad.at[k], sent_x.at[k], sent_y.at[k], k > 0)
-
-
+    propagate(work, tabs, 1)
+    leave_slice(work, spot, patches.at[k], waves.at[k], grad, sent_x, sent_y, k > 0)
+    if k > 0:
+        save(work, refs[10])
+
+
+PLANE = jax.ShapeDtypeStruct((N, N), F32)
 STATE = jax.ShapeDtypeStruct((2, 2 * N, N), BF)
 
 
@@ -274,7 +276,7 @@
 
 
 def turn_kernel(channel, spots, *refs):
-    grads, came, outs = refs[0:2], refs[2:4], refs[4:8]
+    low, high, came_low, came_high, outs = refs[0:2], refs[2], refs[3:5], refs[5], refs[6:10]
     here = [spots[i] for i in range(3)]
     there = [spots[4 + i] for i in range(3)]
     cols, there_cols = own_cols(here), own_cols(there)
@@ -287,9 +289,8 @@
             first, second, mask = cols, rows, own_rows(there, r0)
         for q in range(2):
             sent, kept = [], []
-            for grad, block in zip(grads, came):
-                g = jnp.where(first, grad[q, channel, sl], 0.0)
-                v = block[q, sl]
+            for grad, v in ((low[q][channel, sl], came_low[q][sl]), (high[q, channel, sl], came_high[q, sl])):
+                g = jnp.where(first, grad, 0.0)
                 sent.append(jnp.where(second, 0.0, g) + jnp.where(mask, 0.0, v))
                 kept.append(jnp.where(second, g, 0.0) + jnp.where(mask, v, 0.0))
             outs[0][q, sl] = jnp.where(upper, sent[1], sent[0])
@@ -298,14 +299,21 @@
             outs[3][q, sl] = jnp.where(upper, kept[0], kept[1])
 
 
+def presum_kernel(spot, *refs):
+    for c in range(2):
+        for q in range(2):
+            for sl, _, _ in chunks():
+                a, b, x = (refs[3 * c + i][q, sl] for i in range(3))
+                refs[6 + c][q, sl] = (a + b) + x
+
+
 def final_kernel(spot, *refs):
-    out, buffer, done = refs[8], refs[9], refs[10]
+    out, buffer, done = refs[4], refs[5], refs[6]
     copies = []
     for q in range(2):
         for c in range(2):
             for sl, _, _ in chunks():
-                a, b, x, y = (refs[4 * c + i][q, sl] for i in range(4))
-                buffer[q, c, sl] = (a + b) + (x + y)
+                buffer[q, c, sl] = refs[c][q, sl] + refs[2 + c][q, sl]
             copies.append(pltpu.make_async_copy(buffer.at[q, c], out.at[q, c], done.at[2 * q + c]))
             copies[-1].start()
     for copy in copies:
@@ -377,18 +385,27 @@
         [spectrum, intensity[0, 0], shared, waves, patches, *tabs], WORK
     )
     came_high = [permute(x_high, SCATTER[0]), permute(y_high, SCATTER[1])]
-    grad_low, x_low, y_low = call(up_kernel, [PAIR, FIELD, FIELD], here, [state, waves, patches, *tabs], WORK)
-    came_low = [permute(x_low, SCATTER[0]), permute(y_low, SCATTER[1])]
-    parts = []
+    grad_low, came_low = [None, None], [None, None]
+    for k in (1, 0):
+        outs = call(
+            functools.partial(up_kernel, k), [FIELD, PLANE, PLANE] + [STATE] * k, here,
+            [state, waves, patches, *tabs], WORK
+        )
+        grad_low[k] = outs[0]
+        came_low[k] = [permute(outs[1], SCATTER[0]), permute(outs[2], SCATTER[1])]
+        state = outs[3] if k else None
+    parts, crosses = [], []
     for channel, there in ((0, at_x), (1, at_y)):
         straight, cross, stay, leaving = call(
             functools.partial(turn_kernel, channel), [FIELD] * 4, jnp.concatenate([here, there]),
-            [grad_low, grad_high, came_low[channel], came_high[channel]]
+            [*grad_low, grad_high, came_low[0][channel], came_low[1][channel], came_high[channel]]
         )
         way = 1 - channel
-        parts += [stay, permute(leaving, SWAP), permute(straight, SCATTER[way]), permute(cross, CROSSED[way])]
+        parts += [stay, permute(leaving, SWAP), permute(straight, SCATTER[way])]
+        crosses.append(permute(cross, CROSSED[way]))
+    sums = call(presum_kernel, [FIELD] * 2, here, parts)
     scratch = [pltpu.VMEM((2, 2, N, N), F32), pltpu.SemaphoreType.DMA((4,))]
-    out, = call(final_kernel, [PAIR], here, parts, scratch, pl.BlockSpec(memory_space=pl.ANY))
+    out, = call(final_kernel, [PAIR], here, [*sums, *crosses], scratch, pl.BlockSpec(memory_space=pl.ANY))
     return out[:, :, None]
 
 

time: 95 us -> 99.3 us (1.045)
  waiting for transfers between devices: 40.1 us -> 42.5 us
  Pallas kernels: 18.7 us -> 19.9 us
    ppermute x19 -> x21, waiting for transfers between devices: 40.1 us -> 42.5 us  [permute(): return lax.ppermute(block, ('depth', 'tiles'), pairs)]
    pallas_call x9 -> x11, Pallas kernels: 16 us -> 17.2 us  [call(): pl.pallas_call(kernel, out_shape=outs, in_specs=[SS] + [VS] * len(args),...]
    ppermute x19 -> x21, starting transfers between devices: 31.5 us -> 32.2 us  [permute(): return lax.ppermute(block, ('depth', 'tiles'), pairs)]
  transfers between devices with their start and end apart: 19 -> 21, of which waited for: 9 -> 12; matrix products, arithmetic and copies ran while one was open for 2% -> 2% of each run, Pallas kernels for 12% -> 16%
where the time goes in v6:
time: 99.3 us; the launch traced here: 99.1 us
  waiting for transfers between devices  42.5 us (43%)
  starting transfers between devices  32.2 us (32%)
  Pallas kernels  19.9 us (20%)
  other arithmetic  2.16 us (2%)
  local copies, waits for them, and re-layouts  1.35 us (1%)
  between operations  1.03 us (1%)
    ppermute x21, waiting for transfers between devices, permute(): return lax.ppermute(block, ('depth', 'tiles'), pairs)  42.5 us
    ppermute x21, starting transfers between devices, permute(): return lax.ppermute(block, ('depth', 'tiles'), pairs)  32.2 us
    pallas_call x11, Pallas kernels, call(): pl.pallas_call(kernel, out_shape=outs, in_specs=[SS] + [VS] * len(args),...  17.2 us
    pallas_call x1, Pallas kernels, tables(): pl.pallas_call(tables_kernel, out_shape=[jax.ShapeDtypeStruct((4, 2 * N,...  2.7 us
  transfers between devices with their start and end apart: 21, of which 12 were waited for; matrix products, arithmetic and copies ran while one was open for 2% of the time, Pallas kernels for 16%

profile of v6, /device:TPU:1, one launch (start us, length us, event | category | flops | bytes accessed | tf_op | source)
XLA Modules:
  0.0 99.1 jit_solution(4307131775465212754)
XLA Ops:
  0.0 1.4 %collective-permute-start.5 = (f32[2,2,256,256]{3,2,1,0:T(8,128)}, f32[2,2,256,256]{3,2,1,0:T(8,128)S(1)}, u32[]{:S(2)}, u32[]{:S(2)}) collective-permute-start(f32[2,2,256,256]{3,2,1,0:T(8,128)} %bitcast.14), channel_id=1, source_target_pairs={{0,64},{1,65},{2,66},{3,67},{4,68},{5,69},{6,70},{7,71},{8,72},{9,... | collective-permute-start | bytes 3145736 | tf_op jit(solution)/shard_map/ppermute | solution.py:344
  1.4 1.3 %collective-permute-start.3 = (f32[2,2,256,256]{3,2,1,0:T(8,128)}, f32[2,2,256,256]{3,2,1,0:T(8,128)S(1)}, u32[]{:S(2)}, u32[]{:S(2)}) collective-permute-start(f32[2,2,256,256]{3,2,1,0:T(8,128)} %bitcast.15), channel_id=1, source_target_pairs={{0,3},{1,0},{2,1},{3,2},{4,7},{5,4},{6,5},{7,6},{8,11},{9,8},{10,9... | collective-permute-start | bytes 3145736 | tf_op jit(solution)/shard_map/ppermute | solution.py:344
  2.7 1.2 %collective-permute-done.5.own.refs_3_ = f32[2,2,256,256]{3,2,1,0:T(8,128)S(1)} collective-permute-done((f32[2,2,256,256]{3,2,1,0:T(8,128)}, f32[2,2,256,256]{3,2,1,0:T(8,128)S(1)}, u32[]{:S(2)}, u32[]{:S(2)}) %collective-permute-start.5) | collective-permute-done | bytes 1048608 | tf_op jit(solution)/shard_map/ppermute | solution.py:344
  3.9 1.4 %collective-permute-start.6 = (f32[2,2,256,256]{3,2,1,0:T(8,128)S(1)}, f32[2,2,256,256]{3,2,1,0:T(8,128)S(1)}, u32[]{:S(2)}, u32[]{:S(2)}) collective-permute-start(f32[2,2,256,256]{3,2,1,0:T(8,128)S(1)} %collective-permute-done.5.own.refs_3_), channel_id=1, source_target_pairs={{0,60},{1,61},{2,62},{3,63},{4,0},{5,1},{6,2},{7,3},{8,4},{9,5},{1... | collective-permute-start | bytes 3145736 | tf_op jit(solution)/shard_map/ppermute | solution.py:344
  5.9 0.8 fusion.6
  6.7 0.1 pad_add_fusion.spot
  6.8 1.2 %collective-permute-start.1 = (s32[4]{0:T(128)S(1)}, s32[4]{0:T(128)S(1)}, u32[]{:S(2)}, u32[]{:S(2)}) collective-permute-start(s32[4]{0:T(128)S(1)} %pad_add_fusion.spot), channel_id=1, source_target_pairs={{0,1},{1,2},{2,3},{3,0},{4,5},{5,6},{6,7},{7,4},{8,9},{9,10},{10,1... | collective-permute-start | bytes 56 | tf_op jit(solution)/shard_map/ppermute | solution.py:344
  8.0 1.3 %collective-permute-start.2 = (s32[4]{0:T(128)S(1)}, s32[4]{0:T(128)S(1)}, u32[]{:S(2)}, u32[]{:S(2)}) collective-permute-start(s32[4]{0:T(128)S(1)} %pad_add_fusion.spot), channel_id=1, source_target_pairs={{0,4},{1,5},{2,6},{3,7},{4,8},{5,9},{6,10},{7,11},{8,12},{9,13},{1... | collective-permute-start | bytes 56 | tf_op jit(solution)/shard_map/ppermute | solution.py:344
  9.3 3.8 %collective-permute-start = (s32[4]{0:T(128)S(1)}, s32[4]{0:T(128)S(1)}, u32[]{:S(2)}, u32[]{:S(2)}) collective-permute-start(s32[4]{0:T(128)S(1)} %pad_add_fusion.spot), channel_id=1, source_target_pairs={{64,69},{65,70},{66,71},{67,68},{68,73},{69,74},{70,75},{71,72},{7... | collective-permute-start | bytes 56 | tf_op jit(solution)/shard_map/ppermute | solution.py:344
  13.1 0.0 copy-start
  13.1 1.2 %copy-done = f32[2,2,1,256,256]{4,3,2,1,0:T(8,128)S(1)} copy-done((f32[2,2,1,256,256]{4,3,2,1,0:T(8,128)S(1)}, f32[2,2,1,256,256]{4,3,2,1,0:T(8,128)}, u32[]{:S(2)}) %copy-start) | copy-done | bytes 1048600
  14.4 0.6 shard_map.64.own.refs_0_
  15.0 1.8 %collective-permute-done.1 = s32[4]{0:T(128)S(1)} collective-permute-done((s32[4]{0:T(128)S(1)}, s32[4]{0:T(128)S(1)}, u32[]{:S(2)}, u32[]{:S(2)}) %collective-permute-start.1) | collective-permute-done | bytes 48 | tf_op jit(solution)/shard_map/ppermute | solution.py:344
  16.7 5.7 %collective-permute-done.2 = s32[4]{0:T(128)S(1)} collective-permute-done((s32[4]{0:T(128)S(1)}, s32[4]{0:T(128)S(1)}, u32[]{:S(2)}, u32[]{:S(2)}) %collective-permute-start.2) | collective-permute-done | bytes 48 | tf_op jit(solution)/shard_map/ppermute | solution.py:344
  22.5 0.0 collective-permute-done.3.near.refs_1_
  22.5 0.7 shard_map.65
  23.1 0.0 copy-start.2
  23.2 0.1 collective-permute-start.4
  23.2 0.0 collective-permute-done.6.near.refs_4_
  23.3 0.0 copy-start.3
  23.3 0.7 shard_map.66
  23.9 0.0 copy-start.1
  23.9 1.3 %collective-permute-start.7 = (f32[2,2,256,256]{3,2,1,0:T(8,128)S(1)}, f32[2,2,256,256]{3,2,1,0:T(8,128)S(1)}, u32[]{:S(2)}, u32[]{:S(2)}) collective-permute-start(f32[2,2,256,256]{3,2,1,0:T(8,128)S(1)} %shard_map.66), channel_id=1, source_target_pairs={{0,3},{1,0},{2,1},{3,2},{4,7},{5,4},{6,5},{7,6},{8,11},{9,8},{10,9... | collective-permute-start | bytes 3145736 | tf_op jit(solution)/shard_map/ppermute | solution.py:344
  25.3 2.1 %collective-permute-start.8 = (f32[256,256]{1,0:T(8,128)S(1)}, f32[256,256]{1,0:T(8,128)S(1)}, u32[]{:S(2)}, u32[]{:S(2)}) collective-permute-start(f32[256,256]{1,0:T(8,128)S(1)} %get-tuple-element.61), channel_id=1, source_target_pairs={{64,69},{65,70},{66,71},{67,68},{68,73},{69,74},{70,75},{71,72},{7... | collective-permute-start | bytes 786440 | tf_op jit(solution)/shard_map/ppermute | solution.py:344
  27.4 0.1 pad_slice_fusion.1
  27.5 1.1 %negate_multiply_fusion = (f32[1,256,256]{2,1,0:T(8,128)S(1)}, f32[1,256,256]{2,1,0:T(8,128)S(1)}) fusion(), kind=kLoop, calls=%fused_computation.9 | loop fusion | flops 1114112 | bytes 524288 | tf_op jit(solution)/shard_map/mul | solution.py:352
  28.6 0.1 pad_maximum_fusion.1.taps
  28.6 0.0 collective-permute-done
  28.6 0.1 broadcast_select_fusion.3.spot
  28.7 2.7 %tables.1 = (bf16[4,512,512]{2,1,0:T(8,128)(2,1)S(1)}, bf16[4,512,512]{2,1,0:T(8,128)(2,1)S(1)}, bf16[4,512,256]{2,1,0:T(8,128)(2,1)S(1)}, bf16[4,512,256]{2,1,0:T(8,128)(2,1)S(1)}) custom-call(s32[4]{0:T(128)S(1)} %broadcast_select_fusion.3.spot, f32[8,256]{1,0:T(8,128)S(1)} %pad_maximum_fusion.1.taps, f32[2,256,256]{2,1,0:T(8,128)S(1)} %pad_maximum_fusion.dft), custom_call_target="tpu_custom_call" | custom-call | tf_op jit(solution)/shard_map/tables/pallas_call | solution.py:97
  31.4 8.8 %collective-permute-done.4.refs_2_ = f32[2,2,256,256]{3,2,1,0:T(8,128)S(1)} collective-permute-done((f32[2,2,256,256]{3,2,1,0:T(8,128)S(1)}, f32[2,2,256,256]{3,2,1,0:T(8,128)S(1)}, u32[]{:S(2)}, u32[]{:S(2)}) %collective-permute-start.4) | collective-permute-done | bytes 1048608 | tf_op jit(solution)/shard_map/ppermute | solution.py:344
  40.2 0.0 collective-permute-done.7.refs_5_
  40.2 5.2 %shard_map.67 = (f32[4,2,256,256]{3,2,1,0:T(8,128)S(1)}, f32[4,2,256,256]{3,2,1,0:T(8,128)S(1)}, f32[2,256,256]{2,1,0:T(8,128)S(1)}) custom-call(s32[4]{0:T(128)S(1)} %broadcast_select_fusion.3.spot, f32[2,2,256,256]{3,2,1,0:T(8,128)S(1)} %shard_map.64.own.refs_0_, f32[2,2,256,256]{3,2,1,0:T(8,128)S(1)} %collective-permute-done.3.near.refs_1_, ...), custom_call_target="tpu_custom_call" | custom-call | tf_op jit(solution)/shard_map/pallas_call | solution.py:252
  45.4 0.7 collective-permute-done.8.refs_2_
  46.1 2.8 %shard_map.68 = (f32[2,2,256,256]{3,2,1,0:T(8,128)S(1)}, f32[2,256,256]{2,1,0:T(8,128)S(1)}, f32[2,256,256]{2,1,0:T(8,128)S(1)}, bf16[2,512,256]{2,1,0:T(8,128)(2,1)S(1)}) custom-call(s32[4]{0:T(128)S(1)} %broadcast_select_fusion.3.spot, f32[2,256,256]{2,1,0:T(8,128)S(1)} %get-tuple-element.37.refs_0_, f32[256,256]{1,0:T(8,128)S(1)} %get-tuple-element.62.refs_1_, ...), custom_call_target="tpu_custom_call" | custom-call | tf_op jit(solution)/shard_map/pallas_call | solution.py:252
  49.0 2.8 %collective-permute-start.16 = (f32[2,256,256]{2,1,0:T(8,128)S(1)}, f32[2,256,256]{2,1,0:T(8,128)S(1)}, u32[]{:S(2)}, u32[]{:S(2)}) collective-permute-start(f32[2,256,256]{2,1,0:T(8,128)S(1)} %get-tuple-element.53), channel_id=1, source_target_pairs={{0,4},{1,5},{2,6},{3,7},{4,8},{5,9},{6,10},{7,11},{8,12},{9,13},{1... | collective-permute-start | bytes 1572872 | tf_op jit(solution)/shard_map/ppermute | solution.py:344
  51.7 1.6 %shard_map.69 = (f32[2,256,256]{2,1,0:T(8,128)S(1)}, f32[256,256]{1,0:T(8,128)S(1)}, f32[256,256]{1,0:T(8,128)S(1)}, bf16[2,512,256]{2,1,0:T(8,128)(2,1)S(1)}) custom-call(s32[4]{0:T(128)S(1)} %broadcast_select_fusion.3.spot, bf16[2,512,256]{2,1,0:T(8,128)(2,1)S(1)} %get-tuple-element.40.refs_0_, f32[4,2,256,256]{3,2,1,0:T(8,128)S(1)} %get-tuple-element.38.refs_3_.refs_1_, ...), custom_call_target="tpu_custom_call" | custom-call | tf_op jit(solution)/shard_map/pallas_call | solution.py:252
  53.4 1.6 %shard_map.70 = (f32[2,256,256]{2,1,0:T(8,128)S(1)}, f32[256,256]{1,0:T(8,128)S(1)}, f32[256,256]{1,0:T(8,128)S(1)}) custom-call(s32[4]{0:T(128)S(1)} %broadcast_select_fusion.3.spot, bf16[2,512,256]{2,1,0:T(8,128)(2,1)S(1)} %get-tuple-element.41.refs_0_, f32[4,2,256,256]{3,2,1,0:T(8,128)S(1)} %get-tuple-element.38.refs_3_.refs_1_, ...), custom_call_target="tpu_custom_call" | custom-call | tf_op jit(solution)/shard_map/pallas_call | solution.py:252
  54.9 0.1 collective-permute-start.14
  55.0 0.1 collective-permute-start.15
  55.1 0.1 pad_add_fusion.2
  55.2 1.8 %collective-permute-start.11 = (f32[2,256,256]{2,1,0:T(8,128)S(1)}, f32[2,256,256]{2,1,0:T(8,128)S(1)}, u32[]{:S(2)}, u32[]{:S(2)}) collective-permute-start(f32[2,256,256]{2,1,0:T(8,128)S(1)} %get-tuple-element.47), channel_id=1, source_target_pairs={{0,1},{1,2},{2,3},{3,0},{4,5},{5,6},{6,7},{7,4},{8,9},{9,10},{10,1... | collective-permute-start | bytes 1572872 | tf_op jit(solution)/shard_map/ppermute | solution.py:344
  57.0 3.7 %collective-permute-done.14.refs_3_ = f32[256,256]{1,0:T(8,128)S(1)} collective-permute-done((f32[256,256]{1,0:T(8,128)S(1)}, f32[256,256]{1,0:T(8,128)S(1)}, u32[]{:S(2)}, u32[]{:S(2)}) %collective-permute-start.14) | collective-permute-done | bytes 262176 | tf_op jit(solution)/shard_map/ppermute | solution.py:344
  60.7 2.8 %collective-permute-done.15.refs_4_ = f32[256,256]{1,0:T(8,128)S(1)} collective-permute-done((f32[256,256]{1,0:T(8,128)S(1)}, f32[256,256]{1,0:T(8,128)S(1)}, u32[]{:S(2)}, u32[]{:S(2)}) %collective-permute-start.15) | collective-permute-done | bytes 262176 | tf_op jit(solution)/shard_map/ppermute | solution.py:344
  63.5 0.0 collective-permute-done.16.refs_5_
  63.5 0.9 shard_map.72
  64.4 3.6 %collective-permute-start.17 = (f32[2,256,256]{2,1,0:T(8,128)S(1)}, f32[2,256,256]{2,1,0:T(8,128)S(1)}, u32[]{:S(2)}, u32[]{:S(2)}) collective-permute-start(f32[2,256,256]{2,1,0:T(8,128)S(1)} %get-tuple-element.55), channel_id=1, source_target_pairs={{0,64},{1,65},{2,66},{3,67},{4,68},{5,69},{6,70},{7,71},{8,72},{9,... | collective-permute-start | bytes 1572872 | tf_op jit(solution)/shard_map/ppermute | solution.py:344
  68.0 3.4 %collective-permute-start.9 = (f32[256,256]{1,0:T(8,128)S(1)}, f32[256,256]{1,0:T(8,128)S(1)}, u32[]{:S(2)}, u32[]{:S(2)}) collective-permute-start(f32[256,256]{1,0:T(8,128)S(1)} %get-tuple-element.45), channel_id=1, source_target_pairs={{0,1},{1,2},{2,3},{3,0},{4,5},{5,6},{6,7},{7,4},{8,9},{9,10},{10,1... | collective-permute-start | bytes 786440 | tf_op jit(solution)/shard_map/ppermute | solution.py:344
  71.4 0.0 collective-permute-start.10
  71.4 0.0 collective-permute-start.18
  71.4 3.3 %collective-permute-done.9.refs_3_ = f32[256,256]{1,0:T(8,128)S(1)} collective-permute-done((f32[256,256]{1,0:T(8,128)S(1)}, f32[256,256]{1,0:T(8,128)S(1)}, u32[]{:S(2)}, u32[]{:S(2)}) %collective-permute-start.9) | collective-permute-done | bytes 262176 | tf_op jit(solution)/shard_map/ppermute | solution.py:344
  74.7 2.8 %collective-permute-done.10.refs_4_ = f32[256,256]{1,0:T(8,128)S(1)} collective-permute-done((f32[256,256]{1,0:T(8,128)S(1)}, f32[256,256]{1,0:T(8,128)S(1)}, u32[]{:S(2)}, u32[]{:S(2)}) %collective-permute-start.10) | collective-permute-done | bytes 262176 | tf_op jit(solution)/shard_map/ppermute | solution.py:344
  77.5 0.9 shard_map.71
  78.4 1.5 %collective-permute-start.12 = (f32[2,256,256]{2,1,0:T(8,128)S(1)}, f32[2,256,256]{2,1,0:T(8,128)S(1)}, u32[]{:S(2)}, u32[]{:S(2)}) collective-permute-start(f32[2,256,256]{2,1,0:T(8,128)S(1)} %get-tuple-element.49), channel_id=1, source_target_pairs={{0,64},{1,65},{2,66},{3,67},{4,68},{5,69},{6,70},{7,71},{8,72},{9,... | collective-permute-start | bytes 1572872 | tf_op jit(solution)/shard_map/ppermute | solution.py:344
  79.9 1.7 %collective-permute-start.13 = (f32[2,256,256]{2,1,0:T(8,128)S(1)}, f32[2,256,256]{2,1,0:T(8,128)S(1)}, u32[]{:S(2)}, u32[]{:S(2)}) collective-permute-start(f32[2,256,256]{2,1,0:T(8,128)S(1)} %get-tuple-element.50), channel_id=1, source_target_pairs={{0,4},{1,5},{2,6},{3,7},{4,8},{5,9},{6,10},{7,11},{8,12},{9,13},{1... | collective-permute-start | bytes 1572872 | tf_op jit(solution)/shard_map/ppermute | solution.py:344
  81.6 0.4 collective-permute-start.20
  82.0 0.0 collective-permute-done.17.refs_4_
  82.0 2.9 %collective-permute-start.19 = (f32[2,256,256]{2,1,0:T(8,128)S(1)}, f32[2,256,256]{2,1,0:T(8,128)S(1)}, u32[]{:S(2)}, u32[]{:S(2)}) collective-permute-start(f32[2,256,256]{2,1,0:T(8,128)S(1)} %get-tuple-element.59), channel_id=1, source_target_pairs={{0,68},{1,69},{2,70},{3,71},{4,72},{5,73},{6,74},{7,75},{8,76},{9,... | collective-permute-start | bytes 1572872 | tf_op jit(solution)/shard_map/ppermute | solution.py:344
  84.9 0.0 collective-permute-done.12.refs_1_
  84.9 3.3 %collective-permute-done.13.refs_2_ = f32[2,256,256]{2,1,0:T(8,128)S(1)} collective-permute-done((f32[2,256,256]{2,1,0:T(8,128)S(1)}, f32[2,256,256]{2,1,0:T(8,128)S(1)}, u32[]{:S(2)}, u32[]{:S(2)}) %collective-permute-start.13) | collective-permute-done | bytes 524320 | tf_op jit(solution)/shard_map/ppermute | solution.py:344
  88.2 0.7 shard_map.73
  88.9 2.8 %collective-permute-done.20.refs_3_ = f32[2,256,256]{2,1,0:T(8,128)S(1)} collective-permute-done((f32[2,256,256]{2,1,0:T(8,128)S(1)}, f32[2,256,256]{2,1,0:T(8,128)S(1)}, u32[]{:S(2)}, u32[]{:S(2)}) %collective-permute-start.20) | collective-permute-done | bytes 524320 | tf_op jit(solution)/shard_map/ppermute | solution.py:344
  91.7 5.7 %collective-permute-done.19.refs_2_ = f32[2,256,256]{2,1,0:T(8,128)S(1)} collective-permute-done((f32[2,256,256]{2,1,0:T(8,128)S(1)}, f32[2,256,256]{2,1,0:T(8,128)S(1)}, u32[]{:S(2)}, u32[]{:S(2)}) %collective-permute-start.19) | collective-permute-done | bytes 524320 | tf_op jit(solution)/shard_map/ppermute | solution.py:344
  97.4 1.6 %shard_map.74 = f32[2,2,256,256]{3,2,1,0:T(8,128)} custom-call(s32[4]{0:T(128)S(1)} %broadcast_select_fusion.3.spot, f32[2,256,256]{2,1,0:T(8,128)S(1)} %get-tuple-element.57.refs_0_, f32[2,256,256]{2,1,0:T(8,128)S(1)} %get-tuple-element.58.refs_1_, f32[2,256,256]{2,1,0:T(8,128)S(1)} %collective-permute-done.19.refs_2_, ...), custom_call_target="tpu_custom_call" | custom-call | tf_op jit(solution)/shard_map/pallas_call | solution.py:252
  (9 shorter events, 0.1 us)
Async XLA Ops:
  0.0 3.9 %collective-permute-start.5 = (f32[2,2,256,256]{3,2,1,0:T(8,128)}, f32[2,2,256,256]{3,2,1,0:T(8,128)S(1)}, u32[]{:S(2)}, u32[]{:S(2)}) collective-permute-start(f32[2,2,256,256]{3,2,1,0:T(8,128)} %bitcast.14), channel_id=1, source_target_pairs={{0,64},{1,65},{2,66},{3,67},{4,68},{5,69},{6,70},{7,71},{8,72},{9,... | collective-permute-start | bytes 3145736 | tf_op jit(solution)/shard_map/ppermute | solution.py:344
  1.4 21.1 %collective-permute-start.3 = (f32[2,2,256,256]{3,2,1,0:T(8,128)}, f32[2,2,256,256]{3,2,1,0:T(8,128)S(1)}, u32[]{:S(2)}, u32[]{:S(2)}) collective-permute-start(f32[2,2,256,256]{3,2,1,0:T(8,128)} %bitcast.15), channel_id=1, source_target_pairs={{0,3},{1,0},{2,1},{3,2},{4,7},{5,4},{6,5},{7,6},{8,11},{9,8},{10,9... | collective-permute-start | bytes 3145736 | tf_op jit(solution)/shard_map/ppermute | solution.py:344
  3.9 19.4 %collective-permute-start.6 = (f32[2,2,256,256]{3,2,1,0:T(8,128)S(1)}, f32[2,2,256,256]{3,2,1,0:T(8,128)S(1)}, u32[]{:S(2)}, u32[]{:S(2)}) collective-permute-start(f32[2,2,256,256]{3,2,1,0:T(8,128)S(1)} %collective-permute-done.5.own.refs_3_), channel_id=1, source_target_pairs={{0,60},{1,61},{2,62},{3,63},{4,0},{5,1},{6,2},{7,3},{8,4},{9,5},{1... | collective-permute-start | bytes 3145736 | tf_op jit(solution)/shard_map/ppermute | solution.py:344
  6.8 10.0 %collective-permute-start.1 = (s32[4]{0:T(128)S(1)}, s32[4]{0:T(128)S(1)}, u32[]{:S(2)}, u32[]{:S(2)}) collective-permute-start(s32[4]{0:T(128)S(1)} %pad_add_fusion.spot), channel_id=1, source_target_pairs={{0,1},{1,2},{2,3},{3,0},{4,5},{5,6},{6,7},{7,4},{8,9},{9,10},{10,1... | collective-permute-start | bytes 56 | tf_op jit(solution)/shard_map/ppermute | solution.py:344
  8.0 14.5 %collective-permute-start.2 = (s32[4]{0:T(128)S(1)}, s32[4]{0:T(128)S(1)}, u32[]{:S(2)}, u32[]{:S(2)}) collective-permute-start(s32[4]{0:T(128)S(1)} %pad_add_fusion.spot), channel_id=1, source_target_pairs={{0,4},{1,5},{2,6},{3,7},{4,8},{5,9},{6,10},{7,11},{8,12},{9,13},{1... | collective-permute-start | bytes 56 | tf_op jit(solution)/shard_map/ppermute | solution.py:344
  9.3 19.4 %collective-permute-start = (s32[4]{0:T(128)S(1)}, s32[4]{0:T(128)S(1)}, u32[]{:S(2)}, u32[]{:S(2)}) collective-permute-start(s32[4]{0:T(128)S(1)} %pad_add_fusion.spot), channel_id=1, source_target_pairs={{64,69},{65,70},{66,71},{67,68},{68,73},{69,74},{70,75},{71,72},{7... | collective-permute-start | bytes 56 | tf_op jit(solution)/shard_map/ppermute | solution.py:344
  13.1 1.2 %copy-start = (f32[2,2,1,256,256]{4,3,2,1,0:T(8,128)S(1)}, f32[2,2,1,256,256]{4,3,2,1,0:T(8,128)}, u32[]{:S(2)}) copy-start(f32[2,2,1,256,256]{4,3,2,1,0:T(8,128)} %param.6) | copy-start | bytes 3145732
  23.1 2.1 %copy-start.2 = (f32[1,2,256,256]{3,2,1,0:T(8,128)S(1)}, f32[1,2,256,256]{3,2,1,0:T(8,128)}, u32[]{:S(2)}) copy-start(f32[1,2,256,256]{3,2,1,0:T(8,128)} %param.9) | copy-start | bytes 1572868
  23.2 17.0 %collective-permute-start.4 = (f32[2,2,256,256]{3,2,1,0:T(8,128)S(1)}, f32[2,2,256,256]{3,2,1,0:T(8,128)S(1)}, u32[]{:S(2)}, u32[]{:S(2)}) collective-permute-start(f32[2,2,256,256]{3,2,1,0:T(8,128)S(1)} %shard_map.65), channel_id=1, source_target_pairs={{0,60},{1,61},{2,62},{3,63},{4,0},{5,1},{6,2},{7,3},{8,4},{9,5},{1... | collective-permute-start | bytes 3145736 | tf_op jit(solution)/shard_map/ppermute | solution.py:344
  23.3 4.1 %copy-start.3 = (f32[2,31]{1,0:T(2,128)S(1)}, f32[2,31]{1,0:T(2,128)}, u32[]{:S(2)}) copy-start(f32[2,31]{1,0:T(2,128)} %param.8) | copy-start | bytes 748
  23.9 16.3 %copy-start.1 = (f32[2,256,256]{2,1,0:T(8,128)S(1)}, f32[2,256,256]{2,1,0:T(8,128)}, u32[]{:S(2)}) copy-start(f32[2,256,256]{2,1,0:T(8,128)} %refs_6_.1) | copy-start | bytes 1572868
  23.9 16.3 %collective-permute-start.7 = (f32[2,2,256,256]{3,2,1,0:T(8,128)S(1)}, f32[2,2,256,256]{3,2,1,0:T(8,128)S(1)}, u32[]{:S(2)}, u32[]{:S(2)}) collective-permute-start(f32[2,2,256,256]{3,2,1,0:T(8,128)S(1)} %shard_map.66), channel_id=1, source_target_pairs={{0,3},{1,0},{2,1},{3,2},{4,7},{5,4},{6,5},{7,6},{8,11},{9,8},{10,9... | collective-permute-start | bytes 3145736 | tf_op jit(solution)/shard_map/ppermute | solution.py:344
  25.3 20.9 %collective-permute-start.8 = (f32[256,256]{1,0:T(8,128)S(1)}, f32[256,256]{1,0:T(8,128)S(1)}, u32[]{:S(2)}, u32[]{:S(2)}) collective-permute-start(f32[256,256]{1,0:T(8,128)S(1)} %get-tuple-element.61), channel_id=1, source_target_pairs={{64,69},{65,70},{66,71},{67,68},{68,73},{69,74},{70,75},{71,72},{7... | collective-permute-start | bytes 786440 | tf_op jit(solution)/shard_map/ppermute | solution.py:344
  49.0 14.5 %collective-permute-start.16 = (f32[2,256,256]{2,1,0:T(8,128)S(1)}, f32[2,256,256]{2,1,0:T(8,128)S(1)}, u32[]{:S(2)}, u32[]{:S(2)}) collective-permute-start(f32[2,256,256]{2,1,0:T(8,128)S(1)} %get-tuple-element.53), channel_id=1, source_target_pairs={{0,4},{1,5},{2,6},{3,7},{4,8},{5,9},{6,10},{7,11},{8,12},{9,13},{1... | collective-permute-start | bytes 1572872 | tf_op jit(solution)/shard_map/ppermute | solution.py:344
  54.9 5.7 %collective-permute-start.14 = (f32[256,256]{1,0:T(8,128)S(1)}, f32[256,256]{1,0:T(8,128)S(1)}, u32[]{:S(2)}, u32[]{:S(2)}) collective-permute-start(f32[256,256]{1,0:T(8,128)S(1)} %get-tuple-element.51), channel_id=1, source_target_pairs={{0,4},{1,5},{2,6},{3,7},{4,8},{5,9},{6,10},{7,11},{8,12},{9,13},{1... | collective-permute-start | bytes 786440 | tf_op jit(solution)/shard_map/ppermute | solution.py:344
  55.0 8.4 %collective-permute-start.15 = (f32[256,256]{1,0:T(8,128)S(1)}, f32[256,256]{1,0:T(8,128)S(1)}, u32[]{:S(2)}, u32[]{:S(2)}) collective-permute-start(f32[256,256]{1,0:T(8,128)S(1)} %get-tuple-element.52), channel_id=1, source_target_pairs={{0,4},{1,5},{2,6},{3,7},{4,8},{5,9},{6,10},{7,11},{8,12},{9,13},{1... | collective-permute-start | bytes 786440 | tf_op jit(solution)/shard_map/ppermute | solution.py:344
  55.2 22.3 %collective-permute-start.11 = (f32[2,256,256]{2,1,0:T(8,128)S(1)}, f32[2,256,256]{2,1,0:T(8,128)S(1)}, u32[]{:S(2)}, u32[]{:S(2)}) collective-permute-start(f32[2,256,256]{2,1,0:T(8,128)S(1)} %get-tuple-element.47), channel_id=1, source_target_pairs={{0,1},{1,2},{2,3},{3,0},{4,5},{5,6},{6,7},{7,4},{8,9},{9,10},{10,1... | collective-permute-start | bytes 1572872 | tf_op jit(solution)/shard_map/ppermute | solution.py:344
  64.4 17.6 %collective-permute-start.17 = (f32[2,256,256]{2,1,0:T(8,128)S(1)}, f32[2,256,256]{2,1,0:T(8,128)S(1)}, u32[]{:S(2)}, u32[]{:S(2)}) collective-permute-start(f32[2,256,256]{2,1,0:T(8,128)S(1)} %get-tuple-element.55), channel_id=1, source_target_pairs={{0,64},{1,65},{2,66},{3,67},{4,68},{5,69},{6,70},{7,71},{8,72},{9,... | collective-permute-start | bytes 1572872 | tf_op jit(solution)/shard_map/ppermute | solution.py:344
  68.0 6.7 %collective-permute-start.9 = (f32[256,256]{1,0:T(8,128)S(1)}, f32[256,256]{1,0:T(8,128)S(1)}, u32[]{:S(2)}, u32[]{:S(2)}) collective-permute-start(f32[256,256]{1,0:T(8,128)S(1)} %get-tuple-element.45), channel_id=1, source_target_pairs={{0,1},{1,2},{2,3},{3,0},{4,5},{5,6},{6,7},{7,4},{8,9},{9,10},{10,1... | collective-permute-start | bytes 786440 | tf_op jit(solution)/shard_map/ppermute | solution.py:344
  71.4 6.1 %collective-permute-start.10 = (f32[256,256]{1,0:T(8,128)S(1)}, f32[256,256]{1,0:T(8,128)S(1)}, u32[]{:S(2)}, u32[]{:S(2)}) collective-permute-start(f32[256,256]{1,0:T(8,128)S(1)} %get-tuple-element.46), channel_id=1, source_target_pairs={{0,1},{1,2},{2,3},{3,0},{4,5},{5,6},{6,7},{7,4},{8,9},{9,10},{10,1... | collective-permute-start | bytes 786440 | tf_op jit(solution)/shard_map/ppermute | solution.py:344
  71.4 13.5 %collective-permute-start.18 = (f32[2,256,256]{2,1,0:T(8,128)S(1)}, f32[2,256,256]{2,1,0:T(8,128)S(1)}, u32[]{:S(2)}, u32[]{:S(2)}) collective-permute-start(f32[2,256,256]{2,1,0:T(8,128)S(1)} %get-tuple-element.56), channel_id=1, source_target_pairs={{0,1},{1,2},{2,3},{3,0},{4,5},{5,6},{6,7},{7,4},{8,9},{9,10},{10,1... | collective-permute-start | bytes 1572872 | tf_op jit(solution)/shard_map/ppermute | solution.py:344
  78.4 6.5 %collective-permute-start.12 = (f32[2,256,256]{2,1,0:T(8,128)S(1)}, f32[2,256,256]{2,1,0:T(8,128)S(1)}, u32[]{:S(2)}, u32[]{:S(2)}) collective-permute-start(f32[2,256,256]{2,1,0:T(8,128)S(1)} %get-tuple-element.49), channel_id=1, source_target_pairs={{0,64},{1,65},{2,66},{3,67},{4,68},{5,69},{6,70},{7,71},{8,72},{9,... | collective-permute-start | bytes 1572872 | tf_op jit(solution)/shard_map/ppermute | solution.py:344
  79.9 8.3 %collective-permute-start.13 = (f32[2,256,256]{2,1,0:T(8,128)S(1)}, f32[2,256,256]{2,1,0:T(8,128)S(1)}, u32[]{:S(2)}, u32[]{:S(2)}) collective-permute-start(f32[2,256,256]{2,1,0:T(8,128)S(1)} %get-tuple-element.50), channel_id=1, source_target_pairs={{0,4},{1,5},{2,6},{3,7},{4,8},{5,9},{6,10},{7,11},{8,12},{9,13},{1... | collective-permute-start | bytes 1572872 | tf_op jit(solution)/shard_map/ppermute | solution.py:344
  81.6 10.1 %collective-permute-start.20 = (f32[2,256,256]{2,1,0:T(8,128)S(1)}, f32[2,256,256]{2,1,0:T(8,128)S(1)}, u32[]{:S(2)}, u32[]{:S(2)}) collective-permute-start(f32[2,256,256]{2,1,0:T(8,128)S(1)} %get-tuple-element.60), channel_id=1, source_target_pairs={{0,65},{1,66},{2,67},{3,64},{4,69},{5,70},{6,71},{7,68},{8,73},{9,... | collective-permute-start | bytes 1572872 | tf_op jit(solution)/shard_map/ppermute | solution.py:344
  82.0 15.4 %collective-permute-start.19 = (f32[2,256,256]{2,1,0:T(8,128)S(1)}, f32[2,256,256]{2,1,0:T(8,128)S(1)}, u32[]{:S(2)}, u32[]{:S(2)}) collective-permute-start(f32[2,256,256]{2,1,0:T(8,128)S(1)} %get-tuple-element.59), channel_id=1, source_target_pairs={{0,68},{1,69},{2,70},{3,71},{4,72},{5,73},{6,74},{7,75},{8,76},{9,... | collective-permute-start | bytes 1572872 | tf_op jit(solution)/shard_map/ppermute | solution.py:344

commit v7 on v6

--- a/solution.py
+++ b/solution.py
@@ -17,7 +17,6 @@
 F32 = jnp.float32
 FIELD = jax.ShapeDtypeStruct((2, N, N), F32)
 PAIR = jax.ShapeDtypeStruct((2, 2, N, N), F32)
-ALL = jax.ShapeDtypeStruct((4, 2, N, N), F32)
 VS = pl.BlockSpec(memory_space=pltpu.VMEM)
 SS = pl.BlockSpec(memory_space=pltpu.SMEM)
 
@@ -186,27 +185,35 @@
             put_field(work, r0, wr * mr + wi * mi, wr * mi - wi * mr)
 
 
-def down_kernel(spot, *refs):
-    mine, near_x, far_y, other, near_y, far_x = refs[0:6]
-    probe, tabs = refs[6], refs[7:11]
-    patches, waves, spectrum = refs[11:14]
-    work = refs[14:]
-    core = spot[2]
+def gather_patch(spot, p, own, near, far, out):
     cols = own_cols(spot)
-    for q in range(2):
-        for sl, _, r0 in chunks():
-            rows = own_rows(spot, r0)
-            for c in range(2):
-                inner = jnp.where(cols, mine[q, c, sl], near_x[q, c, sl])
-                patches[2 * core + q, c, sl] = jnp.where(rows, inner, far_y[q, c, sl])
-                inner = jnp.where(rows, other[q, c, sl], near_y[q, c, sl])
-                patches[2 - 2 * core + q, c, sl] = jnp.where(cols, inner, far_x[q, c, sl])
+    for sl, _, r0 in chunks():
+        rows = own_rows(spot, r0)
+        inner, outer = (cols, rows) if p % 2 == 0 else (rows, cols)
+        for c in range(2):
+            out[c, sl] = jnp.where(outer, jnp.where(inner, own[c, sl], near[c, sl]), far[c, sl])
+
+
+def first_kernel(spot, *refs):
+    own, near, far, probe, tabs = refs[0:2], refs[2:4], refs[4:6], refs[6], refs[7:11]
+    patches, waves, work = refs[11:13], refs[13:16], refs[16:]
     for c in range(2):
-        waves[0, c] = pltpu.roll(pltpu.roll(probe[c], spot[0], 0), spot[1], 1)
-    for k in range(4):
-        enter_slice(work, patches.at[k], waves.at[k])
-        propagate(work, tabs, 0 if k < 3 else 2)
-        leave(work, waves.at[k + 1] if k < 3 else spectrum)
+        waves[0][c] = pltpu.roll(pltpu.roll(probe[c], spot[0], 0), spot[1], 1)
+    for p in range(2):
+        gather_patch(spot, p, own[p], near[p], far[p], patches[p])
+        enter_slice(work, patches[p], waves[p])
+        propagate(work, tabs, 0)
+        leave(work, waves[p + 1])
+
+
+def second_kernel(spot, *refs):
+    own, near, far, wave, tabs = refs[0:2], refs[2:4], refs[4:6], refs[6], refs[7:11]
+    patches, middle, spectrum, work = refs[11:13], refs[13], refs[14], refs[15:]
+    for p in range(2):
+        gather_patch(spot, p, own[p], near[p], far[p], patches[p])
+        enter_slice(work, patches[p], middle if p else wave)
+        propagate(work, tabs, 2 * p)
+        leave(work, spectrum if p else middle)
 
 
 def save(work, state):
@@ -215,9 +222,9 @@
 
 
 def turn_up_kernel(spot, *refs):
-    spectrum, measured, shared, waves, patches, tabs = refs[0], refs[1], refs[2], refs[3], refs[4], refs[5:9]
-    grad, sent_x, sent_y, state = refs[9:13]
-    work = refs[13:]
+    spectrum, measured, shared, waves, patches, tabs = refs[0], refs[1], refs[2], refs[3:5], refs[5:7], refs[7:11]
+    grad, sent_x, sent_y, state = refs[11:15]
+    work = refs[15:]
     upper = spot[2] == 1
     scale = 2.0 * spot[3].astype(F32)
     for sl, _, r0 in chunks():
@@ -227,18 +234,18 @@
         put_field(work, r0, misfit * sr, misfit * si)
     for k in (3, 2):
         propagate(work, tabs, 3 if k == 3 else 1)
-        leave_slice(work, spot, patches.at[k], waves.at[k], grad.at[k - 2], sent_x.at[k - 2], sent_y.at[k - 2], True)
+        leave_slice(work, spot, patches[k - 2], waves[k - 2], grad.at[k - 2], sent_x.at[k - 2], sent_y.at[k - 2], True)
     save(work, state)
 
 
 def up_kernel(k, spot, *refs):
-    state, waves, patches, tabs = refs[0], refs[1], refs[2], refs[3:7]
+    state, wave, patch, tabs = refs[0], refs[1], refs[2], refs[3:7]
     grad, sent_x, sent_y = refs[7:10]
     work = refs[11:] if k > 0 else refs[10:]
     work[0][...] = state[0]
     work[1][...] = state[1]
     propagate(work, tabs, 1)
-    leave_slice(work, spot, patches.at[k], waves.at[k], grad, sent_x, sent_y, k > 0)
+    leave_slice(work, spot, patch, wave, grad, sent_x, sent_y, k > 0)
     if k > 0:
         save(work, refs[10])
 
@@ -259,20 +266,21 @@
     )(spot, *args)
 
 
-def load_kernel(spot, block, out):
-    for q in range(2):
+def order_kernel(spot, mine, other, *outs):
+    upper = spot[2] == 1
+    for k in range(4):
         for c in range(2):
             for sl, _, _ in chunks():
-                out[q, c, sl] = block[q, c, sl]
+                a, b = mine[k % 2, c, sl], other[k % 2, c, sl]
+                outs[k][c, sl] = jnp.where(upper, b, a) if k < 2 else jnp.where(upper, a, b)
 
 
 def blend_kernel(by_rows, spot, own, near, mixed):
     cols = own_cols(spot)
     for sl, _, r0 in chunks():
         mask = own_rows(spot, r0) if by_rows else cols
-        for q in range(2):
-            for c in range(2):
-                mixed[q, c, sl] = jnp.where(mask, own[q, c, sl], near[q, c, sl])
+        for c in range(2):
+            mixed[c, sl] = jnp.where(mask, own[c, sl], near[c, sl])
 
 
 def turn_kernel(channel, spots, *refs):
@@ -356,7 +364,6 @@
     core = lax.axis_index("depth").astype(jnp.int32)
     mine = transmission[:, :, 0]
     other = permute(mine, SWAP)
-    near_x = permute(mine, GATHER[0])
     alive = (core < counts[0]).astype(jnp.int32)
     info = jnp.concatenate([jnp.where(core == 0, offsets[0, 0], offsets[0, 1]), core[None], alive[None]])
     left = permute(info, INFO[0])
@@ -365,31 +372,32 @@
     here = jnp.where(core == 0, info, upleft)
     at_y = jnp.where(core == 0, up, left)
     at_x = jnp.where(core == 0, left, up)
-    near_y = permute(other, GATHER[1])
-
-    mine, = call(load_kernel, [PAIR], info, [mine])
-    mixed, = call(functools.partial(blend_kernel, False), [PAIR], at_y, [mine, near_x])
-    far_y = permute(mixed, GATHER[1])
-    mixed, = call(functools.partial(blend_kernel, True), [PAIR], at_x, [other, near_y])
-    far_x = permute(mixed, GATHER[0])
+    own = call(order_kernel, [FIELD] * 4, info, [mine, other])
+    near = [permute(own[p], GATHER[p % 2]) for p in range(4)]
+    far = []
+    for p in range(4):
+        mixed, = call(functools.partial(blend_kernel, p % 2 == 1), [FIELD], (at_y, at_x)[p % 2], [own[p], near[p]])
+        far.append(permute(mixed, GATHER[1 - p % 2]))
     second_slot = intensity[0, 1]
     shared = permute(second_slot, DIAGONAL)
 
     tabs = tables(here, tap_rows(fresnel_taps), fourier())
-    patches, waves, spectrum = call(
-        down_kernel, [ALL, ALL, FIELD], here,
-        [mine, near_x, far_y, other, near_y, far_x, illumination, *tabs], WORK
+    patch0, patch1, wave0, wave1, wave2 = call(
+        first_kernel, [FIELD] * 5, here, [*own[:2], *near[:2], *far[:2], illumination, *tabs], WORK
+    )
+    patch2, patch3, wave3, spectrum = call(
+        second_kernel, [FIELD] * 4, here, [*own[2:], *near[2:], *far[2:], wave2, *tabs], WORK
     )
     grad_high, x_high, y_high, state = call(
         turn_up_kernel, [PAIR, FIELD, FIELD, STATE], here,
-        [spectrum, intensity[0, 0], shared, waves, patches, *tabs], WORK
+        [spectrum, intensity[0, 0], shared, wave2, wave3, patch2, patch3, *tabs], WORK
     )
     came_high = [permute(x_high, SCATTER[0]), permute(y_high, SCATTER[1])]
     grad_low, came_low = [None, None], [None, None]
     for k in (1, 0):
         outs = call(
             functools.partial(up_kernel, k), [FIELD, PLANE, PLANE] + [STATE] * k, here,
-            [state, waves, patches, *tabs], WORK
+            [state, (wave0, wave1)[k], (patch0, patch1)[k], *tabs], WORK
         )
         grad_low[k] = outs[0]
         came_low[k] = [permute(outs[1], SCATTER[0]), permute(outs[2], SCATTER[1])]

time: 99.3 us -> 102 us (1.027)
  starting transfers between devices: 32.2 us -> 25.5 us
  waiting for transfers between devices: 42.5 us -> 49.2 us
  Pallas kernels: 19.9 us -> 21.5 us
    ppermute x21 -> x25, starting transfers between devices: 32.2 us -> 25.5 us  [permute(): return lax.ppermute(block, ('depth', 'tiles'), pairs)]
    ppermute x21 -> x25, waiting for transfers between devices: 42.5 us -> 49.2 us  [permute(): return lax.ppermute(block, ('depth', 'tiles'), pairs)]
    pallas_call x11 -> x14, Pallas kernels: 17.2 us -> 18.8 us  [call(): pl.pallas_call(kernel, out_shape=outs, in_specs=[SS] + [VS] * len(args),...]
  transfers between devices with their start and end apart: 21 -> 25, of which waited for: 12 -> 12; matrix products, arithmetic and copies ran while one was open for 2% -> 3% of each run, Pallas kernels for 16% -> 17%
where the time goes in v7:
time: 102 us; the launch traced here: 101 us
  waiting for transfers between devices  49.2 us (48%)
  starting transfers between devices  25.5 us (25%)
  Pallas kernels  21.5 us (21%)
  other arithmetic  2.16 us (2%)
  local copies, waits for them, and re-layouts  2.03 us (2%)
  between operations  1.1 us (1%)
    ppermute x25, waiting for transfers between devices, permute(): return lax.ppermute(block, ('depth', 'tiles'), pairs)  49.2 us
    ppermute x25, starting transfers between devices, permute(): return lax.ppermute(block, ('depth', 'tiles'), pairs)  25.5 us
    pallas_call x14, Pallas kernels, call(): pl.pallas_call(kernel, out_shape=outs, in_specs=[SS] + [VS] * len(args),...  18.8 us
    pallas_call x1, Pallas kernels, tables(): pl.pallas_call(tables_kernel, out_shape=[jax.ShapeDtypeStruct((4, 2 * N,...  2.7 us
  transfers between devices with their start and end apart: 25, of which 12 were waited for; matrix products, arithmetic and copies ran while one was open for 3% of the time, Pallas kernels for 17%

profile of v7, /device:TPU:1, one launch (start us, length us, event | category | flops | bytes accessed | tf_op | source)
XLA Modules:
  0.0 101.5 jit_solution(17686963378118082369)
XLA Ops:
  0.0 1.4 %collective-permute-start.3 = (f32[2,2,256,256]{3,2,1,0:T(8,128)}, f32[2,2,256,256]{3,2,1,0:T(8,128)S(1)}, u32[]{:S(2)}, u32[]{:S(2)}) collective-permute-start(f32[2,2,256,256]{3,2,1,0:T(8,128)} %bitcast.14), channel_id=1, source_target_pairs={{0,64},{1,65},{2,66},{3,67},{4,68},{5,69},{6,70},{7,71},{8,72},{9,... | collective-permute-start | bytes 3145736 | tf_op jit(solution)/shard_map/ppermute | solution.py:352
  2.0 0.8 fusion.6
  2.8 0.1 pad_add_fusion.spot
  2.9 1.3 %collective-permute-start.1 = (s32[4]{0:T(128)S(1)}, s32[4]{0:T(128)S(1)}, u32[]{:S(2)}, u32[]{:S(2)}) collective-permute-start(s32[4]{0:T(128)S(1)} %pad_add_fusion.spot), channel_id=1, source_target_pairs={{0,1},{1,2},{2,3},{3,0},{4,5},{5,6},{6,7},{7,4},{8,9},{9,10},{10,1... | collective-permute-start | bytes 56 | tf_op jit(solution)/shard_map/ppermute | solution.py:352
  4.2 0.8 pad_slice_fusion.1
  5.0 0.0 collective-permute-done.3.other
  5.0 1.2 %copy-done = f32[2,2,1,256,256]{4,3,2,1,0:T(8,128)S(1)} copy-done((f32[2,2,1,256,256]{4,3,2,1,0:T(8,128)S(1)}, f32[2,2,1,256,256]{4,3,2,1,0:T(8,128)}, u32[]{:S(2)}) %copy-start) | copy-done | bytes 1048600
  6.2 0.8 shard_map.64
  7.0 1.3 %collective-permute-start.8 = (f32[2,256,256]{2,1,0:T(8,128)S(1)}, f32[2,256,256]{2,1,0:T(8,128)S(1)}, u32[]{:S(2)}, u32[]{:S(2)}) collective-permute-start(f32[2,256,256]{2,1,0:T(8,128)S(1)} %get-tuple-element.45.own.refs_0_), channel_id=1, source_target_pairs={{0,3},{1,0},{2,1},{3,2},{4,7},{5,4},{6,5},{7,6},{8,11},{9,8},{10,9... | collective-permute-start | bytes 1572872 | tf_op jit(solution)/shard_map/ppermute | solution.py:352
  8.2 1.3 %collective-permute-start.9 = (f32[2,256,256]{2,1,0:T(8,128)S(1)}, f32[2,256,256]{2,1,0:T(8,128)S(1)}, u32[]{:S(2)}, u32[]{:S(2)}) collective-permute-start(f32[2,256,256]{2,1,0:T(8,128)S(1)} %get-tuple-element.46.own.refs_1_), channel_id=1, source_target_pairs={{0,60},{1,61},{2,62},{3,63},{4,0},{5,1},{6,2},{7,3},{8,4},{9,5},{1... | collective-permute-start | bytes 1572872 | tf_op jit(solution)/shard_map/ppermute | solution.py:352
  9.5 1.3 %collective-permute-start.5 = (f32[2,256,256]{2,1,0:T(8,128)S(1)}, f32[2,256,256]{2,1,0:T(8,128)S(1)}, u32[]{:S(2)}, u32[]{:S(2)}) collective-permute-start(f32[2,256,256]{2,1,0:T(8,128)S(1)} %get-tuple-element.44.own.refs_1_), channel_id=1, source_target_pairs={{0,60},{1,61},{2,62},{3,63},{4,0},{5,1},{6,2},{7,3},{8,4},{9,5},{1... | collective-permute-start | bytes 1572872 | tf_op jit(solution)/shard_map/ppermute | solution.py:352
  10.8 0.9 collective-permute-start.4
  11.7 1.1 %negate_multiply_fusion = (f32[1,256,256]{2,1,0:T(8,128)S(1)}, f32[1,256,256]{2,1,0:T(8,128)S(1)}) fusion(), kind=kLoop, calls=%fused_computation.9 | loop fusion | flops 1114112 | bytes 524288 | tf_op jit(solution)/shard_map/mul | solution.py:360
  12.9 1.1 %collective-permute-start.2 = (s32[4]{0:T(128)S(1)}, s32[4]{0:T(128)S(1)}, u32[]{:S(2)}, u32[]{:S(2)}) collective-permute-start(s32[4]{0:T(128)S(1)} %pad_add_fusion.spot), channel_id=1, source_target_pairs={{0,4},{1,5},{2,6},{3,7},{4,8},{5,9},{6,10},{7,11},{8,12},{9,13},{1... | collective-permute-start | bytes 56 | tf_op jit(solution)/shard_map/ppermute | solution.py:352
  13.9 12.8 %collective-permute-done.2 = s32[4]{0:T(128)S(1)} collective-permute-done((s32[4]{0:T(128)S(1)}, s32[4]{0:T(128)S(1)}, u32[]{:S(2)}, u32[]{:S(2)}) %collective-permute-start.2) | collective-permute-done | bytes 48 | tf_op jit(solution)/shard_map/ppermute | solution.py:352
  26.7 1.9 %collective-permute-start = (s32[4]{0:T(128)S(1)}, s32[4]{0:T(128)S(1)}, u32[]{:S(2)}, u32[]{:S(2)}) collective-permute-start(s32[4]{0:T(128)S(1)} %pad_add_fusion.spot), channel_id=1, source_target_pairs={{64,69},{65,70},{66,71},{67,68},{68,73},{69,74},{70,75},{71,72},{7... | collective-permute-start | bytes 56 | tf_op jit(solution)/shard_map/ppermute | solution.py:352
  28.6 0.0 collective-permute-done.8.near.refs_2_
  28.7 0.6 shard_map.67
  29.3 0.1 collective-permute-start.10
  29.3 0.0 collective-permute-done.9.near.refs_3_
  29.4 0.0 copy-start.2
  29.4 0.6 shard_map.68
  30.0 0.0 copy-start.1
  30.0 1.0 collective-permute-start.11
  31.0 0.6 shard_map.66
  31.6 0.3 collective-permute-start.7
  31.9 0.6 shard_map.65
  32.5 0.1 collective-permute-start.6
  32.6 3.8 %collective-permute-done = s32[4]{0:T(128)S(1)} collective-permute-done((s32[4]{0:T(128)S(1)}, s32[4]{0:T(128)S(1)}, u32[]{:S(2)}, u32[]{:S(2)}) %collective-permute-start) | collective-permute-done | bytes 48 | tf_op jit(solution)/shard_map/ppermute | solution.py:352
  36.5 2.3 %collective-permute-start.12 = (f32[256,256]{1,0:T(8,128)S(1)}, f32[256,256]{1,0:T(8,128)S(1)}, u32[]{:S(2)}, u32[]{:S(2)}) collective-permute-start(f32[256,256]{1,0:T(8,128)S(1)} %get-tuple-element.81), channel_id=1, source_target_pairs={{64,69},{65,70},{66,71},{67,68},{68,73},{69,74},{70,75},{71,72},{7... | collective-permute-start | bytes 786440 | tf_op jit(solution)/shard_map/ppermute | solution.py:352
  38.7 0.1 pad_maximum_fusion.1.taps
  38.8 0.1 broadcast_select_fusion.3.spot
  38.9 2.7 %tables.1 = (bf16[4,512,512]{2,1,0:T(8,128)(2,1)S(1)}, bf16[4,512,512]{2,1,0:T(8,128)(2,1)S(1)}, bf16[4,512,256]{2,1,0:T(8,128)(2,1)S(1)}, bf16[4,512,256]{2,1,0:T(8,128)(2,1)S(1)}) custom-call(s32[4]{0:T(128)S(1)} %broadcast_select_fusion.3.spot, f32[8,256]{1,0:T(8,128)S(1)} %pad_maximum_fusion.1.taps, f32[2,256,256]{2,1,0:T(8,128)S(1)} %pad_maximum_fusion.dft), custom_call_target="tpu_custom_call" | custom-call | tf_op jit(solution)/shard_map/tables/pallas_call | solution.py:96
  41.6 3.0 %shard_map.69 = (f32[2,256,256]{2,1,0:T(8,128)S(1)}, f32[2,256,256]{2,1,0:T(8,128)S(1)}, f32[2,256,256]{2,1,0:T(8,128)S(1)}, f32[2,256,256]{2,1,0:T(8,128)S(1)}, f32[2,256,256]{2,1,0:T(8,128)S(1)}) custom-call(s32[4]{0:T(128)S(1)} %broadcast_select_fusion.3.spot, f32[2,256,256]{2,1,0:T(8,128)S(1)} %get-tuple-element.45.own.refs_0_, ...), custom_call_target="tpu_custom_call" | custom-call | tf_op jit(solution)/shard_map/pallas_call | solution.py:259
  44.6 0.3 collective-permute-done.7.refs_5_
  44.9 2.0 %collective-permute-done.6.refs_4_ = f32[2,256,256]{2,1,0:T(8,128)S(1)} collective-permute-done((f32[2,256,256]{2,1,0:T(8,128)S(1)}, f32[2,256,256]{2,1,0:T(8,128)S(1)}, u32[]{:S(2)}, u32[]{:S(2)}) %collective-permute-start.6) | collective-permute-done | bytes 524320 | tf_op jit(solution)/shard_map/ppermute | solution.py:352
  46.9 2.7 %shard_map.70 = (f32[2,256,256]{2,1,0:T(8,128)S(1)}, f32[2,256,256]{2,1,0:T(8,128)S(1)}, f32[2,256,256]{2,1,0:T(8,128)S(1)}, f32[2,256,256]{2,1,0:T(8,128)S(1)}) custom-call(s32[4]{0:T(128)S(1)} %broadcast_select_fusion.3.spot, f32[2,256,256]{2,1,0:T(8,128)S(1)} %get-tuple-element.43.own.refs_0_, f32[2,256,256]{2,1,0:T(8,128)S(1)} %get-tuple-element.44.own.refs_1_, ...), custom_call_target="tpu_custom_call" | custom-call | tf_op jit(solution)/shard_map/pallas_call | solution.py:259
  49.6 3.2 %collective-permute-done.12.refs_2_ = f32[256,256]{1,0:T(8,128)S(1)} collective-permute-done((f32[256,256]{1,0:T(8,128)S(1)}, f32[256,256]{1,0:T(8,128)S(1)}, u32[]{:S(2)}, u32[]{:S(2)}) %collective-permute-start.12) | collective-permute-done | bytes 262176 | tf_op jit(solution)/shard_map/ppermute | solution.py:352
  52.8 2.8 %shard_map.71 = (f32[2,2,256,256]{3,2,1,0:T(8,128)S(1)}, f32[2,256,256]{2,1,0:T(8,128)S(1)}, f32[2,256,256]{2,1,0:T(8,128)S(1)}, bf16[2,512,256]{2,1,0:T(8,128)(2,1)S(1)}) custom-call(s32[4]{0:T(128)S(1)} %broadcast_select_fusion.3.spot, f32[2,256,256]{2,1,0:T(8,128)S(1)} %get-tuple-element.52.refs_0_, f32[256,256]{1,0:T(8,128)S(1)} %get-tuple-element.82.refs_1_, ...), custom_call_target="tpu_custom_call" | custom-call | tf_op jit(solution)/shard_map/pallas_call | solution.py:259
  55.7 1.5 %collective-permute-start.20 = (f32[2,256,256]{2,1,0:T(8,128)S(1)}, f32[2,256,256]{2,1,0:T(8,128)S(1)}, u32[]{:S(2)}, u32[]{:S(2)}) collective-permute-start(f32[2,256,256]{2,1,0:T(8,128)S(1)} %get-tuple-element.73), channel_id=1, source_target_pairs={{0,4},{1,5},{2,6},{3,7},{4,8},{5,9},{6,10},{7,11},{8,12},{9,13},{1... | collective-permute-start | bytes 1572872 | tf_op jit(solution)/shard_map/ppermute | solution.py:352
  57.2 1.6 %shard_map.72 = (f32[2,256,256]{2,1,0:T(8,128)S(1)}, f32[256,256]{1,0:T(8,128)S(1)}, f32[256,256]{1,0:T(8,128)S(1)}, bf16[2,512,256]{2,1,0:T(8,128)(2,1)S(1)}) custom-call(s32[4]{0:T(128)S(1)} %broadcast_select_fusion.3.spot, bf16[2,512,256]{2,1,0:T(8,128)(2,1)S(1)} %get-tuple-element.56.refs_0_, f32[2,256,256]{2,1,0:T(8,128)S(1)} %get-tuple-element.57.refs_1_, ...), custom_call_target="tpu_custom_call" | custom-call | tf_op jit(solution)/shard_map/pallas_call | solution.py:259
  58.8 1.6 %shard_map.73 = (f32[2,256,256]{2,1,0:T(8,128)S(1)}, f32[256,256]{1,0:T(8,128)S(1)}, f32[256,256]{1,0:T(8,128)S(1)}) custom-call(s32[4]{0:T(128)S(1)} %broadcast_select_fusion.3.spot, bf16[2,512,256]{2,1,0:T(8,128)(2,1)S(1)} %get-tuple-element.59.refs_0_, f32[2,256,256]{2,1,0:T(8,128)S(1)} %get-tuple-element.60.refs_1_, ...), custom_call_target="tpu_custom_call" | custom-call | tf_op jit(solution)/shard_map/pallas_call | solution.py:259
  60.4 0.3 collective-permute-start.18
  60.6 0.1 collective-permute-start.19
  60.7 0.1 pad_add_fusion.2
  60.8 0.6 collective-permute-start.15
  61.3 5.5 %collective-permute-done.18.refs_3_ = f32[256,256]{1,0:T(8,128)S(1)} collective-permute-done((f32[256,256]{1,0:T(8,128)S(1)}, f32[256,256]{1,0:T(8,128)S(1)}, u32[]{:S(2)}, u32[]{:S(2)}) %collective-permute-start.18) | collective-permute-done | bytes 262176 | tf_op jit(solution)/shard_map/ppermute | solution.py:352
  66.9 2.5 %collective-permute-done.19.refs_4_ = f32[256,256]{1,0:T(8,128)S(1)} collective-permute-done((f32[256,256]{1,0:T(8,128)S(1)}, f32[256,256]{1,0:T(8,128)S(1)}, u32[]{:S(2)}, u32[]{:S(2)}) %collective-permute-start.19) | collective-permute-done | bytes 262176 | tf_op jit(solution)/shard_map/ppermute | solution.py:352
  69.4 0.9 shard_map.75
  70.3 0.1 collective-permute-start.21
  70.4 0.6 collective-permute-start.13
  71.0 0.3 collective-permute-start.14
  71.3 0.3 collective-permute-start.22
  71.6 4.4 %collective-permute-done.13.refs_3_ = f32[256,256]{1,0:T(8,128)S(1)} collective-permute-done((f32[256,256]{1,0:T(8,128)S(1)}, f32[256,256]{1,0:T(8,128)S(1)}, u32[]{:S(2)}, u32[]{:S(2)}) %collective-permute-start.13) | collective-permute-done | bytes 262176 | tf_op jit(solution)/shard_map/ppermute | solution.py:352
  75.9 2.8 %collective-permute-done.14.refs_4_ = f32[256,256]{1,0:T(8,128)S(1)} collective-permute-done((f32[256,256]{1,0:T(8,128)S(1)}, f32[256,256]{1,0:T(8,128)S(1)}, u32[]{:S(2)}, u32[]{:S(2)}) %collective-permute-start.14) | collective-permute-done | bytes 262176 | tf_op jit(solution)/shard_map/ppermute | solution.py:352
  78.8 0.9 shard_map.74
  79.7 2.6 %collective-permute-start.16 = (f32[2,256,256]{2,1,0:T(8,128)S(1)}, f32[2,256,256]{2,1,0:T(8,128)S(1)}, u32[]{:S(2)}, u32[]{:S(2)}) collective-permute-start(f32[2,256,256]{2,1,0:T(8,128)S(1)} %get-tuple-element.69), channel_id=1, source_target_pairs={{0,64},{1,65},{2,66},{3,67},{4,68},{5,69},{6,70},{7,71},{8,72},{9,... | collective-permute-start | bytes 1572872 | tf_op jit(solution)/shard_map/ppermute | solution.py:352
  82.2 4.7 %collective-permute-start.17 = (f32[2,256,256]{2,1,0:T(8,128)S(1)}, f32[2,256,256]{2,1,0:T(8,128)S(1)}, u32[]{:S(2)}, u32[]{:S(2)}) collective-permute-start(f32[2,256,256]{2,1,0:T(8,128)S(1)} %get-tuple-element.70), channel_id=1, source_target_pairs={{0,4},{1,5},{2,6},{3,7},{4,8},{5,9},{6,10},{7,11},{8,12},{9,13},{1... | collective-permute-start | bytes 1572872 | tf_op jit(solution)/shard_map/ppermute | solution.py:352
  87.0 0.3 collective-permute-start.23
  87.3 5.8 %collective-permute-done.17.refs_2_ = f32[2,256,256]{2,1,0:T(8,128)S(1)} collective-permute-done((f32[2,256,256]{2,1,0:T(8,128)S(1)}, f32[2,256,256]{2,1,0:T(8,128)S(1)}, u32[]{:S(2)}, u32[]{:S(2)}) %collective-permute-start.17) | collective-permute-done | bytes 524320 | tf_op jit(solution)/shard_map/ppermute | solution.py:352
  93.1 0.7 shard_map.76
  93.8 3.0 %collective-permute-done.24.refs_3_ = f32[2,256,256]{2,1,0:T(8,128)S(1)} collective-permute-done((f32[2,256,256]{2,1,0:T(8,128)S(1)}, f32[2,256,256]{2,1,0:T(8,128)S(1)}, u32[]{:S(2)}, u32[]{:S(2)}) %collective-permute-start.24) | collective-permute-done | bytes 524320 | tf_op jit(solution)/shard_map/ppermute | solution.py:352
  96.8 2.9 %collective-permute-done.23.refs_2_ = f32[2,256,256]{2,1,0:T(8,128)S(1)} collective-permute-done((f32[2,256,256]{2,1,0:T(8,128)S(1)}, f32[2,256,256]{2,1,0:T(8,128)S(1)}, u32[]{:S(2)}, u32[]{:S(2)}) %collective-permute-start.23) | collective-permute-done | bytes 524320 | tf_op jit(solution)/shard_map/ppermute | solution.py:352
  99.8 1.6 %shard_map.77 = f32[2,2,256,256]{3,2,1,0:T(8,128)} custom-call(s32[4]{0:T(128)S(1)} %broadcast_select_fusion.3.spot, f32[2,256,256]{2,1,0:T(8,128)S(1)} %get-tuple-element.77.refs_0_, f32[2,256,256]{2,1,0:T(8,128)S(1)} %get-tuple-element.78.refs_1_, f32[2,256,256]{2,1,0:T(8,128)S(1)} %collective-permute-done.23.refs_2_, ...), custom_call_target="tpu_custom_call" | custom-call | tf_op jit(solution)/shard_map/pallas_call | solution.py:259
  (20 shorter events, 0.1 us)
Async XLA Ops:
  0.0 11.7 %copy-start.3 = (f32[2,31]{1,0:T(2,128)S(1)}, f32[2,31]{1,0:T(2,128)}, u32[]{:S(2)}) copy-start(f32[2,31]{1,0:T(2,128)} %param.8) | copy-start | bytes 748
  0.0 5.0 %collective-permute-start.3 = (f32[2,2,256,256]{3,2,1,0:T(8,128)}, f32[2,2,256,256]{3,2,1,0:T(8,128)S(1)}, u32[]{:S(2)}, u32[]{:S(2)}) collective-permute-start(f32[2,2,256,256]{3,2,1,0:T(8,128)} %bitcast.14), channel_id=1, source_target_pairs={{0,64},{1,65},{2,66},{3,67},{4,68},{5,69},{6,70},{7,71},{8,72},{9,... | collective-permute-start | bytes 3145736 | tf_op jit(solution)/shard_map/ppermute | solution.py:352
  2.9 10.0 %collective-permute-start.1 = (s32[4]{0:T(128)S(1)}, s32[4]{0:T(128)S(1)}, u32[]{:S(2)}, u32[]{:S(2)}) collective-permute-start(s32[4]{0:T(128)S(1)} %pad_add_fusion.spot), channel_id=1, source_target_pairs={{0,1},{1,2},{2,3},{3,0},{4,5},{5,6},{6,7},{7,4},{8,9},{9,10},{10,1... | collective-permute-start | bytes 56 | tf_op jit(solution)/shard_map/ppermute | solution.py:352
  5.0 1.2 %copy-start = (f32[2,2,1,256,256]{4,3,2,1,0:T(8,128)S(1)}, f32[2,2,1,256,256]{4,3,2,1,0:T(8,128)}, u32[]{:S(2)}) copy-start(f32[2,2,1,256,256]{4,3,2,1,0:T(8,128)} %param.6) | copy-start | bytes 3145732
  7.0 21.7 %collective-permute-start.8 = (f32[2,256,256]{2,1,0:T(8,128)S(1)}, f32[2,256,256]{2,1,0:T(8,128)S(1)}, u32[]{:S(2)}, u32[]{:S(2)}) collective-permute-start(f32[2,256,256]{2,1,0:T(8,128)S(1)} %get-tuple-element.45.own.refs_0_), channel_id=1, source_target_pairs={{0,3},{1,0},{2,1},{3,2},{4,7},{5,4},{6,5},{7,6},{8,11},{9,8},{10,9... | collective-permute-start | bytes 1572872 | tf_op jit(solution)/shard_map/ppermute | solution.py:352
  8.2 21.1 %collective-permute-start.9 = (f32[2,256,256]{2,1,0:T(8,128)S(1)}, f32[2,256,256]{2,1,0:T(8,128)S(1)}, u32[]{:S(2)}, u32[]{:S(2)}) collective-permute-start(f32[2,256,256]{2,1,0:T(8,128)S(1)} %get-tuple-element.46.own.refs_1_), channel_id=1, source_target_pairs={{0,60},{1,61},{2,62},{3,63},{4,0},{5,1},{6,2},{7,3},{8,4},{9,5},{1... | collective-permute-start | bytes 1572872 | tf_op jit(solution)/shard_map/ppermute | solution.py:352
  9.5 21.4 %collective-permute-start.5 = (f32[2,256,256]{2,1,0:T(8,128)S(1)}, f32[2,256,256]{2,1,0:T(8,128)S(1)}, u32[]{:S(2)}, u32[]{:S(2)}) collective-permute-start(f32[2,256,256]{2,1,0:T(8,128)S(1)} %get-tuple-element.44.own.refs_1_), channel_id=1, source_target_pairs={{0,60},{1,61},{2,62},{3,63},{4,0},{5,1},{6,2},{7,3},{8,4},{9,5},{1... | collective-permute-start | bytes 1572872 | tf_op jit(solution)/shard_map/ppermute | solution.py:352
  10.8 21.1 %collective-permute-start.4 = (f32[2,256,256]{2,1,0:T(8,128)S(1)}, f32[2,256,256]{2,1,0:T(8,128)S(1)}, u32[]{:S(2)}, u32[]{:S(2)}) collective-permute-start(f32[2,256,256]{2,1,0:T(8,128)S(1)} %get-tuple-element.43.own.refs_0_), channel_id=1, source_target_pairs={{0,3},{1,0},{2,1},{3,2},{4,7},{5,4},{6,5},{7,6},{8,11},{9,8},{10,9... | collective-permute-start | bytes 1572872 | tf_op jit(solution)/shard_map/ppermute | solution.py:352
  12.9 13.9 %collective-permute-start.2 = (s32[4]{0:T(128)S(1)}, s32[4]{0:T(128)S(1)}, u32[]{:S(2)}, u32[]{:S(2)}) collective-permute-start(s32[4]{0:T(128)S(1)} %pad_add_fusion.spot), channel_id=1, source_target_pairs={{0,4},{1,5},{2,6},{3,7},{4,8},{5,9},{6,10},{7,11},{8,12},{9,13},{1... | collective-permute-start | bytes 56 | tf_op jit(solution)/shard_map/ppermute | solution.py:352
  26.7 9.7 %collective-permute-start = (s32[4]{0:T(128)S(1)}, s32[4]{0:T(128)S(1)}, u32[]{:S(2)}, u32[]{:S(2)}) collective-permute-start(s32[4]{0:T(128)S(1)} %pad_add_fusion.spot), channel_id=1, source_target_pairs={{64,69},{65,70},{66,71},{67,68},{68,73},{69,74},{70,75},{71,72},{7... | collective-permute-start | bytes 56 | tf_op jit(solution)/shard_map/ppermute | solution.py:352
  29.3 12.3 %collective-permute-start.10 = (f32[2,256,256]{2,1,0:T(8,128)S(1)}, f32[2,256,256]{2,1,0:T(8,128)S(1)}, u32[]{:S(2)}, u32[]{:S(2)}) collective-permute-start(f32[2,256,256]{2,1,0:T(8,128)S(1)} %shard_map.67), channel_id=1, source_target_pairs={{0,60},{1,61},{2,62},{3,63},{4,0},{5,1},{6,2},{7,3},{8,4},{9,5},{1... | collective-permute-start | bytes 1572872 | tf_op jit(solution)/shard_map/ppermute | solution.py:352
  29.4 3.2 %copy-start.2 = (f32[1,2,256,256]{3,2,1,0:T(8,128)S(1)}, f32[1,2,256,256]{3,2,1,0:T(8,128)}, u32[]{:S(2)}) copy-start(f32[1,2,256,256]{3,2,1,0:T(8,128)} %param.9) | copy-start | bytes 1572868
  30.0 11.6 %copy-start.1 = (f32[2,256,256]{2,1,0:T(8,128)S(1)}, f32[2,256,256]{2,1,0:T(8,128)}, u32[]{:S(2)}) copy-start(f32[2,256,256]{2,1,0:T(8,128)} %refs_6_.1) | copy-start | bytes 1572868
  30.0 11.6 %collective-permute-start.11 = (f32[2,256,256]{2,1,0:T(8,128)S(1)}, f32[2,256,256]{2,1,0:T(8,128)S(1)}, u32[]{:S(2)}, u32[]{:S(2)}) collective-permute-start(f32[2,256,256]{2,1,0:T(8,128)S(1)} %shard_map.68), channel_id=1, source_target_pairs={{0,3},{1,0},{2,1},{3,2},{4,7},{5,4},{6,5},{7,6},{8,11},{9,8},{10,9... | collective-permute-start | bytes 1572872 | tf_op jit(solution)/shard_map/ppermute | solution.py:352
  31.6 13.3 %collective-permute-start.7 = (f32[2,256,256]{2,1,0:T(8,128)S(1)}, f32[2,256,256]{2,1,0:T(8,128)S(1)}, u32[]{:S(2)}, u32[]{:S(2)}) collective-permute-start(f32[2,256,256]{2,1,0:T(8,128)S(1)} %shard_map.66), channel_id=1, source_target_pairs={{0,3},{1,0},{2,1},{3,2},{4,7},{5,4},{6,5},{7,6},{8,11},{9,8},{10,9... | collective-permute-start | bytes 1572872 | tf_op jit(solution)/shard_map/ppermute | solution.py:352
  32.5 14.4 %collective-permute-start.6 = (f32[2,256,256]{2,1,0:T(8,128)S(1)}, f32[2,256,256]{2,1,0:T(8,128)S(1)}, u32[]{:S(2)}, u32[]{:S(2)}) collective-permute-start(f32[2,256,256]{2,1,0:T(8,128)S(1)} %shard_map.65), channel_id=1, source_target_pairs={{0,60},{1,61},{2,62},{3,63},{4,0},{5,1},{6,2},{7,3},{8,4},{9,5},{1... | collective-permute-start | bytes 1572872 | tf_op jit(solution)/shard_map/ppermute | solution.py:352
  36.5 16.4 %collective-permute-start.12 = (f32[256,256]{1,0:T(8,128)S(1)}, f32[256,256]{1,0:T(8,128)S(1)}, u32[]{:S(2)}, u32[]{:S(2)}) collective-permute-start(f32[256,256]{1,0:T(8,128)S(1)} %get-tuple-element.81), channel_id=1, source_target_pairs={{64,69},{65,70},{66,71},{67,68},{68,73},{69,74},{70,75},{71,72},{7... | collective-permute-start | bytes 786440 | tf_op jit(solution)/shard_map/ppermute | solution.py:352
  55.7 13.7 %collective-permute-start.20 = (f32[2,256,256]{2,1,0:T(8,128)S(1)}, f32[2,256,256]{2,1,0:T(8,128)S(1)}, u32[]{:S(2)}, u32[]{:S(2)}) collective-permute-start(f32[2,256,256]{2,1,0:T(8,128)S(1)} %get-tuple-element.73), channel_id=1, source_target_pairs={{0,4},{1,5},{2,6},{3,7},{4,8},{5,9},{6,10},{7,11},{8,12},{9,13},{1... | collective-permute-start | bytes 1572872 | tf_op jit(solution)/shard_map/ppermute | solution.py:352
  60.4 6.5 %collective-permute-start.18 = (f32[256,256]{1,0:T(8,128)S(1)}, f32[256,256]{1,0:T(8,128)S(1)}, u32[]{:S(2)}, u32[]{:S(2)}) collective-permute-start(f32[256,256]{1,0:T(8,128)S(1)} %get-tuple-element.71), channel_id=1, source_target_pairs={{0,4},{1,5},{2,6},{3,7},{4,8},{5,9},{6,10},{7,11},{8,12},{9,13},{1... | collective-permute-start | bytes 786440 | tf_op jit(solution)/shard_map/ppermute | solution.py:352
  60.6 8.7 %collective-permute-start.19 = (f32[256,256]{1,0:T(8,128)S(1)}, f32[256,256]{1,0:T(8,128)S(1)}, u32[]{:S(2)}, u32[]{:S(2)}) collective-permute-start(f32[256,256]{1,0:T(8,128)S(1)} %get-tuple-element.72), channel_id=1, source_target_pairs={{0,4},{1,5},{2,6},{3,7},{4,8},{5,9},{6,10},{7,11},{8,12},{9,13},{1... | collective-permute-start | bytes 786440 | tf_op jit(solution)/shard_map/ppermute | solution.py:352
  60.8 18.0 %collective-permute-start.15 = (f32[2,256,256]{2,1,0:T(8,128)S(1)}, f32[2,256,256]{2,1,0:T(8,128)S(1)}, u32[]{:S(2)}, u32[]{:S(2)}) collective-permute-start(f32[2,256,256]{2,1,0:T(8,128)S(1)} %get-tuple-element.67), channel_id=1, source_target_pairs={{0,1},{1,2},{2,3},{3,0},{4,5},{5,6},{6,7},{7,4},{8,9},{9,10},{10,1... | collective-permute-start | bytes 1572872 | tf_op jit(solution)/shard_map/ppermute | solution.py:352
  70.3 16.7 %collective-permute-start.21 = (f32[2,256,256]{2,1,0:T(8,128)S(1)}, f32[2,256,256]{2,1,0:T(8,128)S(1)}, u32[]{:S(2)}, u32[]{:S(2)}) collective-permute-start(f32[2,256,256]{2,1,0:T(8,128)S(1)} %get-tuple-element.75), channel_id=1, source_target_pairs={{0,64},{1,65},{2,66},{3,67},{4,68},{5,69},{6,70},{7,71},{8,72},{9,... | collective-permute-start | bytes 1572872 | tf_op jit(solution)/shard_map/ppermute | solution.py:352
  70.4 5.6 %collective-permute-start.13 = (f32[256,256]{1,0:T(8,128)S(1)}, f32[256,256]{1,0:T(8,128)S(1)}, u32[]{:S(2)}, u32[]{:S(2)}) collective-permute-start(f32[256,256]{1,0:T(8,128)S(1)} %get-tuple-element.65), channel_id=1, source_target_pairs={{0,1},{1,2},{2,3},{3,0},{4,5},{5,6},{6,7},{7,4},{8,9},{9,10},{10,1... | collective-permute-start | bytes 786440 | tf_op jit(solution)/shard_map/ppermute | solution.py:352
  71.0 7.8 %collective-permute-start.14 = (f32[256,256]{1,0:T(8,128)S(1)}, f32[256,256]{1,0:T(8,128)S(1)}, u32[]{:S(2)}, u32[]{:S(2)}) collective-permute-start(f32[256,256]{1,0:T(8,128)S(1)} %get-tuple-element.66), channel_id=1, source_target_pairs={{0,1},{1,2},{2,3},{3,0},{4,5},{5,6},{6,7},{7,4},{8,9},{9,10},{10,1... | collective-permute-start | bytes 786440 | tf_op jit(solution)/shard_map/ppermute | solution.py:352
  71.3 16.0 %collective-permute-start.22 = (f32[2,256,256]{2,1,0:T(8,128)S(1)}, f32[2,256,256]{2,1,0:T(8,128)S(1)}, u32[]{:S(2)}, u32[]{:S(2)}) collective-permute-start(f32[2,256,256]{2,1,0:T(8,128)S(1)} %get-tuple-element.76), channel_id=1, source_target_pairs={{0,1},{1,2},{2,3},{3,0},{4,5},{5,6},{6,7},{7,4},{8,9},{9,10},{10,1... | collective-permute-start | bytes 1572872 | tf_op jit(solution)/shard_map/ppermute | solution.py:352
  79.7 7.6 %collective-permute-start.16 = (f32[2,256,256]{2,1,0:T(8,128)S(1)}, f32[2,256,256]{2,1,0:T(8,128)S(1)}, u32[]{:S(2)}, u32[]{:S(2)}) collective-permute-start(f32[2,256,256]{2,1,0:T(8,128)S(1)} %get-tuple-element.69), channel_id=1, source_target_pairs={{0,64},{1,65},{2,66},{3,67},{4,68},{5,69},{6,70},{7,71},{8,72},{9,... | collective-permute-start | bytes 1572872 | tf_op jit(solution)/shard_map/ppermute | solution.py:352
  82.2 10.9 %collective-permute-start.17 = (f32[2,256,256]{2,1,0:T(8,128)S(1)}, f32[2,256,256]{2,1,0:T(8,128)S(1)}, u32[]{:S(2)}, u32[]{:S(2)}) collective-permute-start(f32[2,256,256]{2,1,0:T(8,128)S(1)} %get-tuple-element.70), channel_id=1, source_target_pairs={{0,4},{1,5},{2,6},{3,7},{4,8},{5,9},{6,10},{7,11},{8,12},{9,13},{1... | collective-permute-start | bytes 1572872 | tf_op jit(solution)/shard_map/ppermute | solution.py:352
  87.0 9.8 %collective-permute-start.24 = (f32[2,256,256]{2,1,0:T(8,128)S(1)}, f32[2,256,256]{2,1,0:T(8,128)S(1)}, u32[]{:S(2)}, u32[]{:S(2)}) collective-permute-start(f32[2,256,256]{2,1,0:T(8,128)S(1)} %get-tuple-element.80), channel_id=1, source_target_pairs={{0,65},{1,66},{2,67},{3,64},{4,69},{5,70},{6,71},{7,68},{8,73},{9,... | collective-permute-start | bytes 1572872 | tf_op jit(solution)/shard_map/ppermute | solution.py:352
  87.0 12.8 %collective-permute-start.23 = (f32[2,256,256]{2,1,0:T(8,128)S(1)}, f32[2,256,256]{2,1,0:T(8,128)S(1)}, u32[]{:S(2)}, u32[]{:S(2)}) collective-permute-start(f32[2,256,256]{2,1,0:T(8,128)S(1)} %get-tuple-element.79), channel_id=1, source_target_pairs={{0,68},{1,69},{2,70},{3,71},{4,72},{5,73},{6,74},{7,75},{8,76},{9,... | collective-permute-start | bytes 1572872 | tf_op jit(solution)/shard_map/ppermute | solution.py:352
